TPU v7x, 256 devices: a whole 4x4x8 slice. The times are simulated.
256 devices in a mesh: pipe: 4 (over x), seq: 16 (over z, core), chan: 4 (over y).
Axes of the slice: x: 4, y: 4, z: 8, core: 2. Of those that a mesh axis runs over, the one named last changes fastest.
Arguments:
- signal: bfloat16 [4, 4096, 2048], P('pipe', 'seq', 'chan'), may hold values from -6 to 6
- gate_value: bfloat16 [4, 4096, 2048], P('pipe', 'seq', 'chan'), may hold values from -6 to 6
- grad_out: bfloat16 [4, 4096, 2048], P('pipe', 'seq', 'chan'), may hold values from -1.5 to 1.5
- long_filter: bfloat16 [4, 4096, 2048], P('pipe', 'seq', 'chan'), may hold values from -0.09375 to 0.09375
- weight: bfloat16 [4, 4096, 2048], P('pipe', None, 'chan'), may hold values from -0.125 to 0.125
Outputs:
- gate_grad: bfloat16 [4, 4096, 2048], P('pipe', 'seq', 'chan')
- filter_grad: float32 [4, 4096, 2048], P('pipe', 'seq', 'chan')
- input_grad: bfloat16 [4, 4096, 4096], P('pipe', 'seq', 'chan')
All inputs are finite; a program needn't handle non-finite values.
Results may differ from a plain program's by a relative error of at most 0.02.
Values may be sent and summed in bfloat16 or wider, within the bound.
No kernel may reach another device: no remote copies, remote signals or barrier semaphores. Data moves between devices by JAX's collectives and lax.ppermute only.
A program may use at most 128 MiB of HBM per device.

v0:
```python
import math

import jax
import jax.numpy as jnp
from jax import lax
from jax.sharding import PartitionSpec as P

HIGHEST = lax.Precision.HIGHEST
HIGHER = lax.Precision.HIGH


def passed_along(x, axis, by):
    length = lax.axis_size(axis)
    return lax.ppermute(x, axis, [(i, (i + by) % length) for i in range(length)])


def make_tables(panel_len):
    span_len = 2 * panel_len
    row_index = lax.broadcasted_iota(jnp.int32, (span_len, panel_len), 0)
    col_index = lax.broadcasted_iota(jnp.int32, (span_len, panel_len), 1)
    frequency = jnp.where(row_index <= panel_len, row_index, row_index - panel_len)
    angles = (frequency * col_index % span_len).astype(jnp.float32) * (2.0 * math.pi / span_len)
    forward_table = jnp.where(row_index <= panel_len, jnp.cos(angles), -jnp.sin(angles))
    end_rows = jnp.logical_or(row_index == 0, row_index == panel_len)
    weights = jnp.where(end_rows, 1.0, 2.0) / span_len
    inverse_table = (forward_table * weights).T
    return (forward_table, inverse_table)


def make_parity(panel_len):
    row_index = lax.broadcasted_iota(jnp.int32, (2 * panel_len, 1), 0)
    frequency = jnp.where(row_index <= panel_len, row_index, row_index - panel_len)
    return (1 - 2 * (frequency % 2)).astype(jnp.float32)


def spec_product(left_spec, right_spec, interior, conjugate):
    panel_len = left_spec.shape[0] // 2
    left_real, left_imag = (left_spec[:panel_len], left_spec[panel_len:])
    right_real, right_imag = (right_spec[:panel_len], right_spec[panel_len:])
    if conjugate:
        right_imag = right_imag * (1.0 - 2.0 * interior)
    real_part = left_real * right_real - interior * left_imag * right_imag
    imag_part = (
        interior * (left_real * right_imag + left_imag * right_real)
        + (1.0 - interior) * left_imag * right_imag
    )
    return jnp.concatenate([real_part, imag_part], axis=0)


def on_device(signal, gate_value, grad_out, long_filter, weight):
    panel_len = signal.shape[1]
    chan_width = signal.shape[2]
    span_len = 2 * panel_len
    panel_count = lax.axis_size("seq")
    my_panel = lax.axis_index("seq")
    forward_table, inverse_table = make_tables(panel_len)
    parity = make_parity(panel_len)
    interior = (lax.broadcasted_iota(jnp.int32, (panel_len, 1), 0) != 0).astype(jnp.float32)
    gated = (gate_value[0].astype(jnp.float32) * grad_out[0].astype(jnp.float32)).astype(
        jnp.bfloat16
    )
    signals, gateds, filters = (
        lax.all_gather(signal, "seq", axis=1, tiled=True),
        lax.all_gather(gated[None], "seq", axis=1, tiled=True),
        lax.all_gather(long_filter, "seq", axis=1, tiled=True),
    )
    zero_spec = jnp.zeros((span_len, chan_width), jnp.float32)

    def spectrum(gathered, panel_at):
        panel_rows = lax.dynamic_slice_in_dim(gathered[0], panel_at * panel_len, panel_len, 0)
        return jnp.dot(forward_table, panel_rows.astype(jnp.float32), precision=HIGHER)

    def spectrum_if(use_panel, gathered, panel_at):
        return lax.cond(
            use_panel,
            lambda where_at: spectrum(gathered, where_at),
            lambda where_at: zero_spec,
            panel_at,
        )

    def invert(spectrum_in):
        return jnp.dot(inverse_table, spectrum_in, precision=HIGHEST)

    def settle(lag_parts, spectrum_in, use_panel, target):

        def add_rows(parts_now):
            row_at = jnp.maximum(target, 0)
            current = lax.dynamic_index_in_dim(parts_now, row_at, 0, keepdims=True)
            return lax.dynamic_update_index_in_dim(
                parts_now, current + invert(spectrum_in)[None], row_at, 0
            )

        return lax.cond(use_panel, add_rows, lambda parts_now: parts_now, lag_parts)

    own_gated = jnp.dot(forward_table, gated.astype(jnp.float32), precision=HIGHER)
    last_lag = jnp.maximum(my_panel, panel_count - 1 - my_panel)
    extras = (
        zero_spec,
        jnp.array(False),
        jnp.zeros((panel_count, panel_len, chan_width), jnp.float32),
    )

    def lag_step(lag_index, loop_state):
        prior_filter, forward_sum, backward_sum, extras_now = loop_state
        filter_now = spectrum(filters, lag_index)
        filter_full = filter_now + parity * prior_filter
        use_forward = lag_index <= my_panel
        use_backward = lag_index <= panel_count - 1 - my_panel
        signal_spec = spectrum_if(use_forward, signals, jnp.maximum(my_panel - lag_index, 0))
        gated_spec = spectrum_if(
            use_backward, gateds, jnp.minimum(my_panel + lag_index, panel_count - 1)
        )
        forward_sum = forward_sum + spec_product(filter_full, signal_spec, interior, False)
        backward_sum = backward_sum + spec_product(gated_spec, filter_full, interior, True)
        prior_pair, prior_flag, lag_parts = extras_now
        pair_spec = spec_product(own_gated, signal_spec, interior, True)
        ready = jnp.logical_and(lag_index >= 1, jnp.logical_or(prior_flag, use_forward))
        lag_parts = settle(lag_parts, prior_pair + parity * pair_spec, ready, lag_index - 1)
        extras_now = (pair_spec, use_forward, lag_parts)
        return (filter_now, forward_sum, backward_sum, extras_now)

    unused_filter, forward_sum, backward_sum, extras = lax.fori_loop(
        0, last_lag + 1, lag_step, (zero_spec, zero_spec, zero_spec, extras)
    )
    prior_pair, prior_flag, lag_parts = extras
    lag_parts = settle(lag_parts, prior_pair, prior_flag, last_lag)
    filter_grad = lax.psum_scatter(
        lag_parts.reshape(1, panel_count * panel_len, chan_width).astype(jnp.bfloat16),
        "seq",
        scatter_dimension=1,
        tiled=True,
    ).astype(jnp.float32)
    conv = invert(forward_sum)
    gate_grad = (grad_out[0].astype(jnp.float32) * conv).astype(jnp.bfloat16)[None]
    signal_grad = invert(backward_sum).astype(jnp.bfloat16)
    received = passed_along(signal_grad[None], "pipe", -1)
    partial_sums = lax.dot_general(
        received[0], weight[0], (((1,), (1,)), ((), ())), preferred_element_type=jnp.float32
    )
    input_grad = lax.psum_scatter(
        partial_sums[None], "chan", scatter_dimension=2, tiled=True
    ).astype(jnp.bfloat16)
    return (gate_grad, filter_grad, input_grad)


def solution(mesh):
    return jax.shard_map(
        on_device,
        mesh=mesh,
        in_specs=(
            P("pipe", "seq", "chan"),
            P("pipe", "seq", "chan"),
            P("pipe", "seq", "chan"),
            P("pipe", "seq", "chan"),
            P("pipe", None, "chan"),
        ),
        out_specs=(P("pipe", "seq", "chan"), P("pipe", "seq", "chan"), P("pipe", "seq", "chan")),
        check_vma=False,
    )
```

profile of v0, /device:TPU:6, one launch (start us, length us, event | category | flops | bytes accessed | tf_op | source)
XLA Modules:
  0.0 691.9 jit_solution(5440354241216987989)
XLA Ops:
  11.7 4.8 fusion.62
  16.4 39.0 %all-gather.8.cloned.1.call-done = bf16[1,4096,512]{2,1,0:T(8,128)(2,1)} async-done(((bf16[1,256,512]{2,1,0:T(8,128)(2,1)}), bf16[1,4096,512]{2,1,0:T(8,128)(2,1)}) %all-gather.8.cloned.1.call-update) | async-done | bytes 4194320 | tf_op jit(solution)/shard_map/all_gather | solution.py:64
  55.4 42.5 %all-gather.4.cloned.1.call-done = bf16[1,4096,512]{2,1,0:T(8,128)(2,1)} async-done(((bf16[1,256,512]{2,1,0:T(8,128)(2,1)}), bf16[1,4096,512]{2,1,0:T(8,128)(2,1)}) %all-gather.4.cloned.1.call-update) | async-done | bytes 4194320 | tf_op jit(solution)/shard_map/all_gather | solution.py:65
  98.0 42.5 %all-gather.6.cloned.1.call-done = bf16[1,4096,512]{2,1,0:T(8,128)(2,1)} async-done(((bf16[1,256,512]{2,1,0:T(8,128)(2,1)}), bf16[1,4096,512]{2,1,0:T(8,128)(2,1)}) %all-gather.6.cloned.1.call-update) | async-done | bytes 4194320 | tf_op jit(solution)/shard_map/all_gather | solution.py:63
  140.5 4.1 broadcast_in_dim.38
  148.3 299.0 %while.31 = (s32[]{:T(128)}, f32[512,512]{1,0:T(8,128)S(1)}, f32[512,512]{1,0:T(8,128)}, f32[512,512]{1,0:T(8,128)}, f32[512,512]{1,0:T(8,128)}, /*index=5*/pred...) while((s32[]{:T(128)}, f32[512,512]{1,0:T(8,128)S(1)}, ...), condition=%wide.region_7.8_spmd.clone.clone.clone, body=%wide.region_0.7_spmd.clone.clone.clone.sunk | while | flops 2027169536 | bytes 49307344 | solution.py:122
  148.3 4.7 multiply_add_fusion.5
  164.6 3.6 maximum_add_fusion.3
  168.3 4.7 multiply_add_fusion.5
  181.7 7.4 %conditional.19 = (f32[16,256,512]{1,2,0:T(8,128)}) conditional(s32[]{:T(128)} %convert_element_type.270, f32[16,256,512]{1,2,0:T(8,128)} %get-tuple-element.824, (s32[]{:T(128)}, f32[16,256,512]{1,2,0:T(8,128)}, f32[512,1]{0,1:T(1,128)S(1)}, f32[512,512]{1,0:T(8,128)S(1)}, f32[512,512]{1,0:T(8,128)}, /*index=5*/pred[256,512]{1,0:T(32,128)(4,1)S(1)}, ...), branch_computations={%region_5.5_spmd, %region_6.6_spmd} | conditional | flops 806354944 | bytes 4329508 | solution.py:93
  181.7 7.4 %fusion.15 = f32[16,256,512]{1,2,0:T(8,128)} fusion(f32[16,256,512]{1,2,0:T(8,128)} %get-tuple-element.344, s32[]{:T(128)S(6)} %max.13, f32[512,512]{1,0:T(8,128)} %get-tuple-element.346, f32[512,512]{1,0:T(8,128)S(1)} %get-tuple-element.348, pred[256,512]{1,0:T(32,128)(4,1)S(1)} %get-tuple-element.581, f32[256,512]{1,0:T(8,128)S(1)} %get-tuple-element.587, ...), kind=kOutput, calls=%fused_computation.14 | convolution fusion | flops 806354944 | bytes 4329476 | tf_op jit(solution)/shard_map/while/body/cond/branch_1_fun/dot_general | solution.py:82
  190.1 3.6 maximum_add_fusion.3
  193.8 4.7 multiply_add_fusion.5
  208.2 3.6 maximum_add_fusion.3
  211.9 4.7 multiply_add_fusion.5
  226.3 3.6 maximum_add_fusion.3
  230.0 4.7 multiply_add_fusion.5
  244.4 3.6 maximum_add_fusion.3
  248.1 4.7 multiply_add_fusion.5
  262.5 3.6 maximum_add_fusion.3
  266.2 4.7 multiply_add_fusion.5
  280.7 3.6 maximum_add_fusion.3
  284.3 4.7 multiply_add_fusion.5
  298.8 3.6 maximum_add_fusion.3
  302.4 4.7 multiply_add_fusion.5
  316.9 3.6 maximum_add_fusion.3
  320.5 4.7 multiply_add_fusion.5
  335.0 3.6 maximum_add_fusion.3
  338.6 4.7 multiply_add_fusion.5
  353.1 3.6 maximum_add_fusion.3
  356.7 4.7 multiply_add_fusion.5
  371.2 3.6 maximum_add_fusion.3
  374.8 4.7 multiply_add_fusion.5
  389.3 3.6 maximum_add_fusion.3
  393.0 4.7 multiply_add_fusion.5
  407.4 3.6 maximum_add_fusion.3
  411.1 4.7 multiply_add_fusion.5
  425.5 3.6 maximum_add_fusion.3
  429.2 4.7 multiply_add_fusion.5
  443.6 3.6 maximum_add_fusion.3
  447.3 9.3 %conditional.4 = (f32[16,256,512]{2,1,0:T(8,128)}) conditional(s32[]{:T(128)} %convert_element_type.151, (f32[16,256,512]{1,2,0:T(8,128)}) %tuple.109, (s32[]{:T(128)}, f32[16,256,512]{1,2,0:T(8,128)}, pred[256,512]{1,0:T(32,128)(4,1)S(1)}, f32[512,512]{1,0:T(8,128)}, f32[512]{0:T(512)S(1)}, /*index=5*/f32[256,512]{1,0:T(8,128)}, ...), branch_computations={%region_8.9_spmd, %region_9.10_spmd} | conditional | flops 805830656 | bytes 26347600 | solution.py:93
  447.3 9.2 %copy.46 = f32[16,256,512]{2,1,0:T(8,128)} copy(f32[16,256,512]{1,2,0:T(8,128)} %get-tuple-element.589) | data formatting | bytes 16777216 | tf_op jit(solution)/shard_map/while | solution.py:122
  456.6 5.9 convert_element_type.152
  468.2 6.7 collective-permute-done
  474.9 5.5 convolution_bitcast_fusion.5
  481.7 4.0 fusion.50
  485.7 147.3 %reduce-scatter.3.cloned.1.call-done = bf16[1,256,512]{2,1,0:T(8,128)(2,1)} async-done(((bf16[1,4096,512]{2,1,0:T(8,128)(2,1)}), bf16[1,256,512]{2,1,0:T(8,128)(2,1)}) %reduce-scatter.3.cloned.1.call-update) | async-done | bytes 262160 | tf_op jit(solution)/shard_map/reduce_scatter | solution.py:127
  634.7 48.6 %reduce-scatter.5.cloned.1.call-done = f32[1,256,1024]{2,1,0:T(8,128)} async-done(((f32[1,256,4096]{2,1,0:T(8,128)}), f32[1,256,1024]{2,1,0:T(8,128)}) %reduce-scatter.5.cloned.1.call-update) | async-done | bytes 1048592 | tf_op jit(solution)/shard_map/reduce_scatter | solution.py:140
  (415 shorter events, 210.6 us)
Async XLA Ops:
  7.2 48.3 %all-gather.8.cloned.1.call-start = ((), (), s32[]{:S(2)}) async-start(), calls=%async_computation.4 | async-start | bytes 4456448 | tf_op jit(solution)/shard_map/all_gather | solution.py:64
  9.0 89.0 %all-gather.4.cloned.1.call-start = ((), (), s32[]{:S(2)}) async-start(), calls=%async_computation.2 | async-start | bytes 4456448 | tf_op jit(solution)/shard_map/all_gather | solution.py:65
  9.8 130.7 %all-gather.6.cloned.1.call-start = ((), (), s32[]{:S(2)}) async-start(), calls=%async_computation.3 | async-start | bytes 4456448 | tf_op jit(solution)/shard_map/all_gather | solution.py:63
  10.5 622.4 %reduce-scatter.3.cloned.1.call-start = ((), (), s32[]{:S(2)}) async-start(), calls=%async_computation.5 | async-start | bytes 4456448 | tf_op jit(solution)/shard_map/reduce_scatter | solution.py:127
  152.9 2.2 copy-start.5
  164.6 3.6 copy-start.6
  172.9 2.2 copy-start.5
  190.1 3.6 copy-start.6
  198.4 2.2 copy-start.5
  202.8 0.8 copy-start
  208.2 3.6 copy-start.6
  216.5 2.2 copy-start.5
  220.9 0.8 copy-start
  226.3 3.6 copy-start.6
  234.6 2.2 copy-start.5
  239.0 0.8 copy-start
  244.4 3.6 copy-start.6
  252.8 2.2 copy-start.5
  262.5 3.6 copy-start.6
  270.9 2.2 copy-start.5
  280.7 3.6 copy-start.6
  289.0 2.2 copy-start.5
  298.8 3.6 copy-start.6
  307.1 2.2 copy-start.5
  311.5 0.8 copy-start
  316.9 3.6 copy-start.6
  325.2 2.2 copy-start.5
  329.6 0.8 copy-start
  335.0 3.6 copy-start.6
  343.3 2.2 copy-start.5
  353.1 3.6 copy-start.6
  361.4 2.2 copy-start.5
  365.8 0.8 copy-start
  371.2 3.6 copy-start.6
  379.5 2.2 copy-start.5
  389.3 3.6 copy-start.6
  397.6 2.2 copy-start.5
  402.0 0.8 copy-start
  407.4 3.6 copy-start.6
  415.7 2.2 copy-start.5
  425.5 3.6 copy-start.6
  433.8 2.2 copy-start.5
  443.6 3.6 copy-start.6
  462.5 1.2 copy-start.3
  462.5 220.8 %reduce-scatter.5.cloned.1.call-start = ((), (), s32[]{:S(2)}) async-start(), calls=%async_computation.6 | async-start | bytes 5242880 | tf_op jit(solution)/shard_map/reduce_scatter | solution.py:140
  467.0 7.9 %collective-permute-start = (bf16[1,256,512]{2,1,0:T(8,128)(2,1)S(1)}, bf16[1,256,512]{2,1,0:T(8,128)(2,1)S(1)}, u32[]{:S(2)}, u32[]{:S(2)}) collective-permute-start(bf16[1,256,512]{2,1,0:T(8,128)(2,1)S(1)} %fusion.49), channel_id=1, source_target_pairs={{0,192},{64,0},{128,64},{192,128},{1,193},{65,1},{129,65},{193,129... | collective-permute-start | bytes 786440 | tf_op jit(solution)/shard_map/ppermute | solution.py:14
  480.4 1.2 copy-start.2
  480.4 1.3 copy-start.7
  (9 other events, 7.2 us)
Sparse Core Ops, SparseCore 0:
  10.4 45.0 all-gather.7
  57.3 40.6 all-gather.3
  99.8 40.6 all-gather.5
  462.6 170.2 reduce-scatter.2
  635.3 47.9 reduce-scatter.4
where the time goes:
time: 695 us; the launch traced here: 692 us
  waiting for transfers between devices  328 us (47%)
  other arithmetic  162 us (23%)
  matrix products  125 us (18%)
  local copies, waits for them, and re-layouts  58.4 us (8%)
  between operations  13.8 us (2%)
    reduce_scatter x1, waiting for transfers between devices, on_device(): lax.psum_scatter(lag_parts.reshape(1, panel_count * panel_len, chan_width...  147 us
    dot_general x33, matrix products, spectrum(): jnp.dot(forward_table, panel_rows.astype(jnp.float32), precision=HIGHER)  99.8 us
    add x16, other arithmetic, lag_step(): forward_sum + spec_product(filter_full, signal_spec, interior, False)  58.1 us
    sub x16, other arithmetic, spec_product(): real_part = left_real * right_real - interior * left_imag * right_imag  50.7 us
    reduce_scatter x1, waiting for transfers between devices, on_device(): lax.psum_scatter(partial_sums[None], 'chan', scatter_dimension=2, tiled=T...  48.6 us
    all_gather x1, waiting for transfers between devices, on_device(): lax.all_gather(signal, 'seq', axis=1, tiled=True)  42.5 us
    all_gather x1, waiting for transfers between devices, on_device(): lax.all_gather(long_filter, 'seq', axis=1, tiled=True)  42.5 us
    all_gather x1, waiting for transfers between devices, on_device(): lax.all_gather(gated[None], 'seq', axis=1, tiled=True)  39 us
  transfers between devices with their start and end apart: 6, of which 6 were waited for; matrix products, arithmetic and copies ran while one was open for 3% of the time, Pallas kernels for 0%

commit v1 on v0

v1 whole, which is shorter than its diff:
```python
import jax
import jax.numpy as jnp
import ml_dtypes
import numpy as np
from jax import lax
from jax.experimental import pallas as pl
from jax.experimental.pallas import tpu as pltpu
from jax.sharding import PartitionSpec as P


def make_tables(panel_len):
    position = np.arange(panel_len)[:, None]
    odd = 2 * np.arange(panel_len)[None, :] + 1
    angles = (position * odd % (4 * panel_len)) * (np.pi / (2 * panel_len))
    table = np.concatenate([np.cos(angles), -np.sin(angles)], axis=1)
    high = table.astype(np.float32).astype(ml_dtypes.bfloat16)
    low = (table - high.astype(np.float64)).astype(np.float32).astype(ml_dtypes.bfloat16)
    return high, low


def dot(left, right):
    return jnp.dot(left, right, preferred_element_type=jnp.float32)


def spectra(rows_ref, high_ref, low_ref):
    rows = rows_ref[...]
    return dot(rows, high_ref[...]) + dot(rows, low_ref[...])


def inverse(spec, high_ref, low_ref):
    panel_len = high_ref.shape[0]
    top = spec.astype(jnp.bfloat16)
    rest = (spec - top.astype(jnp.float32)).astype(jnp.bfloat16)
    dims = (((1,), (1,)), ((), ()))

    def back(left, right):
        return lax.dot_general(left, right, dims, preferred_element_type=jnp.float32)

    high = high_ref[...]
    return (back(top, high) + (back(rest, high) + back(top, low_ref[...]))) * (1.0 / panel_len)


def widen(plain_ref, full_ref, chans, panels):
    half = plain_ref.shape[1] // 2
    sign = 1.0 - 2.0 * (lax.broadcasted_iota(jnp.int32, (chans, half), 1) % 2).astype(jnp.float32)
    full_ref[pl.ds(0, chans), :] = plain_ref[pl.ds(0, chans), :]
    for panel in range(1, panels):
        now, prior = pl.ds(panel * chans, chans), pl.ds((panel - 1) * chans, chans)
        full_ref[now, :half] = plain_ref[now, :half] - sign * plain_ref[prior, half:]
        full_ref[now, half:] = plain_ref[now, half:] + sign * plain_ref[prior, :half]


def pair_sums(out_ref, one_ref, lag_ref, chans, panels, forward):
    half = out_ref.shape[1] // 2
    group = 4
    for lane in range(0, half, 128):

        def step(row, carry):
            start = pl.multiple_of(row * 8, 8)

            def load(ref, panel):
                rows = pl.ds(panel * chans + start, 8)
                return ref[rows, lane : lane + 128], ref[rows, half + lane : half + lane + 128]

            for first in range(0, panels, group):
                sums = [None] * group
                ones = {}
                lags = range(first + group) if forward else range(panels - first)
                for lag in lags:
                    lag_re, lag_im = load(lag_ref, lag)
                    for at in range(group):
                        other = first + at - lag if forward else first + at + lag
                        if not 0 <= other < panels:
                            continue
                        if other not in ones:
                            ones[other] = load(one_ref, other)
                        one_re, one_im = ones[other]
                        if forward:
                            re = one_re * lag_re - one_im * lag_im
                            im = one_re * lag_im + one_im * lag_re
                        else:
                            re = one_re * lag_re + one_im * lag_im
                            im = one_im * lag_re - one_re * lag_im
                        held = sums[at]
                        sums[at] = (re, im) if held is None else (held[0] + re, held[1] + im)
                for at in range(group):
                    rows = pl.ds((first + at) * chans + start, 8)
                    out_ref[rows, lane : lane + 128] = sums[at][0]
                    out_ref[rows, half + lane : half + lane + 128] = sums[at][1]
            return carry

        lax.fori_loop(0, chans // 8, step, 0)


def signal_grad_kernel(
    panels, gated_ref, filter_ref, high_ref, low_ref, grad_ref, gated_spec, filter_full, plain, sums
):
    chans = gated_ref.shape[0] // panels
    gated_spec[...] = spectra(gated_ref, high_ref, low_ref)
    plain[...] = spectra(filter_ref, high_ref, low_ref)
    widen(plain, filter_full, chans, panels)
    pair_sums(sums, gated_spec, filter_full, chans, panels, False)
    grad_ref[...] = inverse(sums[...], high_ref, low_ref).astype(grad_ref.dtype)


def rest_kernel(
    panels, signal_ref, gated_spec, filter_full, high_ref, low_ref, conv_ref, grad_ref, plain, full, sums
):
    chans = signal_ref.shape[0] // panels
    plain[...] = spectra(signal_ref, high_ref, low_ref)
    widen(plain, full, chans, panels)
    pair_sums(sums, plain, filter_full, chans, panels, True)
    conv_ref[...] = inverse(sums[...], high_ref, low_ref).astype(conv_ref.dtype)
    pair_sums(sums, gated_spec, full, chans, panels, False)
    grad_ref[...] = inverse(sums[...], high_ref, low_ref).astype(grad_ref.dtype)


def whole(count):
    return [pl.BlockSpec(memory_space=pltpu.VMEM)] * count


def call(kernel, panels, outs, scratch, *operands):
    return pl.pallas_call(
        lambda *refs: kernel(panels, *refs),
        out_shape=outs,
        in_specs=whole(len(operands)),
        out_specs=whole(len(outs)),
        scratch_shapes=scratch,
        compiler_params=pltpu.CompilerParams(vmem_limit_bytes=40 * 1024 * 1024),
    )(*operands)


def on_device(signal, gate_value, grad_out, long_filter, weight):
    panel_len, width = signal.shape[1:]
    panels = lax.axis_size("seq")
    groups = lax.axis_size("chan")
    chans = width // panels
    rows = panels * chans
    high, low = make_tables(panel_len)
    high, low = jnp.asarray(high), jnp.asarray(low)

    def to_channels(panel):
        parts = panel.T.reshape(panels, chans, panel_len)
        return lax.all_to_all(parts, "seq", 0, 0, tiled=True).reshape(rows, panel_len)

    def to_panels(by_channel):
        parts = by_channel.reshape(panels, chans, panel_len)
        return lax.all_to_all(parts, "seq", 0, 0, tiled=True).reshape(width, panel_len)

    weight_parts = weight[0].reshape(groups, weight.shape[1] // groups, width)
    weights = lax.all_to_all(weight_parts, "chan", 0, 0, tiled=True)

    gated = (gate_value[0].astype(jnp.float32) * grad_out[0].astype(jnp.float32)).astype(
        jnp.bfloat16
    )
    gated_rows = to_channels(gated)
    filter_rows = to_channels(long_filter[0])
    signal_rows = to_channels(signal[0])

    spec = jax.ShapeDtypeStruct((rows, 2 * panel_len), jnp.float32)
    back = jax.ShapeDtypeStruct((rows, panel_len), jnp.bfloat16)
    held = pltpu.VMEM((rows, 2 * panel_len), jnp.float32)
    signal_grad, gated_spec, filter_full = call(
        signal_grad_kernel, panels, (back, spec, spec), [held, held], gated_rows, filter_rows, high, low
    )
    conv, filter_grad = call(
        rest_kernel,
        panels,
        (back, back),
        [held, held, held],
        signal_rows,
        gated_spec,
        filter_full,
        high,
        low,
    )
    signal_grad = to_panels(signal_grad)
    sections = lax.axis_size("pipe")
    received = lax.ppermute(
        signal_grad, "pipe", [(i, (i - 1) % sections) for i in range(sections)]
    )
    copies = jnp.broadcast_to(received[None], (groups, width, panel_len))
    all_received = lax.all_to_all(copies, "chan", 0, 0, tiled=True)
    input_grad = lax.dot_general(
        all_received, weights, (((0, 1), (0, 2)), ((), ())), preferred_element_type=jnp.float32
    ).astype(jnp.bfloat16)
    conv = to_panels(conv).T
    gate_grad = (grad_out[0].astype(jnp.float32) * conv.astype(jnp.float32)).astype(jnp.bfloat16)
    filter_grad = to_panels(filter_grad).T.astype(jnp.float32)
    return gate_grad[None], filter_grad[None], input_grad[None]


def solution(mesh):
    return jax.shard_map(
        on_device,
        mesh=mesh,
        in_specs=(
            P("pipe", "seq", "chan"),
            P("pipe", "seq", "chan"),
            P("pipe", "seq", "chan"),
            P("pipe", "seq", "chan"),
            P("pipe", None, "chan"),
        ),
        out_specs=(P("pipe", "seq", "chan"), P("pipe", "seq", "chan"), P("pipe", "seq", "chan")),
        check_vma=False,
    )
```

time: 695 us -> 183 us (0.26)
  waiting for transfers between devices: 328 us -> 83.4 us
  other arithmetic: 162 us -> 0.9 us
  matrix products: 125 us -> 4.26 us
  local copies, waits for them, and re-layouts: 58.4 us -> 8.68 us
  blocking collectives: 0 us -> 49.6 us
  starting transfers between devices: 1.38 us -> 25.1 us
  between operations: 13.8 us -> 0.78 us
  Pallas kernels: 0 us -> 9.07 us
    reduce_scatter x2 -> x0, waiting for transfers between devices: 196 us -> none  [the longest x1 147 us: on_device(): lax.psum_scatter(lag_parts.reshape(1, panel_count * panel_len, chan_width...]
    all_gather x3 -> x0, waiting for transfers between devices: 124 us -> none  [the longest x1 42.5 us: on_device(): lax.all_gather(signal, 'seq', axis=1, tiled=True)]
    dot_general x38 -> x1, matrix products: 125 us -> 4.26 us  [on_device(): lax.dot_general(all_received, weights, (((0, 1), (0, 2)), ((), ())), pref...]
    all_to_all x0 -> x5, waiting for transfers between devices: none -> 83.4 us  [the longest x1 47.2 us: on_device(): weights = lax.all_to_all(weight_parts, 'chan', 0, 0, tiled=True)]
    add x16 -> x0, other arithmetic: 58.1 us -> none  [lag_step(): forward_sum + spec_product(filter_full, signal_spec, interior, False)]
    sub x33 -> x0, other arithmetic: 50.8 us -> none  [the longest x16 50.7 us: spec_product(): real_part = left_real * right_real - interior * left_imag * right_imag]
    all_to_all x0 -> x3, blocking collectives: none -> 49.6 us  [the longest x2 29.1 us: to_panels(): lax.all_to_all(parts, 'seq', 0, 0, tiled=True).reshape(width, panel_len)]
    while x113 -> x0, local copies, waits for them, and re-layouts: 38.1 us -> none
  transfers between devices with their start and end apart: 6 -> 6, of which waited for: 6 -> 5; matrix products, arithmetic and copies ran while one was open for 3% -> 3% of each run, Pallas kernels for 0% -> 2%
where the time goes in v1:
time: 183 us; the launch traced here: 182 us
  waiting for transfers between devices  83.4 us (46%)
  blocking collectives  49.6 us (27%)
  starting transfers between devices  25.1 us (14%)
  Pallas kernels  9.07 us (5%)
  local copies, waits for them, and re-layouts  8.68 us (5%)
  matrix products  4.26 us (2%)
    all_to_all x1, waiting for transfers between devices, on_device(): weights = lax.all_to_all(weight_parts, 'chan', 0, 0, tiled=True)  47.2 us
    all_to_all x2, blocking collectives, to_panels(): lax.all_to_all(parts, 'seq', 0, 0, tiled=True).reshape(width, panel_len)  29.1 us
    all_to_all x3, waiting for transfers between devices, to_channels(): lax.all_to_all(parts, 'seq', 0, 0, tiled=True).reshape(rows, panel_len)  26.1 us
    all_to_all x1, blocking collectives, on_device(): all_received = lax.all_to_all(copies, 'chan', 0, 0, tiled=True)  20.5 us
    all_to_all x3, starting transfers between devices, to_channels(): lax.all_to_all(parts, 'seq', 0, 0, tiled=True).reshape(rows, panel_len)  15.6 us
    all_to_all x1, waiting for transfers between devices, to_panels(): lax.all_to_all(parts, 'seq', 0, 0, tiled=True).reshape(width, panel_len)  10.2 us
    pallas_call x2, Pallas kernels, call(): pl.pallas_call(lambda *refs: kernel(panels, *refs), out_shape=outs, in_sp...  9.07 us
    unnamed x16, local copies, waits for them, and re-layouts  8.46 us
  transfers between devices with their start and end apart: 6, of which 5 were waited for; matrix products, arithmetic and copies ran while one was open for 3% of the time, Pallas kernels for 2%

profile of v1, /device:TPU:6, one launch (start us, length us, event | category | flops | bytes accessed | tf_op | source)
XLA Modules:
  0.0 181.8 jit_solution(8039329964117987380)
XLA Ops:
  0.6 0.0 copy-start
  0.6 0.0 copy-start.1
  0.7 1.1 copy.16
  1.8 0.0 copy-start.3
  1.8 1.2 copy.18
  3.0 0.8 fusion.2
  3.8 0.0 copy-done.3
  3.8 8.6 %all-to-all-start.1 = ((bf16[16,32,256]{2,1,0:T(8,128)(2,1)}), bf16[16,32,256]{2,1,0:T(8,128)(2,1)S(1)}, u32[]{:S(2)}, u32[]{:S(2)}) async-start(bf16[16,32,256]{2,1,0:T(8,128)(2,1)} %bitcast.8), calls=%async_computation.1 | async-start | bytes 524288 | tf_op jit(solution)/shard_map/all_to_all | solution.py:144
  12.3 1.8 copy.19
  14.1 9.4 %all-to-all-done.1 = bf16[16,32,256]{2,1,0:T(8,128)(2,1)S(1)} async-done(((bf16[16,32,256]{2,1,0:T(8,128)(2,1)}), bf16[16,32,256]{2,1,0:T(8,128)(2,1)S(1)}, u32[]{:S(2)}, u32[]{:S(2)}) %all-to-all-start.1) | async-done | bytes 262176 | tf_op jit(solution)/shard_map/all_to_all | solution.py:144
  23.5 3.5 %all-to-all-start.2 = ((bf16[16,32,256]{2,1,0:T(8,128)(2,1)}), bf16[16,32,256]{2,1,0:T(8,128)(2,1)S(1)}, u32[]{:S(2)}, u32[]{:S(2)}) async-start(bf16[16,32,256]{2,1,0:T(8,128)(2,1)} %bitcast.12), calls=%async_computation.2 | async-start | bytes 524288 | tf_op jit(solution)/shard_map/all_to_all | solution.py:144
  27.1 1.8 copy.17
  28.9 9.5 %all-to-all-done.2 = bf16[16,32,256]{2,1,0:T(8,128)(2,1)S(1)} async-done(((bf16[16,32,256]{2,1,0:T(8,128)(2,1)}), bf16[16,32,256]{2,1,0:T(8,128)(2,1)S(1)}, u32[]{:S(2)}, u32[]{:S(2)}) %all-to-all-start.2) | async-done | bytes 262176 | tf_op jit(solution)/shard_map/all_to_all | solution.py:144
  38.4 3.5 %all-to-all-start = ((bf16[16,32,256]{2,1,0:T(8,128)(2,1)}), bf16[16,32,256]{2,1,0:T(8,128)(2,1)S(1)}, u32[]{:S(2)}, u32[]{:S(2)}) async-start(bf16[16,32,256]{2,1,0:T(8,128)(2,1)} %bitcast.3), calls=%async_computation | async-start | bytes 524288 | tf_op jit(solution)/shard_map/all_to_all | solution.py:144
  41.9 0.0 copy-done
  41.9 0.0 copy-done.1
  42.0 3.4 %shard_map.94 = (bf16[512,256]{1,0:T(8,128)(2,1)S(1)}, f32[512,512]{1,0:T(8,128)S(1)}, f32[512,512]{1,0:T(8,128)S(1)}) custom-call(bf16[512,256]{1,0:T(8,128)(2,1)S(1)} %bitcast.56, bf16[512,256]{1,0:T(8,128)(2,1)S(1)} %bitcast.57, bf16[256,512]{1,0:T(8,128)(2,1)S(1)} %copy-done, bf16[256,512]{1,0:T(8,128)(2,1)S(1)} %copy-done.1), custom_call_target="tpu_custom_call" | custom-call | tf_op jit(solution)/shard_map/pallas_call | solution.py:123
  45.3 0.0 copy-start.2
  45.4 0.7 copy-done.2
  46.0 7.1 %all-to-all-done = bf16[16,32,256]{2,1,0:T(8,128)(2,1)S(1)} async-done(((bf16[16,32,256]{2,1,0:T(8,128)(2,1)}), bf16[16,32,256]{2,1,0:T(8,128)(2,1)S(1)}, u32[]{:S(2)}, u32[]{:S(2)}) %all-to-all-start) | async-done | bytes 262176 | tf_op jit(solution)/shard_map/all_to_all | solution.py:144
  53.2 5.7 %shard_map.95 = (bf16[512,256]{1,0:T(8,128)(2,1)S(1)}, bf16[512,256]{1,0:T(8,128)(2,1)}) custom-call(bf16[512,256]{1,0:T(8,128)(2,1)S(1)} %bitcast.58, f32[512,512]{1,0:T(8,128)S(1)} %get-tuple-element.8.refs_1_, f32[512,512]{1,0:T(8,128)S(1)} %get-tuple-element.9.refs_2_, bf16[256,512]{1,0:T(8,128)(2,1)S(1)} %copy-done, bf16[256,512]{1,0:T(8,128)(2,1)S(1)} %copy-done.1), custom_call_target="tpu_custom_call" | custom-call | tf_op jit(solution)/shard_map/pallas_call | solution.py:123
  58.9 14.2 %all_to_all.40 = bf16[16,32,256]{2,1,0:T(8,128)(2,1)S(1)} all-to-all(bf16[16,32,256]{2,1,0:T(8,128)(2,1)S(1)} %bitcast.60), channel_id=1, replica_groups=mesh['pipe'=4,'seq'=16,'chan'=4] {'seq'}, dimensions={0} | all-to-all | bytes 524288 | tf_op jit(solution)/shard_map/all_to_all | solution.py:148
  73.1 14.9 %all_to_all.41 = bf16[16,32,256]{2,1,0:T(8,128)(2,1)S(1)} all-to-all(bf16[16,32,256]{2,1,0:T(8,128)(2,1)} %bitcast.59), channel_id=1, replica_groups=mesh['pipe'=4,'seq'=16,'chan'=4] {'seq'}, dimensions={0} | all-to-all | bytes 524288 | tf_op jit(solution)/shard_map/all_to_all | solution.py:148
  88.0 3.5 %all-to-all-start.4 = ((bf16[16,32,256]{2,1,0:T(8,128)(2,1)}), bf16[16,32,256]{2,1,0:T(8,128)(2,1)S(1)}, u32[]{:S(2)}, u32[]{:S(2)}) async-start(bf16[16,32,256]{2,1,0:T(8,128)(2,1)} %bitcast.18), calls=%async_computation.4 | async-start | bytes 524288 | tf_op jit(solution)/shard_map/all_to_all | solution.py:148
  91.5 0.1 copy.20
  91.7 0.9 collective-permute-start
  92.6 10.2 %all-to-all-done.4 = bf16[16,32,256]{2,1,0:T(8,128)(2,1)S(1)} async-done(((bf16[16,32,256]{2,1,0:T(8,128)(2,1)}), bf16[16,32,256]{2,1,0:T(8,128)(2,1)S(1)}, u32[]{:S(2)}, u32[]{:S(2)}) %all-to-all-start.4) | async-done | bytes 262176 | tf_op jit(solution)/shard_map/all_to_all | solution.py:148
  102.7 0.0 collective-permute-done
  102.7 0.1 broadcast_in_dim.21
  102.8 20.5 %all_to_all.42 = bf16[4,512,256]{1,2,0:T(8,128)(2,1)S(1)} all-to-all(bf16[4,512,256]{1,2,0:T(8,128)(2,1)S(1)} %broadcast_in_dim.21), channel_id=1, replica_groups=mesh['pipe'=4,'seq'=16,'chan'=4] {'chan'}, dimensions={0} | all-to-all | bytes 2097152 | tf_op jit(solution)/shard_map/all_to_all | solution.py:183
  123.4 0.0 copy-start.4
  123.4 5.0 %all-to-all-start.7 = ((bf16[4,1024,512]{2,1,0:T(8,128)(2,1)}), bf16[4,1024,512]{2,1,0:T(8,128)(2,1)}, u32[]{:S(2)}, u32[]{:S(2)}) async-start(bf16[4,1024,512]{2,1,0:T(8,128)(2,1)} %bitcast.61), calls=%async_computation.7 | async-start | bytes 8388608 | tf_op jit(solution)/shard_map/all_to_all | solution.py:151
  128.4 0.0 copy-done.4
  128.4 0.1 fusion.4
  128.5 0.8 copy.21
  129.3 0.1 convert_bitcast_fusion
  129.4 1.0 copy.22
  130.4 47.2 %all-to-all-done.7 = bf16[4,1024,512]{2,1,0:T(8,128)(2,1)} async-done(((bf16[4,1024,512]{2,1,0:T(8,128)(2,1)}), bf16[4,1024,512]{2,1,0:T(8,128)(2,1)}, u32[]{:S(2)}, u32[]{:S(2)}) %all-to-all-start.7) | async-done | bytes 4194336 | tf_op jit(solution)/shard_map/all_to_all | solution.py:151
  177.5 4.3 %fusion.1 = bf16[1,256,1024]{2,1,0:T(8,128)(2,1)} fusion(bf16[4,512,256]{1,2,0:T(8,128)(2,1)S(1)} %all_to_all.42, bf16[4,1024,512]{2,1,0:T(8,128)(2,1)} %all-to-all-done.7), kind=kOutput, calls=%fused_computation.2 | convolution fusion | flops 1074003968 | bytes 5767168 | tf_op jit(solution)/shard_map/dot_general | solution.py:184
Async XLA Ops:
  0.6 41.3 %copy-start = (bf16[256,512]{1,0:T(8,128)(2,1)S(1)}, bf16[256,512]{1,0:T(8,128)(2,1)}, u32[]{:S(2)}) copy-start(bf16[256,512]{1,0:T(8,128)(2,1)} %constant.4.clone.refs_2_.refs_3_) | copy-start | bytes 786436
  0.6 41.3 %copy-start.1 = (bf16[256,512]{1,0:T(8,128)(2,1)S(1)}, bf16[256,512]{1,0:T(8,128)(2,1)}, u32[]{:S(2)}) copy-start(bf16[256,512]{1,0:T(8,128)(2,1)} %constant.5.clone.refs_3_.refs_4_) | copy-start | bytes 786436
  1.8 2.0 %copy-start.3 = (bf16[1,256,512]{1,2,0:T(8,128)(2,1)}, bf16[1,256,512]{1,2,0:T(8,128)(2,1)S(1)}, u32[]{:S(2)}) copy-start(bf16[1,256,512]{1,2,0:T(8,128)(2,1)S(1)} %copy.16) | copy-start | bytes 786436
  3.8 19.8 %all-to-all-start.1 = ((bf16[16,32,256]{2,1,0:T(8,128)(2,1)}), bf16[16,32,256]{2,1,0:T(8,128)(2,1)S(1)}, u32[]{:S(2)}, u32[]{:S(2)}) async-start(bf16[16,32,256]{2,1,0:T(8,128)(2,1)} %bitcast.8), calls=%async_computation.1 | async-start | bytes 524288 | tf_op jit(solution)/shard_map/all_to_all | solution.py:144
  23.5 14.9 %all-to-all-start.2 = ((bf16[16,32,256]{2,1,0:T(8,128)(2,1)}), bf16[16,32,256]{2,1,0:T(8,128)(2,1)S(1)}, u32[]{:S(2)}, u32[]{:S(2)}) async-start(bf16[16,32,256]{2,1,0:T(8,128)(2,1)} %bitcast.12), calls=%async_computation.2 | async-start | bytes 524288 | tf_op jit(solution)/shard_map/all_to_all | solution.py:144
  38.4 14.8 %all-to-all-start = ((bf16[16,32,256]{2,1,0:T(8,128)(2,1)}), bf16[16,32,256]{2,1,0:T(8,128)(2,1)S(1)}, u32[]{:S(2)}, u32[]{:S(2)}) async-start(bf16[16,32,256]{2,1,0:T(8,128)(2,1)} %bitcast.3), calls=%async_computation | async-start | bytes 524288 | tf_op jit(solution)/shard_map/all_to_all | solution.py:144
  45.3 0.7 copy-start.2
  88.0 14.8 %all-to-all-start.4 = ((bf16[16,32,256]{2,1,0:T(8,128)(2,1)}), bf16[16,32,256]{2,1,0:T(8,128)(2,1)S(1)}, u32[]{:S(2)}, u32[]{:S(2)}) async-start(bf16[16,32,256]{2,1,0:T(8,128)(2,1)} %bitcast.18), calls=%async_computation.4 | async-start | bytes 524288 | tf_op jit(solution)/shard_map/all_to_all | solution.py:148
  91.7 11.1 %collective-permute-start = (bf16[512,256]{0,1:T(8,128)(2,1)S(1)}, bf16[512,256]{0,1:T(8,128)(2,1)S(1)}, u32[]{:S(2)}, u32[]{:S(2)}) collective-permute-start(bf16[512,256]{0,1:T(8,128)(2,1)S(1)} %copy.20), channel_id=1, source_target_pairs={{0,192},{64,0},{128,64},{192,128},{1,193},{65,1},{129,65},{193,129... | collective-permute-start | bytes 786440 | tf_op jit(solution)/shard_map/ppermute | solution.py:179
  123.4 5.0 %copy-start.4 = (bf16[1,256,512]{1,2,0:T(8,128)(2,1)S(1)}, bf16[1,256,512]{1,2,0:T(8,128)(2,1)}, u32[]{:S(2)}) copy-start(bf16[1,256,512]{1,2,0:T(8,128)(2,1)} %copy-done.3) | copy-start | bytes 786436
  123.4 54.2 %all-to-all-start.7 = ((bf16[4,1024,512]{2,1,0:T(8,128)(2,1)}), bf16[4,1024,512]{2,1,0:T(8,128)(2,1)}, u32[]{:S(2)}, u32[]{:S(2)}) async-start(bf16[4,1024,512]{2,1,0:T(8,128)(2,1)} %bitcast.61), calls=%async_computation.7 | async-start | bytes 8388608 | tf_op jit(solution)/shard_map/all_to_all | solution.py:151

commit v2 on v1

--- a/solution.py
+++ b/solution.py
@@ -22,8 +22,7 @@
     return jnp.dot(left, right, preferred_element_type=jnp.float32)
 
 
-def spectra(rows_ref, high_ref, low_ref):
-    rows = rows_ref[...]
+def spectra(rows, high_ref, low_ref):
     return dot(rows, high_ref[...]) + dot(rows, low_ref[...])
 
 
@@ -92,27 +91,57 @@
         lax.fori_loop(0, chans // 8, step, 0)
 
 
+def by_rows(ref, at, chans):
+    part = ref[:, at * chans : (at + 1) * chans, :]
+    return part.reshape(part.shape[0] * chans, part.shape[2])
+
+
+def send_kernel(panels, signal_ref, gate_ref, grad_ref, filter_ref, out_ref):
+    chans = out_ref.shape[1] // 3
+
+    def put(at, panel):
+        parts = panel.T.reshape(panels, chans, panel.shape[0])
+        out_ref[:, at * chans : (at + 1) * chans, :] = parts
+
+    gated = gate_ref[...].astype(jnp.float32) * grad_ref[...].astype(jnp.float32)
+    put(0, gated.astype(jnp.bfloat16))
+    put(1, filter_ref[...])
+    put(2, signal_ref[...])
+
+
 def signal_grad_kernel(
-    panels, gated_ref, filter_ref, high_ref, low_ref, grad_ref, gated_spec, filter_full, plain, sums
+    panels, parts_ref, high_ref, low_ref, grad_ref, gated_spec, filter_full, plain, sums
 ):
-    chans = gated_ref.shape[0] // panels
-    gated_spec[...] = spectra(gated_ref, high_ref, low_ref)
-    plain[...] = spectra(filter_ref, high_ref, low_ref)
+    chans = parts_ref.shape[1] // 3
+    gated_spec[...] = spectra(by_rows(parts_ref, 0, chans), high_ref, low_ref)
+    plain[...] = spectra(by_rows(parts_ref, 1, chans), high_ref, low_ref)
     widen(plain, filter_full, chans, panels)
     pair_sums(sums, gated_spec, filter_full, chans, panels, False)
     grad_ref[...] = inverse(sums[...], high_ref, low_ref).astype(grad_ref.dtype)
 
 
 def rest_kernel(
-    panels, signal_ref, gated_spec, filter_full, high_ref, low_ref, conv_ref, grad_ref, plain, full, sums
+    panels, parts_ref, gated_spec, filter_full, high_ref, low_ref, out_ref, plain, full, sums
 ):
-    chans = signal_ref.shape[0] // panels
-    plain[...] = spectra(signal_ref, high_ref, low_ref)
+    chans = parts_ref.shape[1] // 3
+
+    def put(at):
+        grad = inverse(sums[...], high_ref, low_ref).astype(out_ref.dtype)
+        out_ref[:, at * chans : (at + 1) * chans, :] = grad.reshape(panels, chans, grad.shape[1])
+
+    plain[...] = spectra(by_rows(parts_ref, 2, chans), high_ref, low_ref)
     widen(plain, full, chans, panels)
     pair_sums(sums, plain, filter_full, chans, panels, True)
-    conv_ref[...] = inverse(sums[...], high_ref, low_ref).astype(conv_ref.dtype)
+    put(0)
     pair_sums(sums, gated_spec, full, chans, panels, False)
-    grad_ref[...] = inverse(sums[...], high_ref, low_ref).astype(grad_ref.dtype)
+    put(1)
+
+
+def finish_kernel(panels, parts_ref, grad_ref, gate_out, filter_out):
+    chans = parts_ref.shape[1] // 2
+    conv = by_rows(parts_ref, 0, chans).T.astype(jnp.float32)
+    gate_out[...] = (grad_ref[...].astype(jnp.float32) * conv).astype(gate_out.dtype)
+    filter_out[...] = by_rows(parts_ref, 1, chans).T.astype(jnp.float32)
 
 
 def whole(count):
@@ -130,6 +159,11 @@
     )(*operands)
 
 
+def shifted(x, axis, by):
+    length = lax.axis_size(axis)
+    return lax.ppermute(x, axis, [(i, (i + by) % length) for i in range(length)])
+
+
 def on_device(signal, gate_value, grad_out, long_filter, weight):
     panel_len, width = signal.shape[1:]
     panels = lax.axis_size("seq")
@@ -139,54 +173,77 @@
     high, low = make_tables(panel_len)
     high, low = jnp.asarray(high), jnp.asarray(low)
 
-    def to_channels(panel):
-        parts = panel.T.reshape(panels, chans, panel_len)
-        return lax.all_to_all(parts, "seq", 0, 0, tiled=True).reshape(rows, panel_len)
-
-    def to_panels(by_channel):
-        parts = by_channel.reshape(panels, chans, panel_len)
-        return lax.all_to_all(parts, "seq", 0, 0, tiled=True).reshape(width, panel_len)
-
+    def swapped(parts):
+        return lax.all_to_all(parts, "seq", 0, 0, tiled=True)
+
+    def shape(*dims, dtype=jnp.bfloat16):
+        return jax.ShapeDtypeStruct(dims, dtype)
+
+    (sent,) = call(
+        send_kernel,
+        panels,
+        (shape(panels, 3 * chans, panel_len),),
+        [],
+        signal[0],
+        gate_value[0],
+        grad_out[0],
+        long_filter[0],
+    )
+    parts = swapped(sent)
+
+    my_group = lax.axis_index("chan")
     weight_parts = weight[0].reshape(groups, weight.shape[1] // groups, width)
-    weights = lax.all_to_all(weight_parts, "chan", 0, 0, tiled=True)
-
-    gated = (gate_value[0].astype(jnp.float32) * grad_out[0].astype(jnp.float32)).astype(
-        jnp.bfloat16
-    )
-    gated_rows = to_channels(gated)
-    filter_rows = to_channels(long_filter[0])
-    signal_rows = to_channels(signal[0])
-
-    spec = jax.ShapeDtypeStruct((rows, 2 * panel_len), jnp.float32)
-    back = jax.ShapeDtypeStruct((rows, panel_len), jnp.bfloat16)
+
+    def weight_for(by):
+        return lax.dynamic_index_in_dim(
+            weight_parts, lax.rem(my_group + by, groups), 0, False
+        )
+
+    weights = [weight_for(0)] + [shifted(weight_for(by), "chan", by) for by in range(1, groups)]
+
+    parts, weights[1], weights[-1] = lax.optimization_barrier((parts, weights[1], weights[-1]))
+
+    spec = shape(rows, 2 * panel_len, dtype=jnp.float32)
     held = pltpu.VMEM((rows, 2 * panel_len), jnp.float32)
     signal_grad, gated_spec, filter_full = call(
-        signal_grad_kernel, panels, (back, spec, spec), [held, held], gated_rows, filter_rows, high, low
-    )
-    conv, filter_grad = call(
+        signal_grad_kernel,
+        panels,
+        (shape(rows, panel_len), spec, spec),
+        [held, held],
+        parts,
+        high,
+        low,
+    )
+    signal_grad = swapped(signal_grad.reshape(panels, chans, panel_len)).reshape(width, panel_len)
+    (rest,) = call(
         rest_kernel,
         panels,
-        (back, back),
+        (shape(panels, 2 * chans, panel_len),),
         [held, held, held],
-        signal_rows,
+        parts,
         gated_spec,
         filter_full,
         high,
         low,
     )
-    signal_grad = to_panels(signal_grad)
-    sections = lax.axis_size("pipe")
-    received = lax.ppermute(
-        signal_grad, "pipe", [(i, (i - 1) % sections) for i in range(sections)]
-    )
-    copies = jnp.broadcast_to(received[None], (groups, width, panel_len))
-    all_received = lax.all_to_all(copies, "chan", 0, 0, tiled=True)
-    input_grad = lax.dot_general(
-        all_received, weights, (((0, 1), (0, 2)), ((), ())), preferred_element_type=jnp.float32
-    ).astype(jnp.bfloat16)
-    conv = to_panels(conv).T
-    gate_grad = (grad_out[0].astype(jnp.float32) * conv.astype(jnp.float32)).astype(jnp.bfloat16)
-    filter_grad = to_panels(filter_grad).T.astype(jnp.float32)
+    signal_grad, rest, weights[2] = lax.optimization_barrier((signal_grad, rest, weights[2]))
+    received = shifted(signal_grad, "pipe", -1)
+    rest = swapped(rest)
+    total = 0.0
+    for by in range(groups):
+        held_by = received if by == 0 else shifted(received, "chan", by)
+        total = total + lax.dot_general(
+            held_by, weights[by], (((0,), (1,)), ((), ())), preferred_element_type=jnp.float32
+        )
+    input_grad = total.astype(jnp.bfloat16)
+    gate_grad, filter_grad = call(
+        finish_kernel,
+        panels,
+        (shape(panel_len, width), shape(panel_len, width, dtype=jnp.float32)),
+        [],
+        rest,
+        grad_out[0],
+    )
     return gate_grad[None], filter_grad[None], input_grad[None]
 
 

time: 183 us -> 126 us (0.69)
  blocking collectives: 49.6 us -> 0 us
  waiting for transfers between devices: 83.4 us -> 69.1 us
  starting transfers between devices: 25.1 us -> 28.7 us
  Pallas kernels: 9.07 us -> 11.3 us
  matrix products: 4.26 us -> 6.41 us
    all_to_all x5 -> x3, waiting for transfers between devices: 83.4 us -> 5.44 us  [swapped(): return lax.all_to_all(parts, 'seq', 0, 0, tiled=True)]
    ppermute x1 -> x7, waiting for transfers between devices: 0.01 us -> 63.6 us  [shifted(): lax.ppermute(x, axis, [(i, (i + by) % length) for i in range(length)])]
    all_to_all x3 -> x0, blocking collectives: 49.6 us -> none  [the longest x2 29.1 us: to_panels(): lax.all_to_all(parts, 'seq', 0, 0, tiled=True).reshape(width, panel_len)]
    ppermute x1 -> x7, starting transfers between devices: 0.91 us -> 9.38 us  [shifted(): lax.ppermute(x, axis, [(i, (i + by) % length) for i in range(length)])]
    all_to_all x5 -> x3, starting transfers between devices: 24.2 us -> 19.3 us  [swapped(): return lax.all_to_all(parts, 'seq', 0, 0, tiled=True)]
    squeeze x0 -> x1, local copies, waits for them, and re-layouts: none -> 3.06 us  [weight_for(): lax.dynamic_index_in_dim(weight_parts, lax.rem(my_group + by, groups), 0,...]
    unnamed x16 -> x20, local copies, waits for them, and re-layouts: 8.46 us -> 5.47 us
    pallas_call x2 -> x4, Pallas kernels: 9.07 us -> 11.3 us  [call(): pl.pallas_call(lambda *refs: kernel(panels, *refs), out_shape=outs, in_sp...]
  transfers between devices with their start and end apart: 6 -> 10, of which waited for: 5 -> 6; matrix products, arithmetic and copies ran while one was open for 3% -> 8% of each run, Pallas kernels for 2% -> 7%
where the time goes in v2:
time: 126 us; the launch traced here: 125 us
  waiting for transfers between devices  69.1 us (55%)
  starting transfers between devices  28.7 us (23%)
  Pallas kernels  11.3 us (9%)
  local copies, waits for them, and re-layouts  8.53 us (7%)
  matrix products  6.41 us (5%)
    ppermute x7, waiting for transfers between devices, shifted(): lax.ppermute(x, axis, [(i, (i + by) % length) for i in range(length)])  63.6 us
    all_to_all x3, starting transfers between devices, swapped(): return lax.all_to_all(parts, 'seq', 0, 0, tiled=True)  19.3 us
    pallas_call x4, Pallas kernels, call(): pl.pallas_call(lambda *refs: kernel(panels, *refs), out_shape=outs, in_sp...  11.3 us
    ppermute x7, starting transfers between devices, shifted(): lax.ppermute(x, axis, [(i, (i + by) % length) for i in range(length)])  9.38 us
    dot_general x4, matrix products, on_device(): lax.dot_general(held_by, weights[by], (((0,), (1,)), ((), ())), preferred...  6.41 us
    unnamed x20, local copies, waits for them, and re-layouts  5.47 us
    all_to_all x3, waiting for transfers between devices, swapped(): return lax.all_to_all(parts, 'seq', 0, 0, tiled=True)  5.44 us
    squeeze x1, local copies, waits for them, and re-layouts, weight_for(): lax.dynamic_index_in_dim(weight_parts, lax.rem(my_group + by, groups), 0,...  3.06 us
  transfers between devices with their start and end apart: 10, of which 6 were waited for; matrix products, arithmetic and copies ran while one was open for 8% of the time, Pallas kernels for 7%

profile of v2, /device:TPU:6, one launch (start us, length us, event | category | flops | bytes accessed | tf_op | source)
XLA Modules:
  0.0 124.8 jit_solution(8187988320213285397)
XLA Ops:
  0.6 0.0 copy-start
  0.6 0.9 copy-done
  1.6 0.0 copy-start.4
  1.6 0.9 copy-done.4
  2.5 0.9 copy-done.5
  3.5 0.0 copy-start.6
  3.5 0.9 copy-done.6
  4.4 1.1 shard_map.94
  5.6 0.0 copy-start.2
  5.6 0.0 copy-start.3
  5.6 8.7 %all-to-all-start = ((bf16[16,96,256]{2,1,0:T(8,128)(2,1)}), bf16[16,96,256]{2,1,0:T(8,128)(2,1)S(1)}, u32[]{:S(2)}, u32[]{:S(2)}) async-start(bf16[16,96,256]{2,1,0:T(8,128)(2,1)} %shard_map.94), calls=%async_computation | async-start | bytes 1572864 | tf_op jit(solution)/shard_map/all_to_all | solution.py:177
  14.3 3.1 %dynamic-slice_bitcast_fusion = (bf16[1024,512]{1,0:T(8,128)(2,1)}, bf16[1024,512]{1,0:T(8,128)(2,1)S(1)}, bf16[1024,512]{1,0:T(8,128)(2,1)S(1)}) fusion(bf16[4,1024,512]{2,1,0:T(8,128)(2,1)} %bitcast.33, s32[]{:T(128)S(6)} %select_n.15, s32[]{:T(128)S(6)} %select_n.14, s32[]{:T(128)S(6)} %select_n.13), kind=kLoop, calls=%fused_computation.8 | loop fusion | bytes 6291468 | tf_op jit(solution)/shard_map/jit(dynamic_index_in_dim)/squeeze | solution.py:198
  17.4 3.0 %collective-permute-start.1 = (bf16[1024,512]{1,0:T(8,128)(2,1)S(1)}, bf16[1024,512]{1,0:T(8,128)(2,1)S(1)}, u32[]{:S(2)}, u32[]{:S(2)}) collective-permute-start(bf16[1024,512]{1,0:T(8,128)(2,1)S(1)} %get-tuple-element.26), channel_id=1, source_target_pairs={{0,3},{1,0},{2,1},{3,2},{4,7},{5,4},{6,5},{7,6},{8,11},{9,8},{10,9... | collective-permute-start | bytes 3145736 | tf_op jit(solution)/shard_map/ppermute | solution.py:164
  20.4 0.0 collective-permute-start
  20.4 2.2 %collective-permute-start.2 = (bf16[1024,512]{1,0:T(8,128)(2,1)}, bf16[1024,512]{1,0:T(8,128)(2,1)}, u32[]{:S(2)}, u32[]{:S(2)}) collective-permute-start(bf16[1024,512]{1,0:T(8,128)(2,1)} %get-tuple-element.25), channel_id=1, source_target_pairs={{0,2},{1,3},{2,0},{3,1},{4,6},{5,7},{6,4},{7,5},{8,10},{9,11},{10,... | collective-permute-start | bytes 3145736 | tf_op jit(solution)/shard_map/ppermute | solution.py:164
  22.6 43.2 %collective-permute-done.1 = bf16[1024,512]{1,0:T(8,128)(2,1)S(1)} collective-permute-done((bf16[1024,512]{1,0:T(8,128)(2,1)S(1)}, bf16[1024,512]{1,0:T(8,128)(2,1)S(1)}, u32[]{:S(2)}, u32[]{:S(2)}) %collective-permute-start.1) | collective-permute-done | bytes 1048608 | tf_op jit(solution)/shard_map/ppermute | solution.py:164
  65.8 0.0 copy-start.8
  65.8 1.0 copy-done.8
  66.8 2.6 %collective-permute-done = bf16[1024,512]{1,0:T(8,128)(2,1)} collective-permute-done((bf16[1024,512]{1,0:T(8,128)(2,1)S(1)}, bf16[1024,512]{1,0:T(8,128)(2,1)}, u32[]{:S(2)}, u32[]{:S(2)}) %collective-permute-start) | collective-permute-done | bytes 1048608 | tf_op jit(solution)/shard_map/ppermute | solution.py:164
  69.3 0.0 all-to-all-done.refs_0_
  69.3 0.0 copy-done.2
  69.3 0.0 copy-done.3
  69.3 3.4 %shard_map.95 = (bf16[512,256]{1,0:T(8,128)(2,1)S(1)}, f32[512,512]{1,0:T(8,128)S(1)}, f32[512,512]{1,0:T(8,128)S(1)}) custom-call(bf16[16,96,256]{2,1,0:T(8,128)(2,1)S(1)} %all-to-all-done.refs_0_, bf16[256,512]{1,0:T(8,128)(2,1)S(1)} %copy-done.3, bf16[256,512]{1,0:T(8,128)(2,1)S(1)} %copy-done.2), custom_call_target="tpu_custom_call" | custom-call | tf_op jit(solution)/shard_map/pallas_call | solution.py:152
  72.7 0.0 copy-start.7
  72.7 0.7 copy-done.7
  73.4 7.0 %all-to-all-start.1 = ((bf16[16,32,256]{2,1,0:T(8,128)(2,1)}), bf16[16,32,256]{2,1,0:T(8,128)(2,1)}, u32[]{:S(2)}, u32[]{:S(2)}) async-start(bf16[16,32,256]{2,1,0:T(8,128)(2,1)} %bitcast.32), calls=%async_computation.1 | async-start | bytes 524288 | tf_op jit(solution)/shard_map/all_to_all | solution.py:177
  80.5 5.8 %shard_map.96 = bf16[16,64,256]{2,1,0:T(8,128)(2,1)} custom-call(bf16[16,96,256]{2,1,0:T(8,128)(2,1)S(1)} %all-to-all-done.refs_0_, f32[512,512]{1,0:T(8,128)S(1)} %get-tuple-element.16.refs_1_, f32[512,512]{1,0:T(8,128)S(1)} %get-tuple-element.17.refs_2_, bf16[256,512]{1,0:T(8,128)(2,1)S(1)} %copy-done.3, bf16[256,512]{1,0:T(8,128)(2,1)S(1)} %copy-done.2), custom_call_target="tpu_custom_call" | custom-call | tf_op jit(solution)/shard_map/pallas_call | solution.py:152
  86.2 0.0 copy-start.9
  86.2 0.0 collective-permute-done.2
  86.2 5.4 %all-to-all-done.1 = bf16[16,32,256]{2,1,0:T(8,128)(2,1)} async-done(((bf16[16,32,256]{2,1,0:T(8,128)(2,1)}), bf16[16,32,256]{2,1,0:T(8,128)(2,1)}, u32[]{:S(2)}, u32[]{:S(2)}) %all-to-all-start.1) | async-done | bytes 262176 | tf_op jit(solution)/shard_map/all_to_all | solution.py:177
  91.7 0.8 collective-permute-start.3
  92.5 9.7 %collective-permute-done.3 = bf16[512,256]{1,0:T(8,128)(2,1)S(1)} collective-permute-done((bf16[512,256]{1,0:T(8,128)(2,1)}, bf16[512,256]{1,0:T(8,128)(2,1)S(1)}, u32[]{:S(2)}, u32[]{:S(2)}) %collective-permute-start.3) | collective-permute-done | bytes 262176 | tf_op jit(solution)/shard_map/ppermute | solution.py:164
  102.3 0.0 collective-permute-start.4
  102.3 3.6 %all-to-all-start.2 = ((bf16[16,64,256]{2,1,0:T(8,128)(2,1)}), bf16[16,64,256]{2,1,0:T(8,128)(2,1)S(1)}, u32[]{:S(2)}, u32[]{:S(2)}) async-start(bf16[16,64,256]{2,1,0:T(8,128)(2,1)} %shard_map.96), calls=%async_computation.2 | async-start | bytes 1048576 | tf_op jit(solution)/shard_map/all_to_all | solution.py:177
  105.8 3.3 %collective-permute-start.6 = (bf16[512,256]{1,0:T(8,128)(2,1)S(1)}, bf16[512,256]{1,0:T(8,128)(2,1)S(1)}, u32[]{:S(2)}, u32[]{:S(2)}) collective-permute-start(bf16[512,256]{1,0:T(8,128)(2,1)S(1)} %collective-permute-done.3), channel_id=1, source_target_pairs={{0,3},{1,0},{2,1},{3,2},{4,7},{5,4},{6,5},{7,6},{8,11},{9,8},{10,9... | collective-permute-start | bytes 786440 | tf_op jit(solution)/shard_map/ppermute | solution.py:164
  109.2 0.0 collective-permute-start.5
  109.2 1.7 %fusion.3 = f32[256,1024]{1,0:T(8,128)S(1)} fusion(bf16[512,256]{1,0:T(8,128)(2,1)S(1)} %collective-permute-done.3, bf16[4,1024,512]{2,1,0:T(8,128)(2,1)} %bitcast.34, s32[]{:T(128)S(6)} %select_n.16), kind=kOutput, calls=%fused_computation.5 | convolution fusion | flops 268435456 | bytes 2359300 | tf_op jit(solution)/shard_map/dot_general | solution.py:235
  110.9 0.0 copy-start.1
  110.9 0.9 collective-permute-done.4
  111.8 1.7 %convolution_add_fusion.1 = f32[256,1024]{1,0:T(8,128)S(1)} fusion(f32[256,1024]{1,0:T(8,128)S(1)} %fusion.3, bf16[512,256]{1,0:T(8,128)(2,1)S(1)} %collective-permute-done.4, bf16[1024,512]{1,0:T(8,128)(2,1)} %collective-permute-done), kind=kOutput, calls=%fused_computation.2 | convolution fusion | flops 268697600 | bytes 3407872 | tf_op jit(solution)/shard_map/dot_general | solution.py:235
  113.5 7.2 %collective-permute-done.6 = bf16[512,256]{1,0:T(8,128)(2,1)S(1)} collective-permute-done((bf16[512,256]{1,0:T(8,128)(2,1)S(1)}, bf16[512,256]{1,0:T(8,128)(2,1)S(1)}, u32[]{:S(2)}, u32[]{:S(2)}) %collective-permute-start.6) | collective-permute-done | bytes 262176 | tf_op jit(solution)/shard_map/ppermute | solution.py:164
  120.7 0.0 copy-done.9
  120.7 0.5 fusion.7
  121.2 0.0 collective-permute-done.5
  121.2 2.5 %fusion.2 = bf16[1,256,1024]{2,1,0:T(8,128)(2,1)} fusion(f32[256,1024]{1,0:T(8,128)S(1)} %fusion.7, f32[256,1024]{1,0:T(8,128)S(1)} %convolution_add_fusion.1, bf16[512,256]{1,0:T(8,128)(2,1)S(1)} %collective-permute-done.5, bf16[1024,512]{1,0:T(8,128)(2,1)} %collective-permute-done.2), kind=kOutput, calls=%fused_computation.4 | convolution fusion | flops 269221888 | bytes 3932160 | tf_op jit(solution)/shard_map/dot_general | solution.py:235
  123.7 0.0 all-to-all-done.2.refs_0_
  123.7 0.0 copy-done.1
  123.7 1.0 shard_map.97
  (1 shorter events, 0.0 us)
Async XLA Ops:
  0.6 1.0 copy-start
  1.6 0.9 copy-start.4
  2.5 0.9 copy-start.5
  3.5 0.9 copy-start.6
  5.6 63.8 %copy-start.2 = (bf16[256,512]{1,0:T(8,128)(2,1)S(1)}, bf16[256,512]{1,0:T(8,128)(2,1)}, u32[]{:S(2)}) copy-start(bf16[256,512]{1,0:T(8,128)(2,1)} %constant.36.clone.refs_2_.refs_4_) | copy-start | bytes 786436
  5.6 63.8 %copy-start.3 = (bf16[256,512]{1,0:T(8,128)(2,1)S(1)}, bf16[256,512]{1,0:T(8,128)(2,1)}, u32[]{:S(2)}) copy-start(bf16[256,512]{1,0:T(8,128)(2,1)} %constant.35.clone.refs_1_.refs_3_) | copy-start | bytes 786436
  5.6 63.8 %all-to-all-start = ((bf16[16,96,256]{2,1,0:T(8,128)(2,1)}), bf16[16,96,256]{2,1,0:T(8,128)(2,1)S(1)}, u32[]{:S(2)}, u32[]{:S(2)}) async-start(bf16[16,96,256]{2,1,0:T(8,128)(2,1)} %shard_map.94), calls=%async_computation | async-start | bytes 1572864 | tf_op jit(solution)/shard_map/all_to_all | solution.py:177
  17.4 48.4 %collective-permute-start.1 = (bf16[1024,512]{1,0:T(8,128)(2,1)S(1)}, bf16[1024,512]{1,0:T(8,128)(2,1)S(1)}, u32[]{:S(2)}, u32[]{:S(2)}) collective-permute-start(bf16[1024,512]{1,0:T(8,128)(2,1)S(1)} %get-tuple-element.26), channel_id=1, source_target_pairs={{0,3},{1,0},{2,1},{3,2},{4,7},{5,4},{6,5},{7,6},{8,11},{9,8},{10,9... | collective-permute-start | bytes 3145736 | tf_op jit(solution)/shard_map/ppermute | solution.py:164
  20.4 48.9 %collective-permute-start = (bf16[1024,512]{1,0:T(8,128)(2,1)S(1)}, bf16[1024,512]{1,0:T(8,128)(2,1)}, u32[]{:S(2)}, u32[]{:S(2)}) collective-permute-start(bf16[1024,512]{1,0:T(8,128)(2,1)S(1)} %get-tuple-element.27), channel_id=1, source_target_pairs={{0,1},{1,2},{2,3},{3,0},{4,5},{5,6},{6,7},{7,4},{8,9},{9,10},{10,1... | collective-permute-start | bytes 3145736 | tf_op jit(solution)/shard_map/ppermute | solution.py:164
  20.4 65.8 %collective-permute-start.2 = (bf16[1024,512]{1,0:T(8,128)(2,1)}, bf16[1024,512]{1,0:T(8,128)(2,1)}, u32[]{:S(2)}, u32[]{:S(2)}) collective-permute-start(bf16[1024,512]{1,0:T(8,128)(2,1)} %get-tuple-element.25), channel_id=1, source_target_pairs={{0,2},{1,3},{2,0},{3,1},{4,6},{5,7},{6,4},{7,5},{8,10},{9,11},{10,... | collective-permute-start | bytes 3145736 | tf_op jit(solution)/shard_map/ppermute | solution.py:164
  65.8 1.0 copy-start.8
  72.7 0.7 copy-start.7
  73.4 18.2 %all-to-all-start.1 = ((bf16[16,32,256]{2,1,0:T(8,128)(2,1)}), bf16[16,32,256]{2,1,0:T(8,128)(2,1)}, u32[]{:S(2)}, u32[]{:S(2)}) async-start(bf16[16,32,256]{2,1,0:T(8,128)(2,1)} %bitcast.32), calls=%async_computation.1 | async-start | bytes 524288 | tf_op jit(solution)/shard_map/all_to_all | solution.py:177
  86.2 34.5 %copy-start.9 = (bf16[1024,512]{1,0:T(8,128)(2,1)S(1)}, bf16[1024,512]{1,0:T(8,128)(2,1)}, u32[]{:S(2)}) copy-start(bf16[1024,512]{1,0:T(8,128)(2,1)} %copy-done.8) | copy-start | bytes 3145732
  91.7 10.6 %collective-permute-start.3 = (bf16[512,256]{1,0:T(8,128)(2,1)}, bf16[512,256]{1,0:T(8,128)(2,1)S(1)}, u32[]{:S(2)}, u32[]{:S(2)}) collective-permute-start(bf16[512,256]{1,0:T(8,128)(2,1)} %bitcast.8), channel_id=1, source_target_pairs={{0,192},{64,0},{128,64},{192,128},{1,193},{65,1},{129,65},{193,129... | collective-permute-start | bytes 786440 | tf_op jit(solution)/shard_map/ppermute | solution.py:164
  102.3 9.5 %collective-permute-start.4 = (bf16[512,256]{1,0:T(8,128)(2,1)S(1)}, bf16[512,256]{1,0:T(8,128)(2,1)S(1)}, u32[]{:S(2)}, u32[]{:S(2)}) collective-permute-start(bf16[512,256]{1,0:T(8,128)(2,1)S(1)} %collective-permute-done.3), channel_id=1, source_target_pairs={{0,1},{1,2},{2,3},{3,0},{4,5},{5,6},{6,7},{7,4},{8,9},{9,10},{10,1... | collective-permute-start | bytes 786440 | tf_op jit(solution)/shard_map/ppermute | solution.py:164
  102.3 21.5 %all-to-all-start.2 = ((bf16[16,64,256]{2,1,0:T(8,128)(2,1)}), bf16[16,64,256]{2,1,0:T(8,128)(2,1)S(1)}, u32[]{:S(2)}, u32[]{:S(2)}) async-start(bf16[16,64,256]{2,1,0:T(8,128)(2,1)} %shard_map.96), calls=%async_computation.2 | async-start | bytes 1048576 | tf_op jit(solution)/shard_map/all_to_all | solution.py:177
  105.8 14.9 %collective-permute-start.6 = (bf16[512,256]{1,0:T(8,128)(2,1)S(1)}, bf16[512,256]{1,0:T(8,128)(2,1)S(1)}, u32[]{:S(2)}, u32[]{:S(2)}) collective-permute-start(bf16[512,256]{1,0:T(8,128)(2,1)S(1)} %collective-permute-done.3), channel_id=1, source_target_pairs={{0,3},{1,0},{2,1},{3,2},{4,7},{5,4},{6,5},{7,6},{8,11},{9,8},{10,9... | collective-permute-start | bytes 786440 | tf_op jit(solution)/shard_map/ppermute | solution.py:164
  109.2 12.1 %collective-permute-start.5 = (bf16[512,256]{1,0:T(8,128)(2,1)S(1)}, bf16[512,256]{1,0:T(8,128)(2,1)S(1)}, u32[]{:S(2)}, u32[]{:S(2)}) collective-permute-start(bf16[512,256]{1,0:T(8,128)(2,1)S(1)} %collective-permute-done.3), channel_id=1, source_target_pairs={{0,2},{1,3},{2,0},{3,1},{4,6},{5,7},{6,4},{7,5},{8,10},{9,11},{10,... | collective-permute-start | bytes 786440 | tf_op jit(solution)/shard_map/ppermute | solution.py:164
  110.9 12.9 %copy-start.1 = (bf16[1,256,512]{2,1,0:T(8,128)(2,1)S(1)}, bf16[1,256,512]{2,1,0:T(8,128)(2,1)}, u32[]{:S(2)}) copy-start(bf16[1,256,512]{2,1,0:T(8,128)(2,1)} %param.9) | copy-start | bytes 786436

commit v3 on v2

--- a/solution.py
+++ b/solution.py
@@ -96,16 +96,28 @@
     return part.reshape(part.shape[0] * chans, part.shape[2])
 
 
-def send_kernel(panels, signal_ref, gate_ref, grad_ref, filter_ref, out_ref):
+def send_kernel(
+    panels, signal_in, gate_in, grad_in, filter_in, out_ref, signal_ref, gate_ref, grad_ref, filter_ref, sems
+):
     chans = out_ref.shape[1] // 3
+    copies = []
+    for at, (source, target) in enumerate(
+        ((gate_in, gate_ref), (grad_in, grad_ref), (filter_in, filter_ref), (signal_in, signal_ref))
+    ):
+        copies.append(pltpu.make_async_copy(source, target, sems.at[at]))
+        copies[-1].start()
 
     def put(at, panel):
         parts = panel.T.reshape(panels, chans, panel.shape[0])
         out_ref[:, at * chans : (at + 1) * chans, :] = parts
 
+    copies[0].wait()
+    copies[1].wait()
     gated = gate_ref[...].astype(jnp.float32) * grad_ref[...].astype(jnp.float32)
     put(0, gated.astype(jnp.bfloat16))
+    copies[2].wait()
     put(1, filter_ref[...])
+    copies[3].wait()
     put(2, signal_ref[...])
 
 
@@ -144,16 +156,12 @@
     filter_out[...] = by_rows(parts_ref, 1, chans).T.astype(jnp.float32)
 
 
-def whole(count):
-    return [pl.BlockSpec(memory_space=pltpu.VMEM)] * count
-
-
-def call(kernel, panels, outs, scratch, *operands):
+def call(kernel, panels, outs, scratch, *operands, space=pltpu.VMEM):
     return pl.pallas_call(
         lambda *refs: kernel(panels, *refs),
         out_shape=outs,
-        in_specs=whole(len(operands)),
-        out_specs=whole(len(outs)),
+        in_specs=[pl.BlockSpec(memory_space=space)] * len(operands),
+        out_specs=[pl.BlockSpec(memory_space=pltpu.VMEM)] * len(outs),
         scratch_shapes=scratch,
         compiler_params=pltpu.CompilerParams(vmem_limit_bytes=40 * 1024 * 1024),
     )(*operands)
@@ -183,11 +191,12 @@
         send_kernel,
         panels,
         (shape(panels, 3 * chans, panel_len),),
-        [],
-        signal[0],
-        gate_value[0],
-        grad_out[0],
-        long_filter[0],
+        [pltpu.VMEM((panel_len, width), jnp.bfloat16)] * 4 + [pltpu.SemaphoreType.DMA((4,))],
+        *(
+            pltpu.with_memory_space_constraint(panel[0], pltpu.HBM)
+            for panel in (signal, gate_value, grad_out, long_filter)
+        ),
+        space=pltpu.HBM,
     )
     parts = swapped(sent)
 
@@ -201,14 +210,12 @@
 
     weights = [weight_for(0)] + [shifted(weight_for(by), "chan", by) for by in range(1, groups)]
 
-    parts, weights[1], weights[-1] = lax.optimization_barrier((parts, weights[1], weights[-1]))
-
     spec = shape(rows, 2 * panel_len, dtype=jnp.float32)
     held = pltpu.VMEM((rows, 2 * panel_len), jnp.float32)
     signal_grad, gated_spec, filter_full = call(
         signal_grad_kernel,
         panels,
-        (shape(rows, panel_len), spec, spec),
+        (pltpu.HBM((rows, panel_len), jnp.bfloat16), spec, spec),
         [held, held],
         parts,
         high,
@@ -226,9 +233,10 @@
         high,
         low,
     )
-    signal_grad, rest, weights[2] = lax.optimization_barrier((signal_grad, rest, weights[2]))
+    signal_grad, rest = lax.optimization_barrier((signal_grad, rest))
     received = shifted(signal_grad, "pipe", -1)
     rest = swapped(rest)
+    received, weights = lax.optimization_barrier((received, weights))
     total = 0.0
     for by in range(groups):
         held_by = received if by == 0 else shifted(received, "chan", by)

time: 126 us -> 97.3 us (0.77)
  waiting for transfers between devices: 69.1 us -> 42.6 us
  local copies, waits for them, and re-layouts: 8.53 us -> 4.28 us
  Pallas kernels: 11.3 us -> 13.2 us
    ppermute x7, waiting for transfers between devices: 63.6 us -> 25.3 us  [shifted(): lax.ppermute(x, axis, [(i, (i + by) % length) for i in range(length)])]
    all_to_all x3, waiting for transfers between devices: 5.44 us -> 17.4 us  [swapped(): return lax.all_to_all(parts, 'seq', 0, 0, tiled=True)]
    unnamed x20 -> x8, local copies, waits for them, and re-layouts: 5.47 us -> 0.02 us
    pallas_call x4, Pallas kernels: 11.3 us -> 13.2 us  [call(): pl.pallas_call(lambda *refs: kernel(panels, *refs), out_shape=outs, in_sp...]
    ppermute x7, starting transfers between devices: 9.38 us -> 7.67 us  [shifted(): lax.ppermute(x, axis, [(i, (i + by) % length) for i in range(length)])]
    all_to_all x3, starting transfers between devices: 19.3 us -> 20.7 us  [swapped(): return lax.all_to_all(parts, 'seq', 0, 0, tiled=True)]
  transfers between devices with their start and end apart: 10 -> 10, of which waited for: 6 -> 6; matrix products, arithmetic and copies ran while one was open for 8% -> 11% of each run, Pallas kernels for 7% -> 10%
where the time goes in v3:
time: 97.3 us; the launch traced here: 95.7 us
  waiting for transfers between devices  42.6 us (44%)
  starting transfers between devices  28.4 us (29%)
  Pallas kernels  13.2 us (14%)
  matrix products  6.42 us (7%)
  local copies, waits for them, and re-layouts  4.28 us (4%)
    ppermute x7, waiting for transfers between devices, shifted(): lax.ppermute(x, axis, [(i, (i + by) % length) for i in range(length)])  25.3 us
    all_to_all x3, starting transfers between devices, swapped(): return lax.all_to_all(parts, 'seq', 0, 0, tiled=True)  20.7 us
    all_to_all x3, waiting for transfers between devices, swapped(): return lax.all_to_all(parts, 'seq', 0, 0, tiled=True)  17.4 us
    pallas_call x4, Pallas kernels, call(): pl.pallas_call(lambda *refs: kernel(panels, *refs), out_shape=outs, in_sp...  13.2 us
    ppermute x7, starting transfers between devices, shifted(): lax.ppermute(x, axis, [(i, (i + by) % length) for i in range(length)])  7.67 us
    dot_general x4, matrix products, on_device(): lax.dot_general(held_by, weights[by], (((0,), (1,)), ((), ())), preferred...  6.42 us
    squeeze x1, local copies, waits for them, and re-layouts, weight_for(): lax.dynamic_index_in_dim(weight_parts, lax.rem(my_group + by, groups), 0,...  4.25 us
  transfers between devices with their start and end apart: 10, of which 6 were waited for; matrix products, arithmetic and copies ran while one was open for 11% of the time, Pallas kernels for 10%

profile of v3, /device:TPU:6, one launch (start us, length us, event | category | flops | bytes accessed | tf_op | source)
XLA Modules:
  0.0 95.7 jit_solution(16929992286264533130)
XLA Ops:
  0.6 2.4 %shard_map.94 = bf16[16,96,256]{2,1,0:T(8,128)(2,1)} custom-call(bf16[256,512]{1,0:T(8,128)(2,1)} %bitcast.30, bf16[256,512]{1,0:T(8,128)(2,1)} %bitcast.31, bf16[256,512]{1,0:T(8,128)(2,1)} %bitcast.27, bf16[256,512]{1,0:T(8,128)(2,1)} %bitcast.32), custom_call_target="tpu_custom_call" | custom-call | tf_op jit(solution)/shard_map/pallas_call | solution.py:160
  3.0 8.6 %all-to-all-start = ((bf16[16,96,256]{2,1,0:T(8,128)(2,1)}), bf16[16,96,256]{2,1,0:T(8,128)(2,1)S(1)}, u32[]{:S(2)}, u32[]{:S(2)}) async-start(bf16[16,96,256]{2,1,0:T(8,128)(2,1)} %shard_map.94), calls=%async_computation | async-start | bytes 1572864 | tf_op jit(solution)/shard_map/all_to_all | solution.py:185
  11.6 0.0 copy-start.1
  11.6 0.0 copy-start.2
  11.6 4.3 %dynamic-slice_bitcast_fusion = (bf16[1024,512]{1,0:T(8,128)(2,1)}, bf16[1024,512]{1,0:T(8,128)(2,1)}, bf16[1024,512]{1,0:T(8,128)(2,1)}, bf16[1024,512]{1,0:T(8,128)(2,1)}) fusion(bf16[4,1024,512]{2,1,0:T(8,128)(2,1)} %bitcast.29, s32[]{:T(128)S(6)} %select_n.16, s32[]{:T(128)S(6)} %select_n.15, s32[]{:T(128)S(6)} %select_n.14, s32[]{:T(128)S(6)} %select_n.13), kind=kLoop, calls=%fused_computation.5 | loop fusion | bytes 8388624 | tf_op jit(solution)/shard_map/jit(dynamic_index_in_dim)/squeeze | solution.py:207
  15.9 3.0 %collective-permute-start.3 = (bf16[1024,512]{1,0:T(8,128)(2,1)}, bf16[1024,512]{1,0:T(8,128)(2,1)}, u32[]{:S(2)}, u32[]{:S(2)}) collective-permute-start(bf16[1024,512]{1,0:T(8,128)(2,1)} %get-tuple-element.27), channel_id=1, source_target_pairs={{0,3},{1,0},{2,1},{3,2},{4,7},{5,4},{6,5},{7,6},{8,11},{9,8},{10,9... | collective-permute-start | bytes 3145736 | tf_op jit(solution)/shard_map/ppermute | solution.py:172
  18.9 0.6 collective-permute-start.2
  19.5 1.0 %collective-permute-start.1 = (bf16[1024,512]{1,0:T(8,128)(2,1)}, bf16[1024,512]{1,0:T(8,128)(2,1)}, u32[]{:S(2)}, u32[]{:S(2)}) collective-permute-start(bf16[1024,512]{1,0:T(8,128)(2,1)} %get-tuple-element.29), channel_id=1, source_target_pairs={{0,1},{1,2},{2,3},{3,0},{4,5},{5,6},{6,7},{7,4},{8,9},{9,10},{10,1... | collective-permute-start | bytes 3145736 | tf_op jit(solution)/shard_map/ppermute | solution.py:172
  20.5 11.8 %all-to-all-done.refs_0_ = bf16[16,96,256]{2,1,0:T(8,128)(2,1)S(1)} async-done(((bf16[16,96,256]{2,1,0:T(8,128)(2,1)}), bf16[16,96,256]{2,1,0:T(8,128)(2,1)S(1)}, u32[]{:S(2)}, u32[]{:S(2)}) %all-to-all-start) | async-done | bytes 786464 | tf_op jit(solution)/shard_map/all_to_all | solution.py:185
  32.3 0.0 copy-done.1
  32.3 0.0 copy-done.2
  32.3 4.1 %shard_map.95 = (bf16[512,256]{1,0:T(8,128)(2,1)}, f32[512,512]{1,0:T(8,128)S(1)}, f32[512,512]{1,0:T(8,128)S(1)}) custom-call(bf16[16,96,256]{2,1,0:T(8,128)(2,1)S(1)} %all-to-all-done.refs_0_, bf16[256,512]{1,0:T(8,128)(2,1)S(1)} %copy-done.2, bf16[256,512]{1,0:T(8,128)(2,1)S(1)} %copy-done.1), custom_call_target="tpu_custom_call" | custom-call | tf_op jit(solution)/shard_map/pallas_call | solution.py:160
  36.4 5.2 %all-to-all-start.1 = ((bf16[16,32,256]{2,1,0:T(8,128)(2,1)}), bf16[16,32,256]{2,1,0:T(8,128)(2,1)}, u32[]{:S(2)}, u32[]{:S(2)}) async-start(bf16[16,32,256]{2,1,0:T(8,128)(2,1)} %bitcast.33), calls=%async_computation.1 | async-start | bytes 524288 | tf_op jit(solution)/shard_map/all_to_all | solution.py:185
  41.6 5.8 %shard_map.96 = bf16[16,64,256]{2,1,0:T(8,128)(2,1)} custom-call(bf16[16,96,256]{2,1,0:T(8,128)(2,1)S(1)} %all-to-all-done.refs_0_, f32[512,512]{1,0:T(8,128)S(1)} %get-tuple-element.16.refs_1_, f32[512,512]{1,0:T(8,128)S(1)} %get-tuple-element.17.refs_2_, bf16[256,512]{1,0:T(8,128)(2,1)S(1)} %copy-done.2, bf16[256,512]{1,0:T(8,128)(2,1)S(1)} %copy-done.1), custom_call_target="tpu_custom_call" | custom-call | tf_op jit(solution)/shard_map/pallas_call | solution.py:160
  47.4 0.0 copy-start.3
  47.4 5.6 %all-to-all-done.1 = bf16[16,32,256]{2,1,0:T(8,128)(2,1)} async-done(((bf16[16,32,256]{2,1,0:T(8,128)(2,1)}), bf16[16,32,256]{2,1,0:T(8,128)(2,1)}, u32[]{:S(2)}, u32[]{:S(2)}) %all-to-all-start.1) | async-done | bytes 262176 | tf_op jit(solution)/shard_map/all_to_all | solution.py:185
  53.0 0.8 collective-permute-start
  53.8 10.9 %collective-permute-done.3 = bf16[1024,512]{1,0:T(8,128)(2,1)} collective-permute-done((bf16[1024,512]{1,0:T(8,128)(2,1)}, bf16[1024,512]{1,0:T(8,128)(2,1)}, u32[]{:S(2)}, u32[]{:S(2)}) %collective-permute-start.3) | collective-permute-done | bytes 1048608 | tf_op jit(solution)/shard_map/ppermute | solution.py:172
  64.7 0.0 collective-permute-done.2
  64.7 3.7 %collective-permute-done.1 = bf16[1024,512]{1,0:T(8,128)(2,1)} collective-permute-done((bf16[1024,512]{1,0:T(8,128)(2,1)}, bf16[1024,512]{1,0:T(8,128)(2,1)}, u32[]{:S(2)}, u32[]{:S(2)}) %collective-permute-start.1) | collective-permute-done | bytes 1048608 | tf_op jit(solution)/shard_map/ppermute | solution.py:172
  68.4 0.0 collective-permute-done
  68.4 0.6 collective-permute-start.6
  69.0 7.0 %all-to-all-start.2 = ((bf16[16,64,256]{2,1,0:T(8,128)(2,1)}), bf16[16,64,256]{2,1,0:T(8,128)(2,1)S(1)}, u32[]{:S(2)}, u32[]{:S(2)}) async-start(bf16[16,64,256]{2,1,0:T(8,128)(2,1)} %shard_map.96), calls=%async_computation.2 | async-start | bytes 1048576 | tf_op jit(solution)/shard_map/all_to_all | solution.py:185
  75.9 0.7 collective-permute-start.5
  76.6 0.9 collective-permute-start.4
  77.5 0.0 collective-permute-done.6
  77.5 1.7 %fusion.6 = f32[256,1024]{1,0:T(8,128)S(1)} fusion(bf16[512,256]{1,0:T(8,128)(2,1)S(1)} %collective-permute-done.6, bf16[1024,512]{1,0:T(8,128)(2,1)} %collective-permute-done.3), kind=kOutput, calls=%fused_computation.11 | convolution fusion | flops 268435456 | bytes 2359296 | tf_op jit(solution)/shard_map/dot_general | solution.py:243
  79.2 7.4 %collective-permute-done.5 = bf16[512,256]{1,0:T(8,128)(2,1)S(1)} collective-permute-done((bf16[512,256]{1,0:T(8,128)(2,1)S(1)}, bf16[512,256]{1,0:T(8,128)(2,1)S(1)}, u32[]{:S(2)}, u32[]{:S(2)}) %collective-permute-start.5) | collective-permute-done | bytes 262176 | tf_op jit(solution)/shard_map/ppermute | solution.py:172
  86.7 1.7 %fusion.5 = f32[256,1024]{1,0:T(8,128)S(1)} fusion(bf16[512,256]{1,0:T(8,128)(2,1)S(1)} %collective-permute-done.5, bf16[1024,512]{1,0:T(8,128)(2,1)} %collective-permute-done.2), kind=kOutput, calls=%fused_computation.10 | convolution fusion | flops 268435456 | bytes 2359296 | tf_op jit(solution)/shard_map/dot_general | solution.py:243
  88.4 0.0 copy-start
  88.4 3.3 %collective-permute-done.4 = bf16[512,256]{1,0:T(8,128)(2,1)S(1)} collective-permute-done((bf16[512,256]{1,0:T(8,128)(2,1)S(1)}, bf16[512,256]{1,0:T(8,128)(2,1)S(1)}, u32[]{:S(2)}, u32[]{:S(2)}) %collective-permute-start.4) | collective-permute-done | bytes 262176 | tf_op jit(solution)/shard_map/ppermute | solution.py:172
  91.7 1.7 %fusion.4 = f32[256,1024]{1,0:T(8,128)S(1)} fusion(bf16[512,256]{1,0:T(8,128)(2,1)S(1)} %collective-permute-done.4, bf16[1024,512]{1,0:T(8,128)(2,1)} %collective-permute-done.1), kind=kOutput, calls=%fused_computation.9 | convolution fusion | flops 268435456 | bytes 2359296 | tf_op jit(solution)/shard_map/dot_general | solution.py:243
  93.4 0.0 copy-done.3
  93.4 1.3 %fusion.3 = bf16[1,256,1024]{2,1,0:T(8,128)(2,1)} fusion(f32[256,1024]{1,0:T(8,128)S(1)} %fusion.6, f32[256,1024]{1,0:T(8,128)S(1)} %fusion.5, f32[256,1024]{1,0:T(8,128)S(1)} %fusion.4, bf16[512,256]{1,0:T(8,128)(2,1)S(1)} %collective-permute-done, bf16[1024,512]{1,0:T(8,128)(2,1)S(1)} %copy-done.3), kind=kOutput, calls=%fused_computation.4 | convolution fusion | flops 269484032 | bytes 4980736 | tf_op jit(solution)/shard_map/dot_general | solution.py:243
  94.7 0.0 all-to-all-done.2.refs_0_
  94.7 0.0 copy-done
  94.7 1.0 %shard_map.97 = (bf16[256,512]{1,0:T(8,128)(2,1)}, f32[256,512]{1,0:T(8,128)}) custom-call(bf16[16,64,256]{2,1,0:T(8,128)(2,1)S(1)} %all-to-all-done.2.refs_0_, bf16[256,512]{1,0:T(8,128)(2,1)S(1)} %bitcast.28), custom_call_target="tpu_custom_call" | custom-call | tf_op jit(solution)/shard_map/pallas_call | solution.py:160
Async XLA Ops:
  3.0 29.3 %all-to-all-start = ((bf16[16,96,256]{2,1,0:T(8,128)(2,1)}), bf16[16,96,256]{2,1,0:T(8,128)(2,1)S(1)}, u32[]{:S(2)}, u32[]{:S(2)}) async-start(bf16[16,96,256]{2,1,0:T(8,128)(2,1)} %shard_map.94), calls=%async_computation | async-start | bytes 1572864 | tf_op jit(solution)/shard_map/all_to_all | solution.py:185
  11.6 20.7 %copy-start.1 = (bf16[256,512]{1,0:T(8,128)(2,1)S(1)}, bf16[256,512]{1,0:T(8,128)(2,1)}, u32[]{:S(2)}) copy-start(bf16[256,512]{1,0:T(8,128)(2,1)} %constant.36.clone.refs_2_.refs_4_) | copy-start | bytes 786436
  11.6 20.7 %copy-start.2 = (bf16[256,512]{1,0:T(8,128)(2,1)S(1)}, bf16[256,512]{1,0:T(8,128)(2,1)}, u32[]{:S(2)}) copy-start(bf16[256,512]{1,0:T(8,128)(2,1)} %constant.35.clone.refs_1_.refs_3_) | copy-start | bytes 786436
  15.9 48.8 %collective-permute-start.3 = (bf16[1024,512]{1,0:T(8,128)(2,1)}, bf16[1024,512]{1,0:T(8,128)(2,1)}, u32[]{:S(2)}, u32[]{:S(2)}) collective-permute-start(bf16[1024,512]{1,0:T(8,128)(2,1)} %get-tuple-element.27), channel_id=1, source_target_pairs={{0,3},{1,0},{2,1},{3,2},{4,7},{5,4},{6,5},{7,6},{8,11},{9,8},{10,9... | collective-permute-start | bytes 3145736 | tf_op jit(solution)/shard_map/ppermute | solution.py:172
  18.9 45.7 %collective-permute-start.2 = (bf16[1024,512]{1,0:T(8,128)(2,1)}, bf16[1024,512]{1,0:T(8,128)(2,1)}, u32[]{:S(2)}, u32[]{:S(2)}) collective-permute-start(bf16[1024,512]{1,0:T(8,128)(2,1)} %get-tuple-element.28), channel_id=1, source_target_pairs={{0,2},{1,3},{2,0},{3,1},{4,6},{5,7},{6,4},{7,5},{8,10},{9,11},{10,... | collective-permute-start | bytes 3145736 | tf_op jit(solution)/shard_map/ppermute | solution.py:172
  19.5 48.8 %collective-permute-start.1 = (bf16[1024,512]{1,0:T(8,128)(2,1)}, bf16[1024,512]{1,0:T(8,128)(2,1)}, u32[]{:S(2)}, u32[]{:S(2)}) collective-permute-start(bf16[1024,512]{1,0:T(8,128)(2,1)} %get-tuple-element.29), channel_id=1, source_target_pairs={{0,1},{1,2},{2,3},{3,0},{4,5},{5,6},{6,7},{7,4},{8,9},{9,10},{10,1... | collective-permute-start | bytes 3145736 | tf_op jit(solution)/shard_map/ppermute | solution.py:172
  36.4 16.6 %all-to-all-start.1 = ((bf16[16,32,256]{2,1,0:T(8,128)(2,1)}), bf16[16,32,256]{2,1,0:T(8,128)(2,1)}, u32[]{:S(2)}, u32[]{:S(2)}) async-start(bf16[16,32,256]{2,1,0:T(8,128)(2,1)} %bitcast.33), calls=%async_computation.1 | async-start | bytes 524288 | tf_op jit(solution)/shard_map/all_to_all | solution.py:185
  47.4 46.0 %copy-start.3 = (bf16[1024,512]{1,0:T(8,128)(2,1)S(1)}, bf16[1024,512]{1,0:T(8,128)(2,1)}, u32[]{:S(2)}) copy-start(bf16[1024,512]{1,0:T(8,128)(2,1)} %get-tuple-element.23) | copy-start | bytes 3145732
  53.0 15.4 %collective-permute-start = (bf16[512,256]{1,0:T(8,128)(2,1)}, bf16[512,256]{1,0:T(8,128)(2,1)S(1)}, u32[]{:S(2)}, u32[]{:S(2)}) collective-permute-start(bf16[512,256]{1,0:T(8,128)(2,1)} %bitcast.5), channel_id=1, source_target_pairs={{0,192},{64,0},{128,64},{192,128},{1,193},{65,1},{129,65},{193,129... | collective-permute-start | bytes 786440 | tf_op jit(solution)/shard_map/ppermute | solution.py:172
  68.4 9.2 %collective-permute-start.6 = (bf16[512,256]{1,0:T(8,128)(2,1)S(1)}, bf16[512,256]{1,0:T(8,128)(2,1)S(1)}, u32[]{:S(2)}, u32[]{:S(2)}) collective-permute-start(bf16[512,256]{1,0:T(8,128)(2,1)S(1)} %collective-permute-done), channel_id=1, source_target_pairs={{0,3},{1,0},{2,1},{3,2},{4,7},{5,4},{6,5},{7,6},{8,11},{9,8},{10,9... | collective-permute-start | bytes 786440 | tf_op jit(solution)/shard_map/ppermute | solution.py:172
  69.0 25.7 %all-to-all-start.2 = ((bf16[16,64,256]{2,1,0:T(8,128)(2,1)}), bf16[16,64,256]{2,1,0:T(8,128)(2,1)S(1)}, u32[]{:S(2)}, u32[]{:S(2)}) async-start(bf16[16,64,256]{2,1,0:T(8,128)(2,1)} %shard_map.96), calls=%async_computation.2 | async-start | bytes 1048576 | tf_op jit(solution)/shard_map/all_to_all | solution.py:185
  75.9 10.8 %collective-permute-start.5 = (bf16[512,256]{1,0:T(8,128)(2,1)S(1)}, bf16[512,256]{1,0:T(8,128)(2,1)S(1)}, u32[]{:S(2)}, u32[]{:S(2)}) collective-permute-start(bf16[512,256]{1,0:T(8,128)(2,1)S(1)} %collective-permute-done), channel_id=1, source_target_pairs={{0,2},{1,3},{2,0},{3,1},{4,6},{5,7},{6,4},{7,5},{8,10},{9,11},{10,... | collective-permute-start | bytes 786440 | tf_op jit(solution)/shard_map/ppermute | solution.py:172
  76.6 15.0 %collective-permute-start.4 = (bf16[512,256]{1,0:T(8,128)(2,1)S(1)}, bf16[512,256]{1,0:T(8,128)(2,1)S(1)}, u32[]{:S(2)}, u32[]{:S(2)}) collective-permute-start(bf16[512,256]{1,0:T(8,128)(2,1)S(1)} %collective-permute-done), channel_id=1, source_target_pairs={{0,1},{1,2},{2,3},{3,0},{4,5},{5,6},{6,7},{7,4},{8,9},{9,10},{10,1... | collective-permute-start | bytes 786440 | tf_op jit(solution)/shard_map/ppermute | solution.py:172
  88.4 6.3 %copy-start = (bf16[1,256,512]{2,1,0:T(8,128)(2,1)S(1)}, bf16[1,256,512]{2,1,0:T(8,128)(2,1)}, u32[]{:S(2)}) copy-start(bf16[1,256,512]{2,1,0:T(8,128)(2,1)} %param.9) | copy-start | bytes 786436

commit v4 on v3

--- a/solution.py
+++ b/solution.py
@@ -121,19 +121,24 @@
     put(2, signal_ref[...])
 
 
+def filter_spectra(parts_ref, high_ref, low_ref, gated_spec, filter_full, plain):
+    panels, chans = parts_ref.shape[0], parts_ref.shape[1] // 3
+    gated_spec[...] = spectra(by_rows(parts_ref, 0, chans), high_ref, low_ref)
+    plain[...] = spectra(by_rows(parts_ref, 1, chans), high_ref, low_ref)
+    widen(plain, filter_full, chans, panels)
+
+
 def signal_grad_kernel(
     panels, parts_ref, high_ref, low_ref, grad_ref, gated_spec, filter_full, plain, sums
 ):
     chans = parts_ref.shape[1] // 3
-    gated_spec[...] = spectra(by_rows(parts_ref, 0, chans), high_ref, low_ref)
-    plain[...] = spectra(by_rows(parts_ref, 1, chans), high_ref, low_ref)
-    widen(plain, filter_full, chans, panels)
+    filter_spectra(parts_ref, high_ref, low_ref, gated_spec, filter_full, plain)
     pair_sums(sums, gated_spec, filter_full, chans, panels, False)
     grad_ref[...] = inverse(sums[...], high_ref, low_ref).astype(grad_ref.dtype)
 
 
 def rest_kernel(
-    panels, parts_ref, gated_spec, filter_full, high_ref, low_ref, out_ref, plain, full, sums
+    panels, parts_ref, high_ref, low_ref, out_ref, gated_spec, filter_full, plain, full, sums
 ):
     chans = parts_ref.shape[1] // 3
 
@@ -141,6 +146,7 @@
         grad = inverse(sums[...], high_ref, low_ref).astype(out_ref.dtype)
         out_ref[:, at * chans : (at + 1) * chans, :] = grad.reshape(panels, chans, grad.shape[1])
 
+    filter_spectra(parts_ref, high_ref, low_ref, gated_spec, filter_full, plain)
     plain[...] = spectra(by_rows(parts_ref, 2, chans), high_ref, low_ref)
     widen(plain, full, chans, panels)
     pair_sums(sums, plain, filter_full, chans, panels, True)
@@ -163,7 +169,7 @@
         in_specs=[pl.BlockSpec(memory_space=space)] * len(operands),
         out_specs=[pl.BlockSpec(memory_space=pltpu.VMEM)] * len(outs),
         scratch_shapes=scratch,
-        compiler_params=pltpu.CompilerParams(vmem_limit_bytes=40 * 1024 * 1024),
+        compiler_params=pltpu.CompilerParams(vmem_limit_bytes=16 * 1024 * 1024),
     )(*operands)
 
 
@@ -190,7 +196,7 @@
     (sent,) = call(
         send_kernel,
         panels,
-        (shape(panels, 3 * chans, panel_len),),
+        (pltpu.HBM((panels, 3 * chans, panel_len), jnp.bfloat16),),
         [pltpu.VMEM((panel_len, width), jnp.bfloat16)] * 4 + [pltpu.SemaphoreType.DMA((4,))],
         *(
             pltpu.with_memory_space_constraint(panel[0], pltpu.HBM)
@@ -200,50 +206,61 @@
     )
     parts = swapped(sent)
 
-    my_group = lax.axis_index("chan")
-    weight_parts = weight[0].reshape(groups, weight.shape[1] // groups, width)
-
-    def weight_for(by):
-        return lax.dynamic_index_in_dim(
-            weight_parts, lax.rem(my_group + by, groups), 0, False
-        )
-
-    weights = [weight_for(0)] + [shifted(weight_for(by), "chan", by) for by in range(1, groups)]
-
-    spec = shape(rows, 2 * panel_len, dtype=jnp.float32)
+    my_group, my_half = lax.axis_index("chan"), lax.rem(lax.axis_index("seq"), 2)
+    outputs = weight.shape[1] // groups
+    weight_parts = weight[0].reshape(groups * 2, outputs // 2, width)
+    pairs = [(i, i ^ 1) for i in range(panels)]
+
+    def fetch(source, by):
+        at = 2 * lax.rem(my_group + by, groups) + my_half
+        return shifted(lax.dynamic_index_in_dim(source, at, 0, False), "chan", by)
+
+    def pair_swap(part):
+        return lax.ppermute(part, "seq", pairs)
+
+    near = [fetch(weight_parts, by) for by in (1, groups - 1)]
+    parts, near = lax.optimization_barrier((parts, near))
+
     held = pltpu.VMEM((rows, 2 * panel_len), jnp.float32)
-    signal_grad, gated_spec, filter_full = call(
+    (signal_grad,) = call(
         signal_grad_kernel,
         panels,
-        (pltpu.HBM((rows, panel_len), jnp.bfloat16), spec, spec),
-        [held, held],
+        (pltpu.HBM((rows, panel_len), jnp.bfloat16),),
+        [held] * 4,
         parts,
         high,
         low,
     )
+    near, signal_grad = lax.optimization_barrier((near, signal_grad))
+    near_others = [pair_swap(part) for part in near]
+    weight_parts, _ = lax.optimization_barrier((weight_parts, near[0]))
+    far = fetch(weight_parts, 2)
     signal_grad = swapped(signal_grad.reshape(panels, chans, panel_len)).reshape(width, panel_len)
     (rest,) = call(
         rest_kernel,
         panels,
-        (shape(panels, 2 * chans, panel_len),),
-        [held, held, held],
+        (pltpu.HBM((panels, 2 * chans, panel_len), jnp.bfloat16),),
+        [held] * 5,
         parts,
-        gated_spec,
-        filter_full,
         high,
         low,
     )
-    signal_grad, rest = lax.optimization_barrier((signal_grad, rest))
+    signal_grad, rest, far, near_others = lax.optimization_barrier(
+        (signal_grad, rest, far, near_others)
+    )
     received = shifted(signal_grad, "pipe", -1)
+    far_other = pair_swap(far)
+    rest, far_other = lax.optimization_barrier((rest, far_other))
+    received, far_other = lax.optimization_barrier((received, far_other))
     rest = swapped(rest)
-    received, weights = lax.optimization_barrier((received, weights))
-    total = 0.0
-    for by in range(groups):
-        held_by = received if by == 0 else shifted(received, "chan", by)
-        total = total + lax.dot_general(
-            held_by, weights[by], (((0,), (1,)), ((), ())), preferred_element_type=jnp.float32
+    fetched = [near[0], far, near[1]]
+    others = [near_others[0], far_other, near_others[1]]
+
+    def project(block, block_weight):
+        return lax.dot_general(
+            block, block_weight, (((0,), (1,)), ((), ())), preferred_element_type=jnp.float32
         )
-    input_grad = total.astype(jnp.bfloat16)
+
     gate_grad, filter_grad = call(
         finish_kernel,
         panels,
@@ -252,6 +269,19 @@
         rest,
         grad_out[0],
     )
+    total = project(received, lax.dynamic_slice_in_dim(weight[0], my_group * outputs, outputs, 0))
+    for at, by in enumerate((1, 2, groups - 1)):
+        ordered = jnp.where(
+            my_half == 0,
+            jnp.concatenate([fetched[at], others[at]]),
+            jnp.concatenate([others[at], fetched[at]]),
+        )
+        block = shifted(received, "chan", by)
+        block, ordered, total = lax.optimization_barrier((block, ordered, total))
+        if at == 2:
+            block, gate_grad, filter_grad = lax.optimization_barrier((block, gate_grad, filter_grad))
+        total = total + project(block, ordered)
+    input_grad = total.astype(jnp.bfloat16)
     return gate_grad[None], filter_grad[None], input_grad[None]
 
 

time: 97.3 us -> 92.6 us (0.952)
  waiting for transfers between devices: 42.6 us -> 31.3 us
  other arithmetic: 0 us -> 6.25 us
  matrix products: 6.42 us -> 3.25 us
  starting transfers between devices: 28.4 us -> 30.8 us
    all_to_all x3, waiting for transfers between devices: 17.4 us -> 8.51 us  [swapped(): return lax.all_to_all(parts, 'seq', 0, 0, tiled=True)]
    select_n x0 -> x3, other arithmetic: none -> 4.96 us  [on_device(): jnp.where(my_half == 0, jnp.concatenate([fetched[at], others[at]]), jnp.c...]
    all_to_all x3, starting transfers between devices: 20.7 us -> 16.5 us  [swapped(): return lax.all_to_all(parts, 'seq', 0, 0, tiled=True)]
    ppermute x0 -> x3, starting transfers between devices: none -> 3.59 us  [pair_swap(): return lax.ppermute(part, 'seq', pairs)]
    dot_general x4, matrix products: 6.42 us -> 3.25 us  [project(): lax.dot_general(block, block_weight, (((0,), (1,)), ((), ())), preferred_...]
    ppermute x7, starting transfers between devices: 7.67 us -> 10.7 us  [shifted(): lax.ppermute(x, axis, [(i, (i + by) % length) for i in range(length)])]
    ppermute x7, waiting for transfers between devices: 25.3 us -> 22.8 us  [shifted(): lax.ppermute(x, axis, [(i, (i + by) % length) for i in range(length)])]
    unnamed x8 -> x14, local copies, waits for them, and re-layouts: 0.02 us -> 1.56 us
  transfers between devices with their start and end apart: 10 -> 13, of which waited for: 6 -> 5; matrix products, arithmetic and copies ran while one was open for 11% -> 12% of each run, Pallas kernels for 10% -> 7%
where the time goes in v4:
time: 92.6 us; the launch traced here: 90.8 us
  waiting for transfers between devices  31.3 us (34%)
  starting transfers between devices  30.8 us (33%)
  Pallas kernels  13.7 us (15%)
  other arithmetic  6.25 us (7%)
  local copies, waits for them, and re-layouts  4.7 us (5%)
  matrix products  3.25 us (4%)
    ppermute x7, waiting for transfers between devices, shifted(): lax.ppermute(x, axis, [(i, (i + by) % length) for i in range(length)])  22.8 us
    all_to_all x3, starting transfers between devices, swapped(): return lax.all_to_all(parts, 'seq', 0, 0, tiled=True)  16.5 us
    pallas_call x4, Pallas kernels, call(): pl.pallas_call(lambda *refs: kernel(panels, *refs), out_shape=outs, in_sp...  13.7 us
    ppermute x7, starting transfers between devices, shifted(): lax.ppermute(x, axis, [(i, (i + by) % length) for i in range(length)])  10.7 us
    all_to_all x3, waiting for transfers between devices, swapped(): return lax.all_to_all(parts, 'seq', 0, 0, tiled=True)  8.51 us
    select_n x3, other arithmetic, on_device(): jnp.where(my_half == 0, jnp.concatenate([fetched[at], others[at]]), jnp.c...  4.96 us
    ppermute x3, starting transfers between devices, pair_swap(): return lax.ppermute(part, 'seq', pairs)  3.59 us
    dot_general x4, matrix products, project(): lax.dot_general(block, block_weight, (((0,), (1,)), ((), ())), preferred_...  3.25 us
  transfers between devices with their start and end apart: 13, of which 5 were waited for; matrix products, arithmetic and copies ran while one was open for 12% of the time, Pallas kernels for 7%

profile of v4, /device:TPU:6, one launch (start us, length us, event | category | flops | bytes accessed | tf_op | source)
XLA Modules:
  0.0 90.8 jit_solution(10119517972644713227)
XLA Ops:
  0.6 2.3 %shard_map.94 = bf16[16,96,256]{2,1,0:T(8,128)(2,1)} custom-call(bf16[256,512]{1,0:T(8,128)(2,1)} %bitcast.32, bf16[256,512]{1,0:T(8,128)(2,1)} %bitcast.33, bf16[256,512]{1,0:T(8,128)(2,1)} %bitcast.27, bf16[256,512]{1,0:T(8,128)(2,1)} %bitcast.34), custom_call_target="tpu_custom_call" | custom-call | tf_op jit(solution)/shard_map/pallas_call | solution.py:166
  3.0 0.0 copy-start.1
  3.0 0.0 copy-start.2
  3.0 8.7 %all-to-all-start = ((bf16[16,96,256]{2,1,0:T(8,128)(2,1)}), bf16[16,96,256]{2,1,0:T(8,128)(2,1)S(1)}, u32[]{:S(2)}, u32[]{:S(2)}) async-start(bf16[16,96,256]{2,1,0:T(8,128)(2,1)} %shard_map.94), calls=%async_computation | async-start | bytes 1572864 | tf_op jit(solution)/shard_map/all_to_all | solution.py:191
  11.7 1.3 %dynamic-slice_bitcast_fusion.1 = (bf16[512,512]{1,0:T(8,128)(2,1)S(1)}, bf16[512,512]{1,0:T(8,128)(2,1)S(1)}) fusion(bf16[8,512,512]{2,1,0:T(8,128)(2,1)} %bitcast.29, s32[]{:T(128)S(6)} %select_n.30, s32[]{:T(128)S(6)} %select_n.29), kind=kLoop, calls=%fused_computation.9 | loop fusion | bytes 2097160 | tf_op jit(solution)/shard_map/jit(dynamic_index_in_dim)/squeeze | solution.py:216
  13.0 1.7 %collective-permute-start = (bf16[512,512]{1,0:T(8,128)(2,1)S(1)}, bf16[512,512]{1,0:T(8,128)(2,1)S(1)}, u32[]{:S(2)}, u32[]{:S(2)}) collective-permute-start(bf16[512,512]{1,0:T(8,128)(2,1)S(1)} %get-tuple-element.64), channel_id=1, source_target_pairs={{0,1},{1,2},{2,3},{3,0},{4,5},{5,6},{6,7},{7,4},{8,9},{9,10},{10,1... | collective-permute-start | bytes 1572872 | tf_op jit(solution)/shard_map/ppermute | solution.py:178
  14.7 1.7 %collective-permute-start.1 = (bf16[512,512]{1,0:T(8,128)(2,1)S(1)}, bf16[512,512]{1,0:T(8,128)(2,1)S(1)}, u32[]{:S(2)}, u32[]{:S(2)}) collective-permute-start(bf16[512,512]{1,0:T(8,128)(2,1)S(1)} %get-tuple-element.63), channel_id=1, source_target_pairs={{0,3},{1,0},{2,1},{3,2},{4,7},{5,4},{6,5},{7,6},{8,11},{9,8},{10,9... | collective-permute-start | bytes 1572872 | tf_op jit(solution)/shard_map/ppermute | solution.py:178
  16.3 12.2 %collective-permute-done = bf16[512,512]{1,0:T(8,128)(2,1)S(1)} collective-permute-done((bf16[512,512]{1,0:T(8,128)(2,1)S(1)}, bf16[512,512]{1,0:T(8,128)(2,1)S(1)}, u32[]{:S(2)}, u32[]{:S(2)}) %collective-permute-start) | collective-permute-done | bytes 524320 | tf_op jit(solution)/shard_map/ppermute | solution.py:178
  28.6 0.0 collective-permute-done.1
  28.6 3.8 %all-to-all-done.refs_0_ = bf16[16,96,256]{2,1,0:T(8,128)(2,1)S(1)} async-done(((bf16[16,96,256]{2,1,0:T(8,128)(2,1)}), bf16[16,96,256]{2,1,0:T(8,128)(2,1)S(1)}, u32[]{:S(2)}, u32[]{:S(2)}) %all-to-all-start) | async-done | bytes 786464 | tf_op jit(solution)/shard_map/all_to_all | solution.py:191
  32.4 4.1 %shard_map.95 = bf16[512,256]{1,0:T(8,128)(2,1)} custom-call(bf16[16,96,256]{2,1,0:T(8,128)(2,1)S(1)} %all-to-all-done.refs_0_, bf16[256,512]{1,0:T(8,128)(2,1)S(1)} %copy-done.1, bf16[256,512]{1,0:T(8,128)(2,1)S(1)} %copy-done.2), custom_call_target="tpu_custom_call" | custom-call | tf_op jit(solution)/shard_map/pallas_call | solution.py:166
  36.5 2.4 %collective-permute-start.3 = (bf16[512,512]{1,0:T(8,128)(2,1)S(1)}, bf16[512,512]{1,0:T(8,128)(2,1)S(1)}, u32[]{:S(2)}, u32[]{:S(2)}) collective-permute-start(bf16[512,512]{1,0:T(8,128)(2,1)S(1)} %collective-permute-done), channel_id=1, source_target_pairs={{0,4},{4,0},{8,12},{12,8},{16,20},{20,16},{24,28},{28,24},{32,36},... | collective-permute-start | bytes 1572872 | tf_op jit(solution)/shard_map/ppermute | solution.py:219
  38.8 1.9 %dynamic-slice_bitcast_fusion = bf16[512,512]{1,0:T(8,128)(2,1)} fusion(bf16[8,512,512]{2,1,0:T(8,128)(2,1)} %bitcast.30, s32[]{:T(128)S(6)} %select_n.31), kind=kLoop, calls=%fused_computation.8 | loop fusion | bytes 1048580 | tf_op jit(solution)/shard_map/jit(dynamic_index_in_dim)/squeeze | solution.py:216
  40.7 3.2 %collective-permute-start.2 = (bf16[512,512]{1,0:T(8,128)(2,1)}, bf16[512,512]{1,0:T(8,128)(2,1)}, u32[]{:S(2)}, u32[]{:S(2)}) collective-permute-start(bf16[512,512]{1,0:T(8,128)(2,1)} %dynamic-slice_bitcast_fusion), channel_id=1, source_target_pairs={{0,2},{1,3},{2,0},{3,1},{4,6},{5,7},{6,4},{7,5},{8,10},{9,11},{10,... | collective-permute-start | bytes 1572872 | tf_op jit(solution)/shard_map/ppermute | solution.py:178
  43.9 0.0 collective-permute-start.4
  43.9 4.2 %all-to-all-start.1 = ((bf16[16,32,256]{2,1,0:T(8,128)(2,1)}), bf16[16,32,256]{2,1,0:T(8,128)(2,1)}, u32[]{:S(2)}, u32[]{:S(2)}) async-start(bf16[16,32,256]{2,1,0:T(8,128)(2,1)} %bitcast.31), calls=%async_computation.1 | async-start | bytes 524288 | tf_op jit(solution)/shard_map/all_to_all | solution.py:191
  48.1 6.4 %shard_map.96 = bf16[16,64,256]{2,1,0:T(8,128)(2,1)} custom-call(bf16[16,96,256]{2,1,0:T(8,128)(2,1)S(1)} %all-to-all-done.refs_0_, bf16[256,512]{1,0:T(8,128)(2,1)S(1)} %copy-done.1, bf16[256,512]{1,0:T(8,128)(2,1)S(1)} %copy-done.2), custom_call_target="tpu_custom_call" | custom-call | tf_op jit(solution)/shard_map/pallas_call | solution.py:166
  54.5 4.7 %all-to-all-done.1 = bf16[16,32,256]{2,1,0:T(8,128)(2,1)} async-done(((bf16[16,32,256]{2,1,0:T(8,128)(2,1)}), bf16[16,32,256]{2,1,0:T(8,128)(2,1)}, u32[]{:S(2)}, u32[]{:S(2)}) %all-to-all-start.1) | async-done | bytes 262176 | tf_op jit(solution)/shard_map/all_to_all | solution.py:191
  59.2 0.0 collective-permute-done.2
  59.2 0.0 collective-permute-done.3
  59.2 0.0 collective-permute-done.4
  59.2 1.2 %collective-permute-start.6 = (bf16[512,512]{1,0:T(8,128)(2,1)}, bf16[512,512]{1,0:T(8,128)(2,1)S(1)}, u32[]{:S(2)}, u32[]{:S(2)}) collective-permute-start(bf16[512,512]{1,0:T(8,128)(2,1)} %collective-permute-done.2), channel_id=1, source_target_pairs={{0,4},{4,0},{8,12},{12,8},{16,20},{20,16},{24,28},{28,24},{32,36},... | collective-permute-start | bytes 1572872 | tf_op jit(solution)/shard_map/ppermute | solution.py:219
  60.4 0.8 collective-permute-start.5
  61.2 1.7 %maximum_select_fusion.2 = bf16[1024,512]{1,0:T(8,128)(2,1)S(1)} fusion(bf16[512,512]{1,0:T(8,128)(2,1)} %copy-done.4, bf16[512,512]{1,0:T(8,128)(2,1)S(1)} %collective-permute-done, pred[]{:T(512)S(6)} %eq.2), kind=kLoop, calls=%fused_computation.2 | loop fusion | flops 4718592 | bytes 2097153 | tf_op jit(solution)/shard_map/jit(_where)/select_n | solution.py:274
  62.9 0.0 collective-permute-done.6
  63.0 0.0 copy-start.5
  63.0 0.8 copy-done.5
  63.8 3.6 %all-to-all-start.2 = ((bf16[16,64,256]{2,1,0:T(8,128)(2,1)}), bf16[16,64,256]{2,1,0:T(8,128)(2,1)S(1)}, u32[]{:S(2)}, u32[]{:S(2)}) async-start(bf16[16,64,256]{2,1,0:T(8,128)(2,1)} %shard_map.96), calls=%async_computation.2 | async-start | bytes 1048576 | tf_op jit(solution)/shard_map/all_to_all | solution.py:191
  67.3 0.0 copy-start.6
  67.3 1.6 %maximum_select_fusion = bf16[1024,512]{1,0:T(8,128)(2,1)S(1)} fusion(bf16[512,512]{1,0:T(8,128)(2,1)} %copy-done.3, bf16[512,512]{1,0:T(8,128)(2,1)S(1)} %collective-permute-done.1, pred[]{:T(512)S(6)} %eq.2), kind=kLoop, calls=%fused_computation | loop fusion | flops 4718592 | bytes 2097153 | tf_op jit(solution)/shard_map/jit(_where)/select_n | solution.py:274
  69.0 2.0 %collective-permute-done.5 = bf16[512,256]{1,0:T(8,128)(2,1)} collective-permute-done((bf16[512,256]{1,0:T(8,128)(2,1)}, bf16[512,256]{1,0:T(8,128)(2,1)}, u32[]{:S(2)}, u32[]{:S(2)}) %collective-permute-start.5) | collective-permute-done | bytes 262176 | tf_op jit(solution)/shard_map/ppermute | solution.py:178
  71.0 0.7 collective-permute-start.9
  71.7 1.8 %collective-permute-start.8 = (bf16[512,256]{1,0:T(8,128)(2,1)}, bf16[512,256]{1,0:T(8,128)(2,1)S(1)}, u32[]{:S(2)}, u32[]{:S(2)}) collective-permute-start(bf16[512,256]{1,0:T(8,128)(2,1)} %collective-permute-done.5), channel_id=1, source_target_pairs={{0,2},{1,3},{2,0},{3,1},{4,6},{5,7},{6,4},{7,5},{8,10},{9,11},{10,... | collective-permute-start | bytes 786440 | tf_op jit(solution)/shard_map/ppermute | solution.py:178
  73.5 0.8 collective-permute-start.7
  74.4 1.6 %maximum_select_fusion.1 = bf16[1024,512]{1,0:T(8,128)(2,1)S(1)} fusion(bf16[512,512]{1,0:T(8,128)(2,1)S(1)} %copy-done.6, bf16[512,512]{1,0:T(8,128)(2,1)} %collective-permute-done.2, pred[]{:T(512)S(6)} %eq.2), kind=kLoop, calls=%fused_computation.1 | loop fusion | flops 4718592 | bytes 2097153 | tf_op jit(solution)/shard_map/jit(_where)/select_n | solution.py:274
  76.0 1.8 %fusion = f32[256,1024]{1,0:T(8,128)S(1)} fusion(bf16[512,256]{1,0:T(8,128)(2,1)} %collective-permute-done.5, bf16[1,4096,512]{2,1,0:T(8,128)(2,1)} %param.11, s32[]{:T(128)S(6)} %select_n.36), kind=kOutput, calls=%fused_computation.3 | convolution fusion | flops 268435456 | bytes 2359300 | tf_op jit(solution)/shard_map/dot_general | solution.py:260
  77.8 8.5 %collective-permute-done.9 = bf16[512,256]{1,0:T(8,128)(2,1)S(1)} collective-permute-done((bf16[512,256]{1,0:T(8,128)(2,1)}, bf16[512,256]{1,0:T(8,128)(2,1)S(1)}, u32[]{:S(2)}, u32[]{:S(2)}) %collective-permute-start.9) | collective-permute-done | bytes 262176 | tf_op jit(solution)/shard_map/ppermute | solution.py:178
  86.3 0.5 fusion.5
  86.8 0.2 add.50
  87.0 0.0 collective-permute-done.8
  87.0 0.5 fusion.6
  87.5 0.0 copy-start
  87.5 0.2 add.51
  87.6 0.0 collective-permute-done.7
  87.7 0.7 copy-done
  88.4 1.0 %shard_map.97 = (bf16[256,512]{1,0:T(8,128)(2,1)}, f32[256,512]{1,0:T(8,128)}) custom-call(bf16[16,64,256]{2,1,0:T(8,128)(2,1)S(1)} %all-to-all-done.2.refs_0_, bf16[256,512]{1,0:T(8,128)(2,1)S(1)} %bitcast.28), custom_call_target="tpu_custom_call" | custom-call | tf_op jit(solution)/shard_map/pallas_call | solution.py:166
  89.4 0.5 fusion.7
  89.9 0.9 %fusion.3 = bf16[1,256,1024]{2,1,0:T(8,128)(2,1)} fusion(f32[256,1024]{1,0:T(8,128)S(1)} %add.51, f32[256,1024]{1,0:T(8,128)S(1)} %fusion.7), kind=kLoop, calls=%fused_computation.7 | loop fusion | flops 524288 | bytes 2621440 | tf_op jit(solution)/shard_map/broadcast_in_dim | solution.py:285
  (8 shorter events, 0.0 us)
Async XLA Ops:
  3.0 29.4 %copy-start.1 = (bf16[256,512]{1,0:T(8,128)(2,1)S(1)}, bf16[256,512]{1,0:T(8,128)(2,1)}, u32[]{:S(2)}) copy-start(bf16[256,512]{1,0:T(8,128)(2,1)} %constant.44.clone.refs_1_) | copy-start | bytes 786436
  3.0 29.4 %copy-start.2 = (bf16[256,512]{1,0:T(8,128)(2,1)S(1)}, bf16[256,512]{1,0:T(8,128)(2,1)}, u32[]{:S(2)}) copy-start(bf16[256,512]{1,0:T(8,128)(2,1)} %constant.45.clone.refs_2_) | copy-start | bytes 786436
  3.0 29.4 %all-to-all-start = ((bf16[16,96,256]{2,1,0:T(8,128)(2,1)}), bf16[16,96,256]{2,1,0:T(8,128)(2,1)S(1)}, u32[]{:S(2)}, u32[]{:S(2)}) async-start(bf16[16,96,256]{2,1,0:T(8,128)(2,1)} %shard_map.94), calls=%async_computation | async-start | bytes 1572864 | tf_op jit(solution)/shard_map/all_to_all | solution.py:191
  13.0 15.6 %collective-permute-start = (bf16[512,512]{1,0:T(8,128)(2,1)S(1)}, bf16[512,512]{1,0:T(8,128)(2,1)S(1)}, u32[]{:S(2)}, u32[]{:S(2)}) collective-permute-start(bf16[512,512]{1,0:T(8,128)(2,1)S(1)} %get-tuple-element.64), channel_id=1, source_target_pairs={{0,1},{1,2},{2,3},{3,0},{4,5},{5,6},{6,7},{7,4},{8,9},{9,10},{10,1... | collective-permute-start | bytes 1572872 | tf_op jit(solution)/shard_map/ppermute | solution.py:178
  14.7 13.9 %collective-permute-start.1 = (bf16[512,512]{1,0:T(8,128)(2,1)S(1)}, bf16[512,512]{1,0:T(8,128)(2,1)S(1)}, u32[]{:S(2)}, u32[]{:S(2)}) collective-permute-start(bf16[512,512]{1,0:T(8,128)(2,1)S(1)} %get-tuple-element.63), channel_id=1, source_target_pairs={{0,3},{1,0},{2,1},{3,2},{4,7},{5,4},{6,5},{7,6},{8,11},{9,8},{10,9... | collective-permute-start | bytes 1572872 | tf_op jit(solution)/shard_map/ppermute | solution.py:178
  36.5 22.7 %collective-permute-start.3 = (bf16[512,512]{1,0:T(8,128)(2,1)S(1)}, bf16[512,512]{1,0:T(8,128)(2,1)S(1)}, u32[]{:S(2)}, u32[]{:S(2)}) collective-permute-start(bf16[512,512]{1,0:T(8,128)(2,1)S(1)} %collective-permute-done), channel_id=1, source_target_pairs={{0,4},{4,0},{8,12},{12,8},{16,20},{20,16},{24,28},{28,24},{32,36},... | collective-permute-start | bytes 1572872 | tf_op jit(solution)/shard_map/ppermute | solution.py:219
  40.7 18.5 %collective-permute-start.2 = (bf16[512,512]{1,0:T(8,128)(2,1)}, bf16[512,512]{1,0:T(8,128)(2,1)}, u32[]{:S(2)}, u32[]{:S(2)}) collective-permute-start(bf16[512,512]{1,0:T(8,128)(2,1)} %dynamic-slice_bitcast_fusion), channel_id=1, source_target_pairs={{0,2},{1,3},{2,0},{3,1},{4,6},{5,7},{6,4},{7,5},{8,10},{9,11},{10,... | collective-permute-start | bytes 1572872 | tf_op jit(solution)/shard_map/ppermute | solution.py:178
  43.9 15.3 %collective-permute-start.4 = (bf16[512,512]{1,0:T(8,128)(2,1)S(1)}, bf16[512,512]{1,0:T(8,128)(2,1)S(1)}, u32[]{:S(2)}, u32[]{:S(2)}) collective-permute-start(bf16[512,512]{1,0:T(8,128)(2,1)S(1)} %collective-permute-done.1), channel_id=1, source_target_pairs={{0,4},{4,0},{8,12},{12,8},{16,20},{20,16},{24,28},{28,24},{32,36},... | collective-permute-start | bytes 1572872 | tf_op jit(solution)/shard_map/ppermute | solution.py:219
  43.9 15.3 %all-to-all-start.1 = ((bf16[16,32,256]{2,1,0:T(8,128)(2,1)}), bf16[16,32,256]{2,1,0:T(8,128)(2,1)}, u32[]{:S(2)}, u32[]{:S(2)}) async-start(bf16[16,32,256]{2,1,0:T(8,128)(2,1)} %bitcast.31), calls=%async_computation.1 | async-start | bytes 524288 | tf_op jit(solution)/shard_map/all_to_all | solution.py:191
  59.2 1.2 %copy-start.4 = (bf16[512,512]{1,0:T(8,128)(2,1)}, bf16[512,512]{1,0:T(8,128)(2,1)S(1)}, u32[]{:S(2)}) copy-start(bf16[512,512]{1,0:T(8,128)(2,1)S(1)} %collective-permute-done.3) | copy-start | bytes 1572868
  59.2 1.2 %copy-start.3 = (bf16[512,512]{1,0:T(8,128)(2,1)}, bf16[512,512]{1,0:T(8,128)(2,1)S(1)}, u32[]{:S(2)}) copy-start(bf16[512,512]{1,0:T(8,128)(2,1)S(1)} %collective-permute-done.4) | copy-start | bytes 1572868
  59.2 3.7 %collective-permute-start.6 = (bf16[512,512]{1,0:T(8,128)(2,1)}, bf16[512,512]{1,0:T(8,128)(2,1)S(1)}, u32[]{:S(2)}, u32[]{:S(2)}) collective-permute-start(bf16[512,512]{1,0:T(8,128)(2,1)} %collective-permute-done.2), channel_id=1, source_target_pairs={{0,4},{4,0},{8,12},{12,8},{16,20},{20,16},{24,28},{28,24},{32,36},... | collective-permute-start | bytes 1572872 | tf_op jit(solution)/shard_map/ppermute | solution.py:219
  60.4 10.6 %collective-permute-start.5 = (bf16[512,256]{1,0:T(8,128)(2,1)}, bf16[512,256]{1,0:T(8,128)(2,1)}, u32[]{:S(2)}, u32[]{:S(2)}) collective-permute-start(bf16[512,256]{1,0:T(8,128)(2,1)} %bitcast.8), channel_id=1, source_target_pairs={{0,192},{64,0},{128,64},{192,128},{1,193},{65,1},{129,65},{193,129... | collective-permute-start | bytes 786440 | tf_op jit(solution)/shard_map/ppermute | solution.py:178
  63.0 0.8 copy-start.5
  63.8 23.9 %all-to-all-start.2 = ((bf16[16,64,256]{2,1,0:T(8,128)(2,1)}), bf16[16,64,256]{2,1,0:T(8,128)(2,1)S(1)}, u32[]{:S(2)}, u32[]{:S(2)}) async-start(bf16[16,64,256]{2,1,0:T(8,128)(2,1)} %shard_map.96), calls=%async_computation.2 | async-start | bytes 1048576 | tf_op jit(solution)/shard_map/all_to_all | solution.py:191
  67.3 7.0 %copy-start.6 = (bf16[512,512]{1,0:T(8,128)(2,1)S(1)}, bf16[512,512]{1,0:T(8,128)(2,1)}, u32[]{:S(2)}) copy-start(bf16[512,512]{1,0:T(8,128)(2,1)} %copy-done.5) | copy-start | bytes 1572868
  71.0 15.3 %collective-permute-start.9 = (bf16[512,256]{1,0:T(8,128)(2,1)}, bf16[512,256]{1,0:T(8,128)(2,1)S(1)}, u32[]{:S(2)}, u32[]{:S(2)}) collective-permute-start(bf16[512,256]{1,0:T(8,128)(2,1)} %collective-permute-done.5), channel_id=1, source_target_pairs={{0,1},{1,2},{2,3},{3,0},{4,5},{5,6},{6,7},{7,4},{8,9},{9,10},{10,1... | collective-permute-start | bytes 786440 | tf_op jit(solution)/shard_map/ppermute | solution.py:178
  71.7 15.3 %collective-permute-start.8 = (bf16[512,256]{1,0:T(8,128)(2,1)}, bf16[512,256]{1,0:T(8,128)(2,1)S(1)}, u32[]{:S(2)}, u32[]{:S(2)}) collective-permute-start(bf16[512,256]{1,0:T(8,128)(2,1)} %collective-permute-done.5), channel_id=1, source_target_pairs={{0,2},{1,3},{2,0},{3,1},{4,6},{5,7},{6,4},{7,5},{8,10},{9,11},{10,... | collective-permute-start | bytes 786440 | tf_op jit(solution)/shard_map/ppermute | solution.py:178
  73.5 14.1 %collective-permute-start.7 = (bf16[512,256]{1,0:T(8,128)(2,1)}, bf16[512,256]{1,0:T(8,128)(2,1)S(1)}, u32[]{:S(2)}, u32[]{:S(2)}) collective-permute-start(bf16[512,256]{1,0:T(8,128)(2,1)} %collective-permute-done.5), channel_id=1, source_target_pairs={{0,3},{1,0},{2,1},{3,2},{4,7},{5,4},{6,5},{7,6},{8,11},{9,8},{10,9... | collective-permute-start | bytes 786440 | tf_op jit(solution)/shard_map/ppermute | solution.py:178
  87.5 1.0 %copy-start = (bf16[1,256,512]{2,1,0:T(8,128)(2,1)S(1)}, bf16[1,256,512]{2,1,0:T(8,128)(2,1)}, u32[]{:S(2)}) copy-start(bf16[1,256,512]{2,1,0:T(8,128)(2,1)} %param.9) | copy-start | bytes 786436

commit v5 on v3

--- a/solution.py
+++ b/solution.py
@@ -133,7 +133,7 @@
 
 
 def rest_kernel(
-    panels, parts_ref, gated_spec, filter_full, high_ref, low_ref, out_ref, plain, full, sums
+    panels, parts_ref, high_ref, low_ref, out_ref, gated_spec, signal_spec, filter_spec, full, sums
 ):
     chans = parts_ref.shape[1] // 3
 
@@ -141,15 +141,28 @@
         grad = inverse(sums[...], high_ref, low_ref).astype(out_ref.dtype)
         out_ref[:, at * chans : (at + 1) * chans, :] = grad.reshape(panels, chans, grad.shape[1])
 
-    plain[...] = spectra(by_rows(parts_ref, 2, chans), high_ref, low_ref)
-    widen(plain, full, chans, panels)
-    pair_sums(sums, plain, filter_full, chans, panels, True)
+    for at, spec in enumerate((gated_spec, filter_spec, signal_spec)):
+        spec[...] = spectra(by_rows(parts_ref, at, chans), high_ref, low_ref)
+    widen(signal_spec, full, chans, panels)
+    pair_sums(sums, filter_spec, full, chans, panels, True)
     put(0)
     pair_sums(sums, gated_spec, full, chans, panels, False)
     put(1)
 
 
-def finish_kernel(panels, parts_ref, grad_ref, gate_out, filter_out):
+def weight_kernel(starts_ref, weight_ref, *refs):
+    outs, sems = refs[:-1], refs[-1]
+    copies = []
+    for at, out in enumerate(outs):
+        rows = out.shape[0]
+        start = pl.multiple_of(starts_ref[at], 256)
+        copies.append(pltpu.make_async_copy(weight_ref.at[pl.ds(start, rows)], out, sems.at[at]))
+        copies[-1].start()
+    for copy in copies:
+        copy.wait()
+
+
+def finish_kernel(panels, parts_ref, grad_ref, token_ref, gate_out, filter_out):
     chans = parts_ref.shape[1] // 2
     conv = by_rows(parts_ref, 0, chans).T.astype(jnp.float32)
     gate_out[...] = (grad_ref[...].astype(jnp.float32) * conv).astype(gate_out.dtype)
@@ -163,7 +176,7 @@
         in_specs=[pl.BlockSpec(memory_space=space)] * len(operands),
         out_specs=[pl.BlockSpec(memory_space=pltpu.VMEM)] * len(outs),
         scratch_shapes=scratch,
-        compiler_params=pltpu.CompilerParams(vmem_limit_bytes=40 * 1024 * 1024),
+        compiler_params=pltpu.CompilerParams(vmem_limit_bytes=16 * 1024 * 1024),
     )(*operands)
 
 
@@ -190,7 +203,7 @@
     (sent,) = call(
         send_kernel,
         panels,
-        (shape(panels, 3 * chans, panel_len),),
+        (pltpu.HBM((panels, 3 * chans, panel_len), jnp.bfloat16),),
         [pltpu.VMEM((panel_len, width), jnp.bfloat16)] * 4 + [pltpu.SemaphoreType.DMA((4,))],
         *(
             pltpu.with_memory_space_constraint(panel[0], pltpu.HBM)
@@ -201,22 +214,26 @@
     parts = swapped(sent)
 
     my_group = lax.axis_index("chan")
-    weight_parts = weight[0].reshape(groups, weight.shape[1] // groups, width)
-
-    def weight_for(by):
-        return lax.dynamic_index_in_dim(
-            weight_parts, lax.rem(my_group + by, groups), 0, False
-        )
-
-    weights = [weight_for(0)] + [shifted(weight_for(by), "chan", by) for by in range(1, groups)]
-
-    spec = shape(rows, 2 * panel_len, dtype=jnp.float32)
+    outputs = weight.shape[1] // groups
+    starts = [outputs * lax.rem(my_group + by, groups) for by in (1, 3, 2)]
+    weight_parts = pl.pallas_call(
+        weight_kernel,
+        out_shape=[pltpu.HBM((outputs, width), jnp.bfloat16)] * 3,
+        in_specs=[
+            pl.BlockSpec(memory_space=pltpu.SMEM),
+            pl.BlockSpec(memory_space=pltpu.HBM),
+        ],
+        out_specs=[pl.BlockSpec(memory_space=pltpu.HBM)] * 3,
+        scratch_shapes=[pltpu.SemaphoreType.DMA((3,))],
+    )(jnp.stack(starts), pltpu.with_memory_space_constraint(weight[0], pltpu.HBM))
+    weights = [shifted(part, "chan", by) for part, by in zip(weight_parts, (1, 3, 2))]
+
     held = pltpu.VMEM((rows, 2 * panel_len), jnp.float32)
-    signal_grad, gated_spec, filter_full = call(
+    (signal_grad,) = call(
         signal_grad_kernel,
         panels,
-        (pltpu.HBM((rows, panel_len), jnp.bfloat16), spec, spec),
-        [held, held],
+        (pltpu.HBM((rows, panel_len), jnp.bfloat16),),
+        [held] * 4,
         parts,
         high,
         low,
@@ -225,25 +242,24 @@
     (rest,) = call(
         rest_kernel,
         panels,
-        (shape(panels, 2 * chans, panel_len),),
-        [held, held, held],
+        (pltpu.HBM((panels, 2 * chans, panel_len), jnp.bfloat16),),
+        [held] * 5,
         parts,
-        gated_spec,
-        filter_full,
         high,
         low,
     )
     signal_grad, rest = lax.optimization_barrier((signal_grad, rest))
     received = shifted(signal_grad, "pipe", -1)
+    token = lax.ppermute(signal_grad[:16, :128], "seq", [(i, i ^ 1) for i in range(panels)])
+    rest, token = lax.optimization_barrier((rest, token))
     rest = swapped(rest)
     received, weights = lax.optimization_barrier((received, weights))
-    total = 0.0
-    for by in range(groups):
-        held_by = received if by == 0 else shifted(received, "chan", by)
-        total = total + lax.dot_general(
-            held_by, weights[by], (((0,), (1,)), ((), ())), preferred_element_type=jnp.float32
+
+    def project(block, block_weight):
+        return lax.dot_general(
+            block, block_weight, (((0,), (1,)), ((), ())), preferred_element_type=jnp.float32
         )
-    input_grad = total.astype(jnp.bfloat16)
+
     gate_grad, filter_grad = call(
         finish_kernel,
         panels,
@@ -251,7 +267,16 @@
         [],
         rest,
         grad_out[0],
-    )
+        token,
+    )
+    total = project(received, lax.dynamic_slice_in_dim(weight[0], my_group * outputs, outputs, 0))
+    for by, part in zip((1, 3, 2), weights):
+        block = shifted(received, "chan", by)
+        block, total = lax.optimization_barrier((block, total))
+        if by == 2:
+            block, gate_grad, filter_grad = lax.optimization_barrier((block, gate_grad, filter_grad))
+        total = total + project(block, part)
+    input_grad = total.astype(jnp.bfloat16)
     return gate_grad[None], filter_grad[None], input_grad[None]
 
 

time: 97.3 us -> 183 us (1.88)
  Pallas kernels: 13.2 us -> 111 us
  waiting for transfers between devices: 42.6 us -> 32.3 us
  local copies, waits for them, and re-layouts: 4.28 us -> 0.02 us
  other arithmetic: 0 us -> 1.94 us
    pallas_call x0 -> x1, Pallas kernels: none -> 97.1 us  [on_device(): pl.pallas_call(weight_kernel, out_shape=[pltpu.HBM((outputs, width), jnp....]
    all_to_all x3, waiting for transfers between devices: 17.4 us -> 4.88 us  [swapped(): return lax.all_to_all(parts, 'seq', 0, 0, tiled=True)]
    squeeze x1 -> x0, local copies, waits for them, and re-layouts: 4.25 us -> none  [weight_for(): lax.dynamic_index_in_dim(weight_parts, lax.rem(my_group + by, groups), 0,...]
    ppermute x7, starting transfers between devices: 7.67 us -> 9.54 us  [shifted(): lax.ppermute(x, axis, [(i, (i + by) % length) for i in range(length)])]
  transfers between devices with their start and end apart: 10 -> 11, of which waited for: 6 -> 5; matrix products, arithmetic and copies ran while one was open for 11% -> 3% of each run, Pallas kernels for 10% -> 59%
where the time goes in v5:
time: 183 us; the launch traced here: 182 us
  Pallas kernels  111 us (61%)
  waiting for transfers between devices  32.3 us (18%)
  starting transfers between devices  29.6 us (16%)
  matrix products  6.55 us (4%)
  other arithmetic  1.94 us (1%)
    pallas_call x1, Pallas kernels, on_device(): pl.pallas_call(weight_kernel, out_shape=[pltpu.HBM((outputs, width), jnp....  97.1 us
    ppermute x7, waiting for transfers between devices, shifted(): lax.ppermute(x, axis, [(i, (i + by) % length) for i in range(length)])  26.6 us
    all_to_all x3, starting transfers between devices, swapped(): return lax.all_to_all(parts, 'seq', 0, 0, tiled=True)  19.4 us
    pallas_call x4, Pallas kernels, call(): pl.pallas_call(lambda *refs: kernel(panels, *refs), out_shape=outs, in_sp...  13.8 us
    ppermute x7, starting transfers between devices, shifted(): lax.ppermute(x, axis, [(i, (i + by) % length) for i in range(length)])  9.54 us
    dot_general x4, matrix products, project(): lax.dot_general(block, block_weight, (((0,), (1,)), ((), ())), preferred_...  6.55 us
    all_to_all x3, waiting for transfers between devices, swapped(): return lax.all_to_all(parts, 'seq', 0, 0, tiled=True)  4.88 us
  transfers between devices with their start and end apart: 11, of which 5 were waited for; matrix products, arithmetic and copies ran while one was open for 3% of the time, Pallas kernels for 59%

profile of v5, /device:TPU:6, one launch (start us, length us, event | category | flops | bytes accessed | tf_op | source)
XLA Modules:
  0.0 182.0 jit_solution(5891811301133561566)
XLA Ops:
  0.6 0.0 copy-start.1
  0.6 0.0 copy-start.2
  0.7 2.4 %shard_map.94 = bf16[16,96,256]{2,1,0:T(8,128)(2,1)} custom-call(bf16[256,512]{1,0:T(8,128)(2,1)} %bitcast.30, bf16[256,512]{1,0:T(8,128)(2,1)} %bitcast.31, bf16[256,512]{1,0:T(8,128)(2,1)} %bitcast.24, bf16[256,512]{1,0:T(8,128)(2,1)} %bitcast.32), custom_call_target="tpu_custom_call" | custom-call | tf_op jit(solution)/shard_map/pallas_call | solution.py:173
  3.1 8.6 %all-to-all-start = ((bf16[16,96,256]{2,1,0:T(8,128)(2,1)}), bf16[16,96,256]{2,1,0:T(8,128)(2,1)S(1)}, u32[]{:S(2)}, u32[]{:S(2)}) async-start(bf16[16,96,256]{2,1,0:T(8,128)(2,1)} %shard_map.94), calls=%async_computation | async-start | bytes 1572864 | tf_op jit(solution)/shard_map/all_to_all | solution.py:198
  11.7 0.7 pad_add_fusion.starts_ref
  12.3 97.1 %shard_map.97 = (bf16[1024,512]{1,0:T(8,128)(2,1)}, bf16[1024,512]{1,0:T(8,128)(2,1)}, bf16[1024,512]{1,0:T(8,128)(2,1)}) custom-call(s32[3]{0:T(128)} %pad_add_fusion.starts_ref, bf16[4096,512]{1,0:T(8,128)(2,1)} %bitcast.26), custom_call_target="tpu_custom_call" | custom-call | tf_op jit(solution)/shard_map/pallas_call | solution.py:219
  109.4 1.7 collective-permute-start.1
  111.1 1.7 collective-permute-start.2
  112.7 2.0 %collective-permute-start.3 = (bf16[1024,512]{1,0:T(8,128)(2,1)}, bf16[1024,512]{1,0:T(8,128)(2,1)S(1)}, u32[]{:S(2)}, u32[]{:S(2)}) collective-permute-start(bf16[1024,512]{1,0:T(8,128)(2,1)} %get-tuple-element.28), channel_id=1, source_target_pairs={{0,2},{1,3},{2,0},{3,1},{4,6},{5,7},{6,4},{7,5},{8,10},{9,11},{10,... | collective-permute-start | bytes 3145736 | tf_op jit(solution)/shard_map/ppermute | solution.py:185
  114.7 0.0 all-to-all-done.refs_0_
  114.7 0.0 copy-done.1
  114.7 0.0 copy-done.2
  114.7 4.1 %shard_map.95 = bf16[512,256]{1,0:T(8,128)(2,1)} custom-call(bf16[16,96,256]{2,1,0:T(8,128)(2,1)S(1)} %all-to-all-done.refs_0_, bf16[256,512]{1,0:T(8,128)(2,1)S(1)} %copy-done.1, bf16[256,512]{1,0:T(8,128)(2,1)S(1)} %copy-done.2), custom_call_target="tpu_custom_call" | custom-call | tf_op jit(solution)/shard_map/pallas_call | solution.py:173
  118.8 7.2 %all-to-all-start.1 = ((bf16[16,32,256]{2,1,0:T(8,128)(2,1)}), bf16[16,32,256]{2,1,0:T(8,128)(2,1)S(1)}, u32[]{:S(2)}, u32[]{:S(2)}) async-start(bf16[16,32,256]{2,1,0:T(8,128)(2,1)} %bitcast.27), calls=%async_computation.1 | async-start | bytes 524288 | tf_op jit(solution)/shard_map/all_to_all | solution.py:198
  126.0 6.3 %shard_map.96 = bf16[16,64,256]{2,1,0:T(8,128)(2,1)} custom-call(bf16[16,96,256]{2,1,0:T(8,128)(2,1)S(1)} %all-to-all-done.refs_0_, bf16[256,512]{1,0:T(8,128)(2,1)S(1)} %copy-done.1, bf16[256,512]{1,0:T(8,128)(2,1)S(1)} %copy-done.2), custom_call_target="tpu_custom_call" | custom-call | tf_op jit(solution)/shard_map/pallas_call | solution.py:173
  132.3 4.9 %all-to-all-done.1 = bf16[16,32,256]{2,1,0:T(8,128)(2,1)S(1)} async-done(((bf16[16,32,256]{2,1,0:T(8,128)(2,1)}), bf16[16,32,256]{2,1,0:T(8,128)(2,1)S(1)}, u32[]{:S(2)}, u32[]{:S(2)}) %all-to-all-start.1) | async-done | bytes 262176 | tf_op jit(solution)/shard_map/all_to_all | solution.py:198
  137.2 0.8 collective-permute-start
  138.0 0.7 collective-permute-start.7
  138.7 0.8 collective-permute-done.7.refs_2_
  139.5 3.6 %all-to-all-start.2 = ((bf16[16,64,256]{2,1,0:T(8,128)(2,1)}), bf16[16,64,256]{2,1,0:T(8,128)(2,1)S(1)}, u32[]{:S(2)}, u32[]{:S(2)}) async-start(bf16[16,64,256]{2,1,0:T(8,128)(2,1)} %shard_map.96), calls=%async_computation.2 | async-start | bytes 1048576 | tf_op jit(solution)/shard_map/all_to_all | solution.py:198
  143.1 0.0 collective-permute-done.1
  143.1 15.3 %collective-permute-done.2 = bf16[1024,512]{1,0:T(8,128)(2,1)} collective-permute-done((bf16[1024,512]{1,0:T(8,128)(2,1)}, bf16[1024,512]{1,0:T(8,128)(2,1)}, u32[]{:S(2)}, u32[]{:S(2)}) %collective-permute-start.2) | collective-permute-done | bytes 1048608 | tf_op jit(solution)/shard_map/ppermute | solution.py:185
  158.4 1.7 collective-permute-done.3
  160.1 0.0 collective-permute-done
  160.1 1.1 collective-permute-start.6
  161.3 2.1 %collective-permute-start.5 = (bf16[512,256]{1,0:T(8,128)(2,1)S(1)}, bf16[512,256]{1,0:T(8,128)(2,1)S(1)}, u32[]{:S(2)}, u32[]{:S(2)}) collective-permute-start(bf16[512,256]{1,0:T(8,128)(2,1)S(1)} %collective-permute-done), channel_id=1, source_target_pairs={{0,3},{1,0},{2,1},{3,2},{4,7},{5,4},{6,5},{7,6},{8,11},{9,8},{10,9... | collective-permute-start | bytes 786440 | tf_op jit(solution)/shard_map/ppermute | solution.py:185
  163.4 0.2 collective-permute-start.4
  163.5 1.7 fusion
  165.3 9.6 %collective-permute-done.6 = bf16[512,256]{1,0:T(8,128)(2,1)S(1)} collective-permute-done((bf16[512,256]{1,0:T(8,128)(2,1)S(1)}, bf16[512,256]{1,0:T(8,128)(2,1)S(1)}, u32[]{:S(2)}, u32[]{:S(2)}) %collective-permute-start.6) | collective-permute-done | bytes 262176 | tf_op jit(solution)/shard_map/ppermute | solution.py:185
  174.8 1.7 fusion.5
  176.5 0.0 copy-start
  176.5 0.2 add.25
  176.7 0.0 collective-permute-done.5
  176.7 1.7 fusion.6
  178.4 0.2 add.26
  178.6 0.0 collective-permute-done.4
  178.6 0.0 all-to-all-done.2.refs_0_
  178.7 0.0 copy-done
  178.7 1.0 shard_map.98
  179.7 1.4 fusion.7
  181.1 0.9 fusion.3
  (1 shorter events, 0.0 us)
Async XLA Ops:
  0.6 114.1 %copy-start.1 = (bf16[256,512]{1,0:T(8,128)(2,1)S(1)}, bf16[256,512]{1,0:T(8,128)(2,1)}, u32[]{:S(2)}) copy-start(bf16[256,512]{1,0:T(8,128)(2,1)} %constant.28.clone.refs_1_) | copy-start | bytes 786436
  0.6 114.1 %copy-start.2 = (bf16[256,512]{1,0:T(8,128)(2,1)S(1)}, bf16[256,512]{1,0:T(8,128)(2,1)}, u32[]{:S(2)}) copy-start(bf16[256,512]{1,0:T(8,128)(2,1)} %constant.29.clone.refs_2_) | copy-start | bytes 786436
  3.1 111.6 %all-to-all-start = ((bf16[16,96,256]{2,1,0:T(8,128)(2,1)}), bf16[16,96,256]{2,1,0:T(8,128)(2,1)S(1)}, u32[]{:S(2)}, u32[]{:S(2)}) async-start(bf16[16,96,256]{2,1,0:T(8,128)(2,1)} %shard_map.94), calls=%async_computation | async-start | bytes 1572864 | tf_op jit(solution)/shard_map/all_to_all | solution.py:198
  109.4 33.7 %collective-permute-start.1 = (bf16[1024,512]{1,0:T(8,128)(2,1)}, bf16[1024,512]{1,0:T(8,128)(2,1)}, u32[]{:S(2)}, u32[]{:S(2)}) collective-permute-start(bf16[1024,512]{1,0:T(8,128)(2,1)} %get-tuple-element.26), channel_id=1, source_target_pairs={{0,1},{1,2},{2,3},{3,0},{4,5},{5,6},{6,7},{7,4},{8,9},{9,10},{10,1... | collective-permute-start | bytes 3145736 | tf_op jit(solution)/shard_map/ppermute | solution.py:185
  111.1 47.3 %collective-permute-start.2 = (bf16[1024,512]{1,0:T(8,128)(2,1)}, bf16[1024,512]{1,0:T(8,128)(2,1)}, u32[]{:S(2)}, u32[]{:S(2)}) collective-permute-start(bf16[1024,512]{1,0:T(8,128)(2,1)} %get-tuple-element.27), channel_id=1, source_target_pairs={{0,3},{1,0},{2,1},{3,2},{4,7},{5,4},{6,5},{7,6},{8,11},{9,8},{10,9... | collective-permute-start | bytes 3145736 | tf_op jit(solution)/shard_map/ppermute | solution.py:185
  112.7 47.4 %collective-permute-start.3 = (bf16[1024,512]{1,0:T(8,128)(2,1)}, bf16[1024,512]{1,0:T(8,128)(2,1)S(1)}, u32[]{:S(2)}, u32[]{:S(2)}) collective-permute-start(bf16[1024,512]{1,0:T(8,128)(2,1)} %get-tuple-element.28), channel_id=1, source_target_pairs={{0,2},{1,3},{2,0},{3,1},{4,6},{5,7},{6,4},{7,5},{8,10},{9,11},{10,... | collective-permute-start | bytes 3145736 | tf_op jit(solution)/shard_map/ppermute | solution.py:185
  118.8 18.4 %all-to-all-start.1 = ((bf16[16,32,256]{2,1,0:T(8,128)(2,1)}), bf16[16,32,256]{2,1,0:T(8,128)(2,1)S(1)}, u32[]{:S(2)}, u32[]{:S(2)}) async-start(bf16[16,32,256]{2,1,0:T(8,128)(2,1)} %bitcast.27), calls=%async_computation.1 | async-start | bytes 524288 | tf_op jit(solution)/shard_map/all_to_all | solution.py:198
  137.2 22.9 %collective-permute-start = (bf16[512,256]{1,0:T(8,128)(2,1)S(1)}, bf16[512,256]{1,0:T(8,128)(2,1)S(1)}, u32[]{:S(2)}, u32[]{:S(2)}) collective-permute-start(bf16[512,256]{1,0:T(8,128)(2,1)S(1)} %bitcast.28), channel_id=1, source_target_pairs={{0,192},{64,0},{128,64},{192,128},{1,193},{65,1},{129,65},{193,129... | collective-permute-start | bytes 786440 | tf_op jit(solution)/shard_map/ppermute | solution.py:185
  138.0 1.5 collective-permute-start.7
  139.5 39.1 %all-to-all-start.2 = ((bf16[16,64,256]{2,1,0:T(8,128)(2,1)}), bf16[16,64,256]{2,1,0:T(8,128)(2,1)S(1)}, u32[]{:S(2)}, u32[]{:S(2)}) async-start(bf16[16,64,256]{2,1,0:T(8,128)(2,1)} %shard_map.96), calls=%async_computation.2 | async-start | bytes 1048576 | tf_op jit(solution)/shard_map/all_to_all | solution.py:198
  160.1 14.7 %collective-permute-start.6 = (bf16[512,256]{1,0:T(8,128)(2,1)S(1)}, bf16[512,256]{1,0:T(8,128)(2,1)S(1)}, u32[]{:S(2)}, u32[]{:S(2)}) collective-permute-start(bf16[512,256]{1,0:T(8,128)(2,1)S(1)} %collective-permute-done), channel_id=1, source_target_pairs={{0,1},{1,2},{2,3},{3,0},{4,5},{5,6},{6,7},{7,4},{8,9},{9,10},{10,1... | collective-permute-start | bytes 786440 | tf_op jit(solution)/shard_map/ppermute | solution.py:185
  161.3 15.4 %collective-permute-start.5 = (bf16[512,256]{1,0:T(8,128)(2,1)S(1)}, bf16[512,256]{1,0:T(8,128)(2,1)S(1)}, u32[]{:S(2)}, u32[]{:S(2)}) collective-permute-start(bf16[512,256]{1,0:T(8,128)(2,1)S(1)} %collective-permute-done), channel_id=1, source_target_pairs={{0,3},{1,0},{2,1},{3,2},{4,7},{5,4},{6,5},{7,6},{8,11},{9,8},{10,9... | collective-permute-start | bytes 786440 | tf_op jit(solution)/shard_map/ppermute | solution.py:185
  163.4 15.3 %collective-permute-start.4 = (bf16[512,256]{1,0:T(8,128)(2,1)S(1)}, bf16[512,256]{1,0:T(8,128)(2,1)}, u32[]{:S(2)}, u32[]{:S(2)}) collective-permute-start(bf16[512,256]{1,0:T(8,128)(2,1)S(1)} %collective-permute-done), channel_id=1, source_target_pairs={{0,2},{1,3},{2,0},{3,1},{4,6},{5,7},{6,4},{7,5},{8,10},{9,11},{10,... | collective-permute-start | bytes 786440 | tf_op jit(solution)/shard_map/ppermute | solution.py:185
  176.5 2.1 %copy-start = (bf16[1,256,512]{2,1,0:T(8,128)(2,1)S(1)}, bf16[1,256,512]{2,1,0:T(8,128)(2,1)}, u32[]{:S(2)}) copy-start(bf16[1,256,512]{2,1,0:T(8,128)(2,1)} %param.9) | copy-start | bytes 786436

commit v6 on v5

--- a/solution.py
+++ b/solution.py
@@ -151,15 +151,22 @@
 
 
 def weight_kernel(starts_ref, weight_ref, *refs):
-    outs, sems = refs[:-1], refs[-1]
-    copies = []
-    for at, out in enumerate(outs):
-        rows = out.shape[0]
+    count = (len(refs) - 1) // 2
+    outs, helds, sems = refs[:count], refs[count:-1], refs[-1]
+    loads, stores = [], []
+    for at in range(count):
+        rows = outs[at].shape[0]
         start = pl.multiple_of(starts_ref[at], 256)
-        copies.append(pltpu.make_async_copy(weight_ref.at[pl.ds(start, rows)], out, sems.at[at]))
-        copies[-1].start()
-    for copy in copies:
-        copy.wait()
+        loads.append(
+            pltpu.make_async_copy(weight_ref.at[pl.ds(start, rows)], helds[at], sems.at[0, at])
+        )
+        stores.append(pltpu.make_async_copy(helds[at], outs[at], sems.at[1, at]))
+        loads[at].start()
+    for at in range(count):
+        loads[at].wait()
+        stores[at].start()
+    for store in stores:
+        store.wait()
 
 
 def finish_kernel(panels, parts_ref, grad_ref, token_ref, gate_out, filter_out):
@@ -224,7 +231,9 @@
             pl.BlockSpec(memory_space=pltpu.HBM),
         ],
         out_specs=[pl.BlockSpec(memory_space=pltpu.HBM)] * 3,
-        scratch_shapes=[pltpu.SemaphoreType.DMA((3,))],
+        scratch_shapes=[pltpu.VMEM((outputs, width), jnp.bfloat16)] * 3
+        + [pltpu.SemaphoreType.DMA((2, 3))],
+        compiler_params=pltpu.CompilerParams(vmem_limit_bytes=16 * 1024 * 1024),
     )(jnp.stack(starts), pltpu.with_memory_space_constraint(weight[0], pltpu.HBM))
     weights = [shifted(part, "chan", by) for part, by in zip(weight_parts, (1, 3, 2))]
 

time: 183 us -> 88.4 us (0.48)
  Pallas kernels: 111 us -> 17.3 us
  starting transfers between devices: 29.6 us -> 27.3 us
  waiting for transfers between devices: 32.3 us -> 34.5 us
    pallas_call x1, Pallas kernels: 97.1 us -> 3.5 us  [on_device(): pl.pallas_call(weight_kernel, out_shape=[pltpu.HBM((outputs, width), jnp....]
    all_to_all x3, waiting for transfers between devices: 4.88 us -> 16.9 us  [swapped(): return lax.all_to_all(parts, 'seq', 0, 0, tiled=True)]
    ppermute x7, waiting for transfers between devices: 26.6 us -> 16.8 us  [shifted(): lax.ppermute(x, axis, [(i, (i + by) % length) for i in range(length)])]
    all_to_all x3, starting transfers between devices: 19.4 us -> 17.3 us  [swapped(): return lax.all_to_all(parts, 'seq', 0, 0, tiled=True)]
  transfers between devices with their start and end apart: 11 -> 11, of which waited for: 5 -> 6; matrix products, arithmetic and copies ran while one was open for 3% -> 6% of each run, Pallas kernels for 59% -> 16%
where the time goes in v6:
time: 88.4 us; the launch traced here: 87.9 us
  waiting for transfers between devices  34.5 us (39%)
  starting transfers between devices  27.3 us (31%)
  Pallas kernels  17.3 us (20%)
  matrix products  6.54 us (7%)
  other arithmetic  1.36 us (2%)
    all_to_all x3, starting transfers between devices, swapped(): return lax.all_to_all(parts, 'seq', 0, 0, tiled=True)  17.3 us
    all_to_all x3, waiting for transfers between devices, swapped(): return lax.all_to_all(parts, 'seq', 0, 0, tiled=True)  16.9 us
    ppermute x7, waiting for transfers between devices, shifted(): lax.ppermute(x, axis, [(i, (i + by) % length) for i in range(length)])  16.8 us
    pallas_call x4, Pallas kernels, call(): pl.pallas_call(lambda *refs: kernel(panels, *refs), out_shape=outs, in_sp...  13.8 us
    ppermute x7, starting transfers between devices, shifted(): lax.ppermute(x, axis, [(i, (i + by) % length) for i in range(length)])  9.54 us
    dot_general x4, matrix products, project(): lax.dot_general(block, block_weight, (((0,), (1,)), ((), ())), preferred_...  6.54 us
    pallas_call x1, Pallas kernels, on_device(): pl.pallas_call(weight_kernel, out_shape=[pltpu.HBM((outputs, width), jnp....  3.5 us
  transfers between devices with their start and end apart: 11, of which 6 were waited for; matrix products, arithmetic and copies ran while one was open for 6% of the time, Pallas kernels for 16%

profile of v6, /device:TPU:6, one launch (start us, length us, event | category | flops | bytes accessed | tf_op | source)
XLA Modules:
  0.0 87.9 jit_solution(9539874530414845185)
XLA Ops:
  0.6 0.0 copy-start.1
  0.6 0.0 copy-start.2
  0.7 2.4 %shard_map.94 = bf16[16,96,256]{2,1,0:T(8,128)(2,1)} custom-call(bf16[256,512]{1,0:T(8,128)(2,1)} %bitcast.30, bf16[256,512]{1,0:T(8,128)(2,1)} %bitcast.31, bf16[256,512]{1,0:T(8,128)(2,1)} %bitcast.24, bf16[256,512]{1,0:T(8,128)(2,1)} %bitcast.32), custom_call_target="tpu_custom_call" | custom-call | tf_op jit(solution)/shard_map/pallas_call | solution.py:180
  3.1 8.6 %all-to-all-start = ((bf16[16,96,256]{2,1,0:T(8,128)(2,1)}), bf16[16,96,256]{2,1,0:T(8,128)(2,1)S(1)}, u32[]{:S(2)}, u32[]{:S(2)}) async-start(bf16[16,96,256]{2,1,0:T(8,128)(2,1)} %shard_map.94), calls=%async_computation | async-start | bytes 1572864 | tf_op jit(solution)/shard_map/all_to_all | solution.py:205
  11.7 0.1 pad_add_fusion.starts_ref
  11.8 3.5 %shard_map.97 = (bf16[1024,512]{1,0:T(8,128)(2,1)}, bf16[1024,512]{1,0:T(8,128)(2,1)}, bf16[1024,512]{1,0:T(8,128)(2,1)}) custom-call(s32[3]{0:T(128)S(1)} %pad_add_fusion.starts_ref, bf16[4096,512]{1,0:T(8,128)(2,1)} %bitcast.26), custom_call_target="tpu_custom_call" | custom-call | tf_op jit(solution)/shard_map/pallas_call | solution.py:226
  15.3 1.7 %collective-permute-start.1 = (bf16[1024,512]{1,0:T(8,128)(2,1)}, bf16[1024,512]{1,0:T(8,128)(2,1)}, u32[]{:S(2)}, u32[]{:S(2)}) collective-permute-start(bf16[1024,512]{1,0:T(8,128)(2,1)} %get-tuple-element.26), channel_id=1, source_target_pairs={{0,1},{1,2},{2,3},{3,0},{4,5},{5,6},{6,7},{7,4},{8,9},{9,10},{10,1... | collective-permute-start | bytes 3145736 | tf_op jit(solution)/shard_map/ppermute | solution.py:192
  16.9 1.7 %collective-permute-start.2 = (bf16[1024,512]{1,0:T(8,128)(2,1)}, bf16[1024,512]{1,0:T(8,128)(2,1)}, u32[]{:S(2)}, u32[]{:S(2)}) collective-permute-start(bf16[1024,512]{1,0:T(8,128)(2,1)} %get-tuple-element.27), channel_id=1, source_target_pairs={{0,3},{1,0},{2,1},{3,2},{4,7},{5,4},{6,5},{7,6},{8,11},{9,8},{10,9... | collective-permute-start | bytes 3145736 | tf_op jit(solution)/shard_map/ppermute | solution.py:192
  18.6 2.0 %collective-permute-start.3 = (bf16[1024,512]{1,0:T(8,128)(2,1)}, bf16[1024,512]{1,0:T(8,128)(2,1)S(1)}, u32[]{:S(2)}, u32[]{:S(2)}) collective-permute-start(bf16[1024,512]{1,0:T(8,128)(2,1)} %get-tuple-element.28), channel_id=1, source_target_pairs={{0,2},{1,3},{2,0},{3,1},{4,6},{5,7},{6,4},{7,5},{8,10},{9,11},{10,... | collective-permute-start | bytes 3145736 | tf_op jit(solution)/shard_map/ppermute | solution.py:192
  20.6 11.8 %all-to-all-done.refs_0_ = bf16[16,96,256]{2,1,0:T(8,128)(2,1)S(1)} async-done(((bf16[16,96,256]{2,1,0:T(8,128)(2,1)}), bf16[16,96,256]{2,1,0:T(8,128)(2,1)S(1)}, u32[]{:S(2)}, u32[]{:S(2)}) %all-to-all-start) | async-done | bytes 786464 | tf_op jit(solution)/shard_map/all_to_all | solution.py:205
  32.4 0.0 copy-done.1
  32.4 0.0 copy-done.2
  32.4 4.1 %shard_map.95 = bf16[512,256]{1,0:T(8,128)(2,1)} custom-call(bf16[16,96,256]{2,1,0:T(8,128)(2,1)S(1)} %all-to-all-done.refs_0_, bf16[256,512]{1,0:T(8,128)(2,1)S(1)} %copy-done.1, bf16[256,512]{1,0:T(8,128)(2,1)S(1)} %copy-done.2), custom_call_target="tpu_custom_call" | custom-call | tf_op jit(solution)/shard_map/pallas_call | solution.py:180
  36.4 5.1 %all-to-all-start.1 = ((bf16[16,32,256]{2,1,0:T(8,128)(2,1)}), bf16[16,32,256]{2,1,0:T(8,128)(2,1)S(1)}, u32[]{:S(2)}, u32[]{:S(2)}) async-start(bf16[16,32,256]{2,1,0:T(8,128)(2,1)} %bitcast.27), calls=%async_computation.1 | async-start | bytes 524288 | tf_op jit(solution)/shard_map/all_to_all | solution.py:205
  41.6 6.3 %shard_map.96 = bf16[16,64,256]{2,1,0:T(8,128)(2,1)} custom-call(bf16[16,96,256]{2,1,0:T(8,128)(2,1)S(1)} %all-to-all-done.refs_0_, bf16[256,512]{1,0:T(8,128)(2,1)S(1)} %copy-done.1, bf16[256,512]{1,0:T(8,128)(2,1)S(1)} %copy-done.2), custom_call_target="tpu_custom_call" | custom-call | tf_op jit(solution)/shard_map/pallas_call | solution.py:180
  47.9 5.1 %all-to-all-done.1 = bf16[16,32,256]{2,1,0:T(8,128)(2,1)S(1)} async-done(((bf16[16,32,256]{2,1,0:T(8,128)(2,1)}), bf16[16,32,256]{2,1,0:T(8,128)(2,1)S(1)}, u32[]{:S(2)}, u32[]{:S(2)}) %all-to-all-start.1) | async-done | bytes 262176 | tf_op jit(solution)/shard_map/all_to_all | solution.py:205
  53.0 0.8 collective-permute-start
  53.8 0.5 collective-permute-start.7
  54.3 0.8 collective-permute-done.7.refs_2_
  55.1 3.6 %all-to-all-start.2 = ((bf16[16,64,256]{2,1,0:T(8,128)(2,1)}), bf16[16,64,256]{2,1,0:T(8,128)(2,1)S(1)}, u32[]{:S(2)}, u32[]{:S(2)}) async-start(bf16[16,64,256]{2,1,0:T(8,128)(2,1)} %shard_map.96), calls=%async_computation.2 | async-start | bytes 1048576 | tf_op jit(solution)/shard_map/all_to_all | solution.py:205
  58.7 0.0 collective-permute-done.1
  58.7 5.5 %collective-permute-done.2 = bf16[1024,512]{1,0:T(8,128)(2,1)} collective-permute-done((bf16[1024,512]{1,0:T(8,128)(2,1)}, bf16[1024,512]{1,0:T(8,128)(2,1)}, u32[]{:S(2)}, u32[]{:S(2)}) %collective-permute-start.2) | collective-permute-done | bytes 1048608 | tf_op jit(solution)/shard_map/ppermute | solution.py:192
  64.2 1.7 %collective-permute-done.3 = bf16[1024,512]{1,0:T(8,128)(2,1)S(1)} collective-permute-done((bf16[1024,512]{1,0:T(8,128)(2,1)}, bf16[1024,512]{1,0:T(8,128)(2,1)S(1)}, u32[]{:S(2)}, u32[]{:S(2)}) %collective-permute-start.3) | collective-permute-done | bytes 1048608 | tf_op jit(solution)/shard_map/ppermute | solution.py:192
  66.0 0.0 collective-permute-done
  66.0 1.1 %collective-permute-start.6 = (bf16[512,256]{1,0:T(8,128)(2,1)S(1)}, bf16[512,256]{1,0:T(8,128)(2,1)S(1)}, u32[]{:S(2)}, u32[]{:S(2)}) collective-permute-start(bf16[512,256]{1,0:T(8,128)(2,1)S(1)} %collective-permute-done), channel_id=1, source_target_pairs={{0,1},{1,2},{2,3},{3,0},{4,5},{5,6},{6,7},{7,4},{8,9},{9,10},{10,1... | collective-permute-start | bytes 786440 | tf_op jit(solution)/shard_map/ppermute | solution.py:192
  67.1 2.1 %collective-permute-start.5 = (bf16[512,256]{1,0:T(8,128)(2,1)S(1)}, bf16[512,256]{1,0:T(8,128)(2,1)S(1)}, u32[]{:S(2)}, u32[]{:S(2)}) collective-permute-start(bf16[512,256]{1,0:T(8,128)(2,1)S(1)} %collective-permute-done), channel_id=1, source_target_pairs={{0,3},{1,0},{2,1},{3,2},{4,7},{5,4},{6,5},{7,6},{8,11},{9,8},{10,9... | collective-permute-start | bytes 786440 | tf_op jit(solution)/shard_map/ppermute | solution.py:192
  69.2 0.2 collective-permute-start.4
  69.4 1.7 %fusion = f32[256,1024]{1,0:T(8,128)S(1)} fusion(bf16[512,256]{1,0:T(8,128)(2,1)S(1)} %collective-permute-done, bf16[1,4096,512]{2,1,0:T(8,128)(2,1)} %param.11, s32[]{:T(128)S(6)} %select_n.3), kind=kOutput, calls=%fused_computation | convolution fusion | flops 268435456 | bytes 2359300 | tf_op jit(solution)/shard_map/dot_general | solution.py:268
  71.1 9.6 %collective-permute-done.6 = bf16[512,256]{1,0:T(8,128)(2,1)S(1)} collective-permute-done((bf16[512,256]{1,0:T(8,128)(2,1)S(1)}, bf16[512,256]{1,0:T(8,128)(2,1)S(1)}, u32[]{:S(2)}, u32[]{:S(2)}) %collective-permute-start.6) | collective-permute-done | bytes 262176 | tf_op jit(solution)/shard_map/ppermute | solution.py:192
  80.6 1.7 %fusion.5 = f32[256,1024]{1,0:T(8,128)S(1)} fusion(bf16[512,256]{1,0:T(8,128)(2,1)S(1)} %collective-permute-done.6, bf16[1024,512]{1,0:T(8,128)(2,1)} %collective-permute-done.1), kind=kOutput, calls=%fused_computation.7 | convolution fusion | flops 268435456 | bytes 2359296 | tf_op jit(solution)/shard_map/dot_general | solution.py:268
  82.4 0.0 copy-start
  82.4 0.2 add.25
  82.6 0.0 collective-permute-done.5
  82.6 1.7 %fusion.6 = f32[256,1024]{1,0:T(8,128)S(1)} fusion(bf16[512,256]{1,0:T(8,128)(2,1)S(1)} %collective-permute-done.5, bf16[1024,512]{1,0:T(8,128)(2,1)} %collective-permute-done.2), kind=kOutput, calls=%fused_computation.8 | convolution fusion | flops 268435456 | bytes 2359296 | tf_op jit(solution)/shard_map/dot_general | solution.py:268
  84.3 0.2 add.26
  84.5 0.0 collective-permute-done.4
  84.5 0.0 all-to-all-done.2.refs_0_
  84.5 0.0 copy-done
  84.5 1.0 %shard_map.98 = (bf16[256,512]{1,0:T(8,128)(2,1)}, f32[256,512]{1,0:T(8,128)}) custom-call(bf16[16,64,256]{2,1,0:T(8,128)(2,1)S(1)} %all-to-all-done.2.refs_0_, bf16[256,512]{1,0:T(8,128)(2,1)S(1)} %bitcast.25, bf16[16,128]{1,0:T(8,128)(2,1)S(1)} %collective-permute-done.7.refs_2_), custom_call_target="tpu_custom_call" | custom-call | tf_op jit(solution)/shard_map/pallas_call | solution.py:180
  85.5 1.4 %fusion.7 = f32[256,1024]{1,0:T(8,128)S(1)} fusion(bf16[512,256]{1,0:T(8,128)(2,1)} %collective-permute-done.4, bf16[1024,512]{1,0:T(8,128)(2,1)S(1)} %collective-permute-done.3), kind=kOutput, calls=%fused_computation.9 | convolution fusion | flops 268435456 | bytes 2359296 | tf_op jit(solution)/shard_map/dot_general | solution.py:268
  87.0 0.9 %fusion.3 = bf16[1,256,1024]{2,1,0:T(8,128)(2,1)} fusion(f32[256,1024]{1,0:T(8,128)S(1)} %add.26, f32[256,1024]{1,0:T(8,128)S(1)} %fusion.7), kind=kLoop, calls=%fused_computation.4 | loop fusion | flops 524288 | bytes 2621440 | tf_op jit(solution)/shard_map/broadcast_in_dim | solution.py:289
  (1 shorter events, 0.0 us)
Async XLA Ops:
  0.6 31.7 %copy-start.1 = (bf16[256,512]{1,0:T(8,128)(2,1)S(1)}, bf16[256,512]{1,0:T(8,128)(2,1)}, u32[]{:S(2)}) copy-start(bf16[256,512]{1,0:T(8,128)(2,1)} %constant.28.clone.refs_1_) | copy-start | bytes 786436
  0.6 31.7 %copy-start.2 = (bf16[256,512]{1,0:T(8,128)(2,1)S(1)}, bf16[256,512]{1,0:T(8,128)(2,1)}, u32[]{:S(2)}) copy-start(bf16[256,512]{1,0:T(8,128)(2,1)} %constant.29.clone.refs_2_) | copy-start | bytes 786436
  3.1 29.3 %all-to-all-start = ((bf16[16,96,256]{2,1,0:T(8,128)(2,1)}), bf16[16,96,256]{2,1,0:T(8,128)(2,1)S(1)}, u32[]{:S(2)}, u32[]{:S(2)}) async-start(bf16[16,96,256]{2,1,0:T(8,128)(2,1)} %shard_map.94), calls=%async_computation | async-start | bytes 1572864 | tf_op jit(solution)/shard_map/all_to_all | solution.py:205
  15.3 43.4 %collective-permute-start.1 = (bf16[1024,512]{1,0:T(8,128)(2,1)}, bf16[1024,512]{1,0:T(8,128)(2,1)}, u32[]{:S(2)}, u32[]{:S(2)}) collective-permute-start(bf16[1024,512]{1,0:T(8,128)(2,1)} %get-tuple-element.26), channel_id=1, source_target_pairs={{0,1},{1,2},{2,3},{3,0},{4,5},{5,6},{6,7},{7,4},{8,9},{9,10},{10,1... | collective-permute-start | bytes 3145736 | tf_op jit(solution)/shard_map/ppermute | solution.py:192
  16.9 47.3 %collective-permute-start.2 = (bf16[1024,512]{1,0:T(8,128)(2,1)}, bf16[1024,512]{1,0:T(8,128)(2,1)}, u32[]{:S(2)}, u32[]{:S(2)}) collective-permute-start(bf16[1024,512]{1,0:T(8,128)(2,1)} %get-tuple-element.27), channel_id=1, source_target_pairs={{0,3},{1,0},{2,1},{3,2},{4,7},{5,4},{6,5},{7,6},{8,11},{9,8},{10,9... | collective-permute-start | bytes 3145736 | tf_op jit(solution)/shard_map/ppermute | solution.py:192
  18.6 47.4 %collective-permute-start.3 = (bf16[1024,512]{1,0:T(8,128)(2,1)}, bf16[1024,512]{1,0:T(8,128)(2,1)S(1)}, u32[]{:S(2)}, u32[]{:S(2)}) collective-permute-start(bf16[1024,512]{1,0:T(8,128)(2,1)} %get-tuple-element.28), channel_id=1, source_target_pairs={{0,2},{1,3},{2,0},{3,1},{4,6},{5,7},{6,4},{7,5},{8,10},{9,11},{10,... | collective-permute-start | bytes 3145736 | tf_op jit(solution)/shard_map/ppermute | solution.py:192
  36.4 16.5 %all-to-all-start.1 = ((bf16[16,32,256]{2,1,0:T(8,128)(2,1)}), bf16[16,32,256]{2,1,0:T(8,128)(2,1)S(1)}, u32[]{:S(2)}, u32[]{:S(2)}) async-start(bf16[16,32,256]{2,1,0:T(8,128)(2,1)} %bitcast.27), calls=%async_computation.1 | async-start | bytes 524288 | tf_op jit(solution)/shard_map/all_to_all | solution.py:205
  53.0 13.0 %collective-permute-start = (bf16[512,256]{1,0:T(8,128)(2,1)S(1)}, bf16[512,256]{1,0:T(8,128)(2,1)S(1)}, u32[]{:S(2)}, u32[]{:S(2)}) collective-permute-start(bf16[512,256]{1,0:T(8,128)(2,1)S(1)} %bitcast.28), channel_id=1, source_target_pairs={{0,192},{64,0},{128,64},{192,128},{1,193},{65,1},{129,65},{193,129... | collective-permute-start | bytes 786440 | tf_op jit(solution)/shard_map/ppermute | solution.py:192
  53.8 1.3 %collective-permute-start.7 = (bf16[16,128]{1,0:T(8,128)(2,1)S(1)}, bf16[16,128]{1,0:T(8,128)(2,1)S(1)}, u32[]{:S(2)}, u32[]{:S(2)}) collective-permute-start(bf16[16,128]{1,0:T(8,128)(2,1)S(1)} %slice.3), channel_id=1, source_target_pairs={{0,4},{4,0},{8,12},{12,8},{16,20},{20,16},{24,28},{28,24},{32,36},... | collective-permute-start | bytes 12296 | tf_op jit(solution)/shard_map/ppermute | solution.py:262
  55.1 29.4 %all-to-all-start.2 = ((bf16[16,64,256]{2,1,0:T(8,128)(2,1)}), bf16[16,64,256]{2,1,0:T(8,128)(2,1)S(1)}, u32[]{:S(2)}, u32[]{:S(2)}) async-start(bf16[16,64,256]{2,1,0:T(8,128)(2,1)} %shard_map.96), calls=%async_computation.2 | async-start | bytes 1048576 | tf_op jit(solution)/shard_map/all_to_all | solution.py:205
  66.0 14.7 %collective-permute-start.6 = (bf16[512,256]{1,0:T(8,128)(2,1)S(1)}, bf16[512,256]{1,0:T(8,128)(2,1)S(1)}, u32[]{:S(2)}, u32[]{:S(2)}) collective-permute-start(bf16[512,256]{1,0:T(8,128)(2,1)S(1)} %collective-permute-done), channel_id=1, source_target_pairs={{0,1},{1,2},{2,3},{3,0},{4,5},{5,6},{6,7},{7,4},{8,9},{9,10},{10,1... | collective-permute-start | bytes 786440 | tf_op jit(solution)/shard_map/ppermute | solution.py:192
  67.1 15.4 %collective-permute-start.5 = (bf16[512,256]{1,0:T(8,128)(2,1)S(1)}, bf16[512,256]{1,0:T(8,128)(2,1)S(1)}, u32[]{:S(2)}, u32[]{:S(2)}) collective-permute-start(bf16[512,256]{1,0:T(8,128)(2,1)S(1)} %collective-permute-done), channel_id=1, source_target_pairs={{0,3},{1,0},{2,1},{3,2},{4,7},{5,4},{6,5},{7,6},{8,11},{9,8},{10,9... | collective-permute-start | bytes 786440 | tf_op jit(solution)/shard_map/ppermute | solution.py:192
  69.2 15.3 %collective-permute-start.4 = (bf16[512,256]{1,0:T(8,128)(2,1)S(1)}, bf16[512,256]{1,0:T(8,128)(2,1)}, u32[]{:S(2)}, u32[]{:S(2)}) collective-permute-start(bf16[512,256]{1,0:T(8,128)(2,1)S(1)} %collective-permute-done), channel_id=1, source_target_pairs={{0,2},{1,3},{2,0},{3,1},{4,6},{5,7},{6,4},{7,5},{8,10},{9,11},{10,... | collective-permute-start | bytes 786440 | tf_op jit(solution)/shard_map/ppermute | solution.py:192
  82.4 2.1 %copy-start = (bf16[1,256,512]{2,1,0:T(8,128)(2,1)S(1)}, bf16[1,256,512]{2,1,0:T(8,128)(2,1)}, u32[]{:S(2)}) copy-start(bf16[1,256,512]{2,1,0:T(8,128)(2,1)} %param.9) | copy-start | bytes 786436

commit v7 on v6

--- a/solution.py
+++ b/solution.py
@@ -6,6 +6,9 @@
 from jax.experimental import pallas as pl
 from jax.experimental.pallas import tpu as pltpu
 from jax.sharding import PartitionSpec as P
+
+
+HINT_SCALE = 14
 
 
 def make_tables(panel_len):
@@ -176,13 +179,32 @@
     filter_out[...] = by_rows(parts_ref, 1, chans).T.astype(jnp.float32)
 
 
-def call(kernel, panels, outs, scratch, *operands, space=pltpu.VMEM):
+def project_kernel(panels, *refs):
+    count = (len(refs) - 3) // 3
+    total_ref, blocks, weights = refs[0], refs[1 : 1 + count], refs[1 + count : 1 + 2 * count]
+    out_ref, held, sems = refs[1 + 2 * count], refs[2 + 2 * count : -1], refs[-1]
+    copies = [pltpu.make_async_copy(weights[at], held[at], sems.at[at]) for at in range(count)]
+    for copy in copies:
+        copy.start()
+    total = total_ref[...]
+    for at in range(count):
+        block = blocks[at][...].T
+        copies[at].wait()
+        total = total + lax.dot_general(
+            block, held[at][...], (((1,), (1,)), ((), ())), preferred_element_type=jnp.float32
+        )
+    out_ref[...] = total.astype(out_ref.dtype)
+
+
+def call(kernel, panels, outs, scratch, *operands, space=pltpu.VMEM, streamed=0, cost=None):
     return pl.pallas_call(
         lambda *refs: kernel(panels, *refs),
         out_shape=outs,
-        in_specs=[pl.BlockSpec(memory_space=space)] * len(operands),
+        in_specs=[pl.BlockSpec(memory_space=space)] * (len(operands) - streamed)
+        + [pl.BlockSpec(memory_space=pltpu.HBM)] * streamed,
         out_specs=[pl.BlockSpec(memory_space=pltpu.VMEM)] * len(outs),
         scratch_shapes=scratch,
+        cost_estimate=cost,
         compiler_params=pltpu.CompilerParams(vmem_limit_bytes=16 * 1024 * 1024),
     )(*operands)
 
@@ -279,13 +301,34 @@
         token,
     )
     total = project(received, lax.dynamic_slice_in_dim(weight[0], my_group * outputs, outputs, 0))
-    for by, part in zip((1, 3, 2), weights):
-        block = shifted(received, "chan", by)
-        block, total = lax.optimization_barrier((block, total))
-        if by == 2:
-            block, gate_grad, filter_grad = lax.optimization_barrier((block, gate_grad, filter_grad))
-        total = total + project(block, part)
-    input_grad = total.astype(jnp.bfloat16)
+    blocks = [shifted(received, "chan", by) for by in (1, 3, 2)]
+
+    def add_blocks(total, which, dtype):
+        count = len(which)
+        (added,) = call(
+            project_kernel,
+            panels,
+            (shape(panel_len, outputs, dtype=dtype),),
+            [pltpu.VMEM((outputs, width), jnp.bfloat16)] * count
+            + [pltpu.SemaphoreType.DMA((count,))],
+            total,
+            *(blocks[at] for at in which),
+            *(pltpu.with_memory_space_constraint(weights[at], pltpu.HBM) for at in which),
+            streamed=count,
+            cost=pl.CostEstimate(
+                flops=HINT_SCALE * 2 * count * panel_len * width * outputs,
+                transcendentals=0,
+                bytes_accessed=HINT_SCALE * 2 * count * outputs * width,
+            ),
+        )
+        return added
+
+    blocks[:2], total = lax.optimization_barrier((blocks[:2], total))
+    total = add_blocks(total, (0, 1), jnp.float32)
+    blocks[2], total, gate_grad, filter_grad = lax.optimization_barrier(
+        (blocks[2], total, gate_grad, filter_grad)
+    )
+    input_grad = add_blocks(total, (2,), jnp.bfloat16)
     return gate_grad[None], filter_grad[None], input_grad[None]
 
 

time: 88.4 us -> 87.7 us (level)
  matrix products: 6.54 us -> 1.71 us
  Pallas kernels: 17.3 us -> 21.9 us
  other arithmetic: 1.36 us -> 0.08 us
    dot_general x4 -> x1, matrix products: 6.54 us -> 1.71 us  [project(): lax.dot_general(block, block_weight, (((0,), (1,)), ((), ())), preferred_...]
    pallas_call x4 -> x6, Pallas kernels: 13.8 us -> 18.4 us  [call(): pl.pallas_call(lambda *refs: kernel(panels, *refs), out_shape=outs, in_sp...]
    broadcast_in_dim x1 -> x0, other arithmetic: 0.93 us -> none  [on_device(): return (gate_grad[None], filter_grad[None], input_grad[None])]
  transfers between devices with their start and end apart: 11 -> 11, of which waited for: 6 -> 7; matrix products, arithmetic and copies ran while one was open for 6% -> 2% of each run, Pallas kernels for 16% -> 19%
where the time goes in v7:
time: 87.7 us; the launch traced here: 87.2 us
  waiting for transfers between devices  35.3 us (40%)
  starting transfers between devices  27.5 us (31%)
  Pallas kernels  21.9 us (25%)
  matrix products  1.71 us (2%)
    pallas_call x6, Pallas kernels, call(): pl.pallas_call(lambda *refs: kernel(panels, *refs), out_shape=outs, in_sp...  18.4 us
    ppermute x7, waiting for transfers between devices, shifted(): lax.ppermute(x, axis, [(i, (i + by) % length) for i in range(length)])  17.6 us
    all_to_all x3, starting transfers between devices, swapped(): return lax.all_to_all(parts, 'seq', 0, 0, tiled=True)  17.3 us
    all_to_all x3, waiting for transfers between devices, swapped(): return lax.all_to_all(parts, 'seq', 0, 0, tiled=True)  16.9 us
    ppermute x7, starting transfers between devices, shifted(): lax.ppermute(x, axis, [(i, (i + by) % length) for i in range(length)])  9.7 us
    pallas_call x1, Pallas kernels, on_device(): pl.pallas_call(weight_kernel, out_shape=[pltpu.HBM((outputs, width), jnp....  3.5 us
  transfers between devices with their start and end apart: 11, of which 7 were waited for; matrix products, arithmetic and copies ran while one was open for 2% of the time, Pallas kernels for 19%

profile of v7, /device:TPU:6, one launch (start us, length us, event | category | flops | bytes accessed | tf_op | source)
XLA Modules:
  0.0 87.2 jit_solution(17095960505837328642)
XLA Ops:
  0.6 0.0 copy-start.1
  0.6 0.0 copy-start.2
  0.7 2.4 %shard_map.94 = bf16[16,96,256]{2,1,0:T(8,128)(2,1)} custom-call(bf16[256,512]{1,0:T(8,128)(2,1)} %bitcast.23, bf16[256,512]{1,0:T(8,128)(2,1)} %bitcast.24, bf16[256,512]{1,0:T(8,128)(2,1)} %bitcast.17, bf16[256,512]{1,0:T(8,128)(2,1)} %bitcast.25), custom_call_target="tpu_custom_call" | custom-call | tf_op jit(solution)/shard_map/pallas_call | solution.py:200
  3.0 8.6 %all-to-all-start = ((bf16[16,96,256]{2,1,0:T(8,128)(2,1)}), bf16[16,96,256]{2,1,0:T(8,128)(2,1)S(1)}, u32[]{:S(2)}, u32[]{:S(2)}) async-start(bf16[16,96,256]{2,1,0:T(8,128)(2,1)} %shard_map.94), calls=%async_computation | async-start | bytes 1572864 | tf_op jit(solution)/shard_map/all_to_all | solution.py:227
  11.6 0.1 pad_add_fusion.starts_ref
  11.7 3.5 %shard_map.97 = (bf16[1024,512]{1,0:T(8,128)(2,1)}, bf16[1024,512]{1,0:T(8,128)(2,1)}, bf16[1024,512]{1,0:T(8,128)(2,1)}) custom-call(s32[3]{0:T(128)S(1)} %pad_add_fusion.starts_ref, bf16[4096,512]{1,0:T(8,128)(2,1)} %bitcast.19), custom_call_target="tpu_custom_call" | custom-call | tf_op jit(solution)/shard_map/pallas_call | solution.py:248
  15.2 1.7 %collective-permute-start.1 = (bf16[1024,512]{1,0:T(8,128)(2,1)}, bf16[1024,512]{1,0:T(8,128)(2,1)}, u32[]{:S(2)}, u32[]{:S(2)}) collective-permute-start(bf16[1024,512]{1,0:T(8,128)(2,1)} %get-tuple-element.24), channel_id=1, source_target_pairs={{0,1},{1,2},{2,3},{3,0},{4,5},{5,6},{6,7},{7,4},{8,9},{9,10},{10,1... | collective-permute-start | bytes 3145736 | tf_op jit(solution)/shard_map/ppermute | solution.py:214
  16.9 1.7 %collective-permute-start.2 = (bf16[1024,512]{1,0:T(8,128)(2,1)}, bf16[1024,512]{1,0:T(8,128)(2,1)}, u32[]{:S(2)}, u32[]{:S(2)}) collective-permute-start(bf16[1024,512]{1,0:T(8,128)(2,1)} %get-tuple-element.25), channel_id=1, source_target_pairs={{0,3},{1,0},{2,1},{3,2},{4,7},{5,4},{6,5},{7,6},{8,11},{9,8},{10,9... | collective-permute-start | bytes 3145736 | tf_op jit(solution)/shard_map/ppermute | solution.py:214
  18.5 2.0 %collective-permute-start.3 = (bf16[1024,512]{1,0:T(8,128)(2,1)}, bf16[1024,512]{1,0:T(8,128)(2,1)S(1)}, u32[]{:S(2)}, u32[]{:S(2)}) collective-permute-start(bf16[1024,512]{1,0:T(8,128)(2,1)} %get-tuple-element.26), channel_id=1, source_target_pairs={{0,2},{1,3},{2,0},{3,1},{4,6},{5,7},{6,4},{7,5},{8,10},{9,11},{10,... | collective-permute-start | bytes 3145736 | tf_op jit(solution)/shard_map/ppermute | solution.py:214
  20.5 11.8 %all-to-all-done.refs_0_ = bf16[16,96,256]{2,1,0:T(8,128)(2,1)S(1)} async-done(((bf16[16,96,256]{2,1,0:T(8,128)(2,1)}), bf16[16,96,256]{2,1,0:T(8,128)(2,1)S(1)}, u32[]{:S(2)}, u32[]{:S(2)}) %all-to-all-start) | async-done | bytes 786464 | tf_op jit(solution)/shard_map/all_to_all | solution.py:227
  32.3 0.0 copy-done.1
  32.3 0.0 copy-done.2
  32.3 4.1 %shard_map.95 = bf16[512,256]{1,0:T(8,128)(2,1)} custom-call(bf16[16,96,256]{2,1,0:T(8,128)(2,1)S(1)} %all-to-all-done.refs_0_, bf16[256,512]{1,0:T(8,128)(2,1)S(1)} %copy-done.2, bf16[256,512]{1,0:T(8,128)(2,1)S(1)} %copy-done.1), custom_call_target="tpu_custom_call" | custom-call | tf_op jit(solution)/shard_map/pallas_call | solution.py:200
  36.4 5.1 %all-to-all-start.1 = ((bf16[16,32,256]{2,1,0:T(8,128)(2,1)}), bf16[16,32,256]{2,1,0:T(8,128)(2,1)S(1)}, u32[]{:S(2)}, u32[]{:S(2)}) async-start(bf16[16,32,256]{2,1,0:T(8,128)(2,1)} %bitcast.20), calls=%async_computation.1 | async-start | bytes 524288 | tf_op jit(solution)/shard_map/all_to_all | solution.py:227
  41.5 6.3 %shard_map.96 = bf16[16,64,256]{2,1,0:T(8,128)(2,1)} custom-call(bf16[16,96,256]{2,1,0:T(8,128)(2,1)S(1)} %all-to-all-done.refs_0_, bf16[256,512]{1,0:T(8,128)(2,1)S(1)} %copy-done.2, bf16[256,512]{1,0:T(8,128)(2,1)S(1)} %copy-done.1), custom_call_target="tpu_custom_call" | custom-call | tf_op jit(solution)/shard_map/pallas_call | solution.py:200
  47.9 5.1 %all-to-all-done.1 = bf16[16,32,256]{2,1,0:T(8,128)(2,1)S(1)} async-done(((bf16[16,32,256]{2,1,0:T(8,128)(2,1)}), bf16[16,32,256]{2,1,0:T(8,128)(2,1)S(1)}, u32[]{:S(2)}, u32[]{:S(2)}) %all-to-all-start.1) | async-done | bytes 262176 | tf_op jit(solution)/shard_map/all_to_all | solution.py:227
  52.9 0.8 collective-permute-start
  53.8 0.5 collective-permute-start.7
  54.3 0.8 collective-permute-done.7.refs_2_
  55.1 3.6 %all-to-all-start.2 = ((bf16[16,64,256]{2,1,0:T(8,128)(2,1)}), bf16[16,64,256]{2,1,0:T(8,128)(2,1)S(1)}, u32[]{:S(2)}, u32[]{:S(2)}) async-start(bf16[16,64,256]{2,1,0:T(8,128)(2,1)} %shard_map.96), calls=%async_computation.2 | async-start | bytes 1048576 | tf_op jit(solution)/shard_map/all_to_all | solution.py:227
  58.7 0.0 collective-permute-done.1.refs_3_
  58.7 5.5 %collective-permute-done.2.refs_4_ = bf16[1024,512]{1,0:T(8,128)(2,1)} collective-permute-done((bf16[1024,512]{1,0:T(8,128)(2,1)}, bf16[1024,512]{1,0:T(8,128)(2,1)}, u32[]{:S(2)}, u32[]{:S(2)}) %collective-permute-start.2) | collective-permute-done | bytes 1048608 | tf_op jit(solution)/shard_map/ppermute | solution.py:214
  64.2 1.7 %collective-permute-done.3.refs_2_ = bf16[1024,512]{1,0:T(8,128)(2,1)S(1)} collective-permute-done((bf16[1024,512]{1,0:T(8,128)(2,1)}, bf16[1024,512]{1,0:T(8,128)(2,1)S(1)}, u32[]{:S(2)}, u32[]{:S(2)}) %collective-permute-start.3) | collective-permute-done | bytes 1048608 | tf_op jit(solution)/shard_map/ppermute | solution.py:214
  65.9 0.0 copy-start.3
  65.9 0.0 collective-permute-done
  65.9 2.0 %collective-permute-start.6 = (bf16[512,256]{1,0:T(8,128)(2,1)S(1)}, bf16[512,256]{1,0:T(8,128)(2,1)S(1)}, u32[]{:S(2)}, u32[]{:S(2)}) collective-permute-start(bf16[512,256]{1,0:T(8,128)(2,1)S(1)} %collective-permute-done), channel_id=1, source_target_pairs={{0,3},{1,0},{2,1},{3,2},{4,7},{5,4},{6,5},{7,6},{8,11},{9,8},{10,9... | collective-permute-start | bytes 786440 | tf_op jit(solution)/shard_map/ppermute | solution.py:214
  68.0 0.0 collective-permute-start.5
  68.0 1.6 %collective-permute-start.4 = (bf16[512,256]{1,0:T(8,128)(2,1)S(1)}, bf16[512,256]{1,0:T(8,128)(2,1)S(1)}, u32[]{:S(2)}, u32[]{:S(2)}) collective-permute-start(bf16[512,256]{1,0:T(8,128)(2,1)S(1)} %collective-permute-done), channel_id=1, source_target_pairs={{0,2},{1,3},{2,0},{3,1},{4,6},{5,7},{6,4},{7,5},{8,10},{9,11},{10,... | collective-permute-start | bytes 786440 | tf_op jit(solution)/shard_map/ppermute | solution.py:214
  69.5 0.0 copy-done.3
  69.5 1.7 %fusion.refs_0_ = f32[256,1024]{1,0:T(8,128)S(1)} fusion(bf16[512,256]{1,0:T(8,128)(2,1)S(1)} %collective-permute-done, bf16[1,4096,512]{2,1,0:T(8,128)(2,1)} %param.11, s32[]{:T(128)S(6)} %select_n.3), kind=kOutput, calls=%fused_computation | convolution fusion | flops 268435456 | bytes 2359300 | tf_op jit(solution)/shard_map/dot_general | solution.py:290
  71.2 0.0 copy-start
  71.2 3.9 %collective-permute-done.6.refs_2_ = bf16[512,256]{1,0:T(8,128)(2,1)S(1)} collective-permute-done((bf16[512,256]{1,0:T(8,128)(2,1)S(1)}, bf16[512,256]{1,0:T(8,128)(2,1)S(1)}, u32[]{:S(2)}, u32[]{:S(2)}) %collective-permute-start.6) | collective-permute-done | bytes 262176 | tf_op jit(solution)/shard_map/ppermute | solution.py:214
  75.2 6.4 %collective-permute-done.5.refs_1_ = bf16[512,256]{1,0:T(8,128)(2,1)S(1)} collective-permute-done((bf16[512,256]{1,0:T(8,128)(2,1)S(1)}, bf16[512,256]{1,0:T(8,128)(2,1)S(1)}, u32[]{:S(2)}, u32[]{:S(2)}) %collective-permute-start.5) | collective-permute-done | bytes 262176 | tf_op jit(solution)/shard_map/ppermute | solution.py:214
  81.6 2.1 %shard_map.98.refs_0_ = f32[256,1024]{1,0:T(8,128)S(1)} custom-call(f32[256,1024]{1,0:T(8,128)S(1)} %fusion.refs_0_, bf16[512,256]{1,0:T(8,128)(2,1)S(1)} %collective-permute-done.5.refs_1_, bf16[512,256]{1,0:T(8,128)(2,1)S(1)} %collective-permute-done.6.refs_2_, bf16[1024,512]{1,0:T(8,128)(2,1)} %collective-permute-done.1.refs_3_, ...), custom_call_target="tpu_custom_call" | custom-call | flops 7516192768 | bytes 29360128 | tf_op jit(solution)/shard_map/pallas_call | solution.py:200
  83.7 0.0 all-to-all-done.2.refs_0_
  83.7 0.0 copy-done
  83.7 1.0 %shard_map.99 = (bf16[256,512]{1,0:T(8,128)(2,1)}, f32[256,512]{1,0:T(8,128)}) custom-call(bf16[16,64,256]{2,1,0:T(8,128)(2,1)S(1)} %all-to-all-done.2.refs_0_, bf16[256,512]{1,0:T(8,128)(2,1)S(1)} %bitcast.18, bf16[16,128]{1,0:T(8,128)(2,1)S(1)} %collective-permute-done.7.refs_2_), custom_call_target="tpu_custom_call" | custom-call | tf_op jit(solution)/shard_map/pallas_call | solution.py:200
  84.7 0.0 collective-permute-done.4.refs_1_
  84.7 2.5 %shard_map.100 = bf16[256,1024]{1,0:T(8,128)(2,1)} custom-call(f32[256,1024]{1,0:T(8,128)S(1)} %shard_map.98.refs_0_, bf16[512,256]{1,0:T(8,128)(2,1)S(1)} %collective-permute-done.4.refs_1_, bf16[1024,512]{1,0:T(8,128)(2,1)} %copy-done.3), custom_call_target="tpu_custom_call" | custom-call | flops 3758096384 | bytes 14680064 | tf_op jit(solution)/shard_map/pallas_call | solution.py:200
  (1 shorter events, 0.0 us)
Async XLA Ops:
  0.6 31.7 %copy-start.1 = (bf16[256,512]{1,0:T(8,128)(2,1)S(1)}, bf16[256,512]{1,0:T(8,128)(2,1)}, u32[]{:S(2)}) copy-start(bf16[256,512]{1,0:T(8,128)(2,1)} %constant.29.clone.refs_2_) | copy-start | bytes 786436
  0.6 31.7 %copy-start.2 = (bf16[256,512]{1,0:T(8,128)(2,1)S(1)}, bf16[256,512]{1,0:T(8,128)(2,1)}, u32[]{:S(2)}) copy-start(bf16[256,512]{1,0:T(8,128)(2,1)} %constant.28.clone.refs_1_) | copy-start | bytes 786436
  3.0 29.3 %all-to-all-start = ((bf16[16,96,256]{2,1,0:T(8,128)(2,1)}), bf16[16,96,256]{2,1,0:T(8,128)(2,1)S(1)}, u32[]{:S(2)}, u32[]{:S(2)}) async-start(bf16[16,96,256]{2,1,0:T(8,128)(2,1)} %shard_map.94), calls=%async_computation | async-start | bytes 1572864 | tf_op jit(solution)/shard_map/all_to_all | solution.py:227
  15.2 43.4 %collective-permute-start.1 = (bf16[1024,512]{1,0:T(8,128)(2,1)}, bf16[1024,512]{1,0:T(8,128)(2,1)}, u32[]{:S(2)}, u32[]{:S(2)}) collective-permute-start(bf16[1024,512]{1,0:T(8,128)(2,1)} %get-tuple-element.24), channel_id=1, source_target_pairs={{0,1},{1,2},{2,3},{3,0},{4,5},{5,6},{6,7},{7,4},{8,9},{9,10},{10,1... | collective-permute-start | bytes 3145736 | tf_op jit(solution)/shard_map/ppermute | solution.py:214
  16.9 47.3 %collective-permute-start.2 = (bf16[1024,512]{1,0:T(8,128)(2,1)}, bf16[1024,512]{1,0:T(8,128)(2,1)}, u32[]{:S(2)}, u32[]{:S(2)}) collective-permute-start(bf16[1024,512]{1,0:T(8,128)(2,1)} %get-tuple-element.25), channel_id=1, source_target_pairs={{0,3},{1,0},{2,1},{3,2},{4,7},{5,4},{6,5},{7,6},{8,11},{9,8},{10,9... | collective-permute-start | bytes 3145736 | tf_op jit(solution)/shard_map/ppermute | solution.py:214
  18.5 47.4 %collective-permute-start.3 = (bf16[1024,512]{1,0:T(8,128)(2,1)}, bf16[1024,512]{1,0:T(8,128)(2,1)S(1)}, u32[]{:S(2)}, u32[]{:S(2)}) collective-permute-start(bf16[1024,512]{1,0:T(8,128)(2,1)} %get-tuple-element.26), channel_id=1, source_target_pairs={{0,2},{1,3},{2,0},{3,1},{4,6},{5,7},{6,4},{7,5},{8,10},{9,11},{10,... | collective-permute-start | bytes 3145736 | tf_op jit(solution)/shard_map/ppermute | solution.py:214
  36.4 16.5 %all-to-all-start.1 = ((bf16[16,32,256]{2,1,0:T(8,128)(2,1)}), bf16[16,32,256]{2,1,0:T(8,128)(2,1)S(1)}, u32[]{:S(2)}, u32[]{:S(2)}) async-start(bf16[16,32,256]{2,1,0:T(8,128)(2,1)} %bitcast.20), calls=%async_computation.1 | async-start | bytes 524288 | tf_op jit(solution)/shard_map/all_to_all | solution.py:227
  52.9 13.0 %collective-permute-start = (bf16[512,256]{1,0:T(8,128)(2,1)S(1)}, bf16[512,256]{1,0:T(8,128)(2,1)S(1)}, u32[]{:S(2)}, u32[]{:S(2)}) collective-permute-start(bf16[512,256]{1,0:T(8,128)(2,1)S(1)} %bitcast.21), channel_id=1, source_target_pairs={{0,192},{64,0},{128,64},{192,128},{1,193},{65,1},{129,65},{193,129... | collective-permute-start | bytes 786440 | tf_op jit(solution)/shard_map/ppermute | solution.py:214
  53.8 1.3 %collective-permute-start.7 = (bf16[16,128]{1,0:T(8,128)(2,1)S(1)}, bf16[16,128]{1,0:T(8,128)(2,1)S(1)}, u32[]{:S(2)}, u32[]{:S(2)}) collective-permute-start(bf16[16,128]{1,0:T(8,128)(2,1)S(1)} %slice.3), channel_id=1, source_target_pairs={{0,4},{4,0},{8,12},{12,8},{16,20},{20,16},{24,28},{28,24},{32,36},... | collective-permute-start | bytes 12296 | tf_op jit(solution)/shard_map/ppermute | solution.py:284
  55.1 28.6 %all-to-all-start.2 = ((bf16[16,64,256]{2,1,0:T(8,128)(2,1)}), bf16[16,64,256]{2,1,0:T(8,128)(2,1)S(1)}, u32[]{:S(2)}, u32[]{:S(2)}) async-start(bf16[16,64,256]{2,1,0:T(8,128)(2,1)} %shard_map.96), calls=%async_computation.2 | async-start | bytes 1048576 | tf_op jit(solution)/shard_map/all_to_all | solution.py:227
  65.9 3.6 %copy-start.3 = (bf16[1024,512]{1,0:T(8,128)(2,1)}, bf16[1024,512]{1,0:T(8,128)(2,1)S(1)}, u32[]{:S(2)}) copy-start(bf16[1024,512]{1,0:T(8,128)(2,1)S(1)} %collective-permute-done.3.refs_2_) | copy-start | bytes 3145732
  65.9 9.2 %collective-permute-start.6 = (bf16[512,256]{1,0:T(8,128)(2,1)S(1)}, bf16[512,256]{1,0:T(8,128)(2,1)S(1)}, u32[]{:S(2)}, u32[]{:S(2)}) collective-permute-start(bf16[512,256]{1,0:T(8,128)(2,1)S(1)} %collective-permute-done), channel_id=1, source_target_pairs={{0,3},{1,0},{2,1},{3,2},{4,7},{5,4},{6,5},{7,6},{8,11},{9,8},{10,9... | collective-permute-start | bytes 786440 | tf_op jit(solution)/shard_map/ppermute | solution.py:214
  68.0 13.6 %collective-permute-start.5 = (bf16[512,256]{1,0:T(8,128)(2,1)S(1)}, bf16[512,256]{1,0:T(8,128)(2,1)S(1)}, u32[]{:S(2)}, u32[]{:S(2)}) collective-permute-start(bf16[512,256]{1,0:T(8,128)(2,1)S(1)} %collective-permute-done), channel_id=1, source_target_pairs={{0,1},{1,2},{2,3},{3,0},{4,5},{5,6},{6,7},{7,4},{8,9},{9,10},{10,1... | collective-permute-start | bytes 786440 | tf_op jit(solution)/shard_map/ppermute | solution.py:214
  68.0 16.7 %collective-permute-start.4 = (bf16[512,256]{1,0:T(8,128)(2,1)S(1)}, bf16[512,256]{1,0:T(8,128)(2,1)S(1)}, u32[]{:S(2)}, u32[]{:S(2)}) collective-permute-start(bf16[512,256]{1,0:T(8,128)(2,1)S(1)} %collective-permute-done), channel_id=1, source_target_pairs={{0,2},{1,3},{2,0},{3,1},{4,6},{5,7},{6,4},{7,5},{8,10},{9,11},{10,... | collective-permute-start | bytes 786440 | tf_op jit(solution)/shard_map/ppermute | solution.py:214
  71.2 12.4 %copy-start = (bf16[1,256,512]{2,1,0:T(8,128)(2,1)S(1)}, bf16[1,256,512]{2,1,0:T(8,128)(2,1)}, u32[]{:S(2)}) copy-start(bf16[1,256,512]{2,1,0:T(8,128)(2,1)} %param.9) | copy-start | bytes 786436

commit v8 on v7

--- a/solution.py
+++ b/solution.py
@@ -196,13 +196,39 @@
     out_ref[...] = total.astype(out_ref.dtype)
 
 
-def call(kernel, panels, outs, scratch, *operands, space=pltpu.VMEM, streamed=0, cost=None):
+def last_kernel(panels, total_ref, block_ref, weight_ref, out_ref, held, done, sems):
+    count = sems.shape[1]
+    size = out_ref.shape[1] // count
+    columns = [pl.ds(at * size, size) for at in range(count)]
+    loads = [
+        pltpu.make_async_copy(weight_ref.at[part], held.at[part], sems.at[0, at])
+        for at, part in enumerate(columns)
+    ]
+    stores = [
+        pltpu.make_async_copy(done.at[:, part], out_ref.at[:, part], sems.at[1, at])
+        for at, part in enumerate(columns)
+    ]
+    for load in loads:
+        load.start()
+    block = block_ref[...].T
+    for at, part in enumerate(columns):
+        loads[at].wait()
+        total = total_ref[:, part] + lax.dot_general(
+            block, held[part, :], (((1,), (1,)), ((), ())), preferred_element_type=jnp.float32
+        )
+        done[:, part] = total.astype(done.dtype)
+        stores[at].start()
+    for store in stores:
+        store.wait()
+
+
+def call(kernel, panels, outs, scratch, *operands, space=pltpu.VMEM, streamed=0, cost=None, out_space=pltpu.VMEM):
     return pl.pallas_call(
         lambda *refs: kernel(panels, *refs),
         out_shape=outs,
         in_specs=[pl.BlockSpec(memory_space=space)] * (len(operands) - streamed)
         + [pl.BlockSpec(memory_space=pltpu.HBM)] * streamed,
-        out_specs=[pl.BlockSpec(memory_space=pltpu.VMEM)] * len(outs),
+        out_specs=[pl.BlockSpec(memory_space=out_space)] * len(outs),
         scratch_shapes=scratch,
         cost_estimate=cost,
         compiler_params=pltpu.CompilerParams(vmem_limit_bytes=16 * 1024 * 1024),
@@ -328,7 +354,26 @@
     blocks[2], total, gate_grad, filter_grad = lax.optimization_barrier(
         (blocks[2], total, gate_grad, filter_grad)
     )
-    input_grad = add_blocks(total, (2,), jnp.bfloat16)
+    (input_grad,) = call(
+        last_kernel,
+        panels,
+        (pltpu.HBM((panel_len, outputs), jnp.bfloat16),),
+        [
+            pltpu.VMEM((outputs, width), jnp.bfloat16),
+            pltpu.VMEM((panel_len, outputs), jnp.bfloat16),
+            pltpu.SemaphoreType.DMA((2, 4)),
+        ],
+        total,
+        blocks[2],
+        pltpu.with_memory_space_constraint(weights[2], pltpu.HBM),
+        streamed=1,
+        out_space=pltpu.HBM,
+        cost=pl.CostEstimate(
+            flops=HINT_SCALE * 2 * panel_len * width * outputs,
+            transcendentals=0,
+            bytes_accessed=HINT_SCALE * 2 * outputs * width,
+        ),
+    )
     return gate_grad[None], filter_grad[None], input_grad[None]
 
 

time: 87.7 us -> 88.2 us (level)
  no operation moved by 1% of the time
where the time goes in v8:
time: 88.2 us; the launch traced here: 87.7 us
  waiting for transfers between devices  35.3 us (40%)
  starting transfers between devices  27.5 us (31%)
  Pallas kernels  22.3 us (25%)
  matrix products  1.71 us (2%)
    pallas_call x6, Pallas kernels, call(): pl.pallas_call(lambda *refs: kernel(panels, *refs), out_shape=outs, in_sp...  18.8 us
    ppermute x7, waiting for transfers between devices, shifted(): lax.ppermute(x, axis, [(i, (i + by) % length) for i in range(length)])  17.6 us
    all_to_all x3, starting transfers between devices, swapped(): return lax.all_to_all(parts, 'seq', 0, 0, tiled=True)  17.3 us
    all_to_all x3, waiting for transfers between devices, swapped(): return lax.all_to_all(parts, 'seq', 0, 0, tiled=True)  16.9 us
    ppermute x7, starting transfers between devices, shifted(): lax.ppermute(x, axis, [(i, (i + by) % length) for i in range(length)])  9.7 us
    pallas_call x1, Pallas kernels, on_device(): pl.pallas_call(weight_kernel, out_shape=[pltpu.HBM((outputs, width), jnp....  3.5 us
  transfers between devices with their start and end apart: 11, of which 7 were waited for; matrix products, arithmetic and copies ran while one was open for 2% of the time, Pallas kernels for 19%

profile of v8, /device:TPU:6, one launch (start us, length us, event | category | flops | bytes accessed | tf_op | source)
XLA Modules:
  0.0 87.7 jit_solution(11046411278791448954)
XLA Ops:
  0.6 0.0 copy-start.1
  0.6 0.0 copy-start.2
  0.7 2.4 %shard_map.94 = bf16[16,96,256]{2,1,0:T(8,128)(2,1)} custom-call(bf16[256,512]{1,0:T(8,128)(2,1)} %bitcast.23, bf16[256,512]{1,0:T(8,128)(2,1)} %bitcast.24, bf16[256,512]{1,0:T(8,128)(2,1)} %bitcast.17, bf16[256,512]{1,0:T(8,128)(2,1)} %bitcast.25), custom_call_target="tpu_custom_call" | custom-call | tf_op jit(solution)/shard_map/pallas_call | solution.py:226
  3.0 8.6 %all-to-all-start = ((bf16[16,96,256]{2,1,0:T(8,128)(2,1)}), bf16[16,96,256]{2,1,0:T(8,128)(2,1)S(1)}, u32[]{:S(2)}, u32[]{:S(2)}) async-start(bf16[16,96,256]{2,1,0:T(8,128)(2,1)} %shard_map.94), calls=%async_computation | async-start | bytes 1572864 | tf_op jit(solution)/shard_map/all_to_all | solution.py:253
  11.6 0.1 pad_add_fusion.starts_ref
  11.7 3.5 %shard_map.97 = (bf16[1024,512]{1,0:T(8,128)(2,1)}, bf16[1024,512]{1,0:T(8,128)(2,1)}, bf16[1024,512]{1,0:T(8,128)(2,1)}) custom-call(s32[3]{0:T(128)S(1)} %pad_add_fusion.starts_ref, bf16[4096,512]{1,0:T(8,128)(2,1)} %bitcast.19), custom_call_target="tpu_custom_call" | custom-call | tf_op jit(solution)/shard_map/pallas_call | solution.py:274
  15.2 1.7 %collective-permute-start.1 = (bf16[1024,512]{1,0:T(8,128)(2,1)}, bf16[1024,512]{1,0:T(8,128)(2,1)}, u32[]{:S(2)}, u32[]{:S(2)}) collective-permute-start(bf16[1024,512]{1,0:T(8,128)(2,1)} %get-tuple-element.24), channel_id=1, source_target_pairs={{0,1},{1,2},{2,3},{3,0},{4,5},{5,6},{6,7},{7,4},{8,9},{9,10},{10,1... | collective-permute-start | bytes 3145736 | tf_op jit(solution)/shard_map/ppermute | solution.py:240
  16.9 1.7 %collective-permute-start.2 = (bf16[1024,512]{1,0:T(8,128)(2,1)}, bf16[1024,512]{1,0:T(8,128)(2,1)}, u32[]{:S(2)}, u32[]{:S(2)}) collective-permute-start(bf16[1024,512]{1,0:T(8,128)(2,1)} %get-tuple-element.25), channel_id=1, source_target_pairs={{0,3},{1,0},{2,1},{3,2},{4,7},{5,4},{6,5},{7,6},{8,11},{9,8},{10,9... | collective-permute-start | bytes 3145736 | tf_op jit(solution)/shard_map/ppermute | solution.py:240
  18.5 2.0 %collective-permute-start.3 = (bf16[1024,512]{1,0:T(8,128)(2,1)}, bf16[1024,512]{1,0:T(8,128)(2,1)S(1)}, u32[]{:S(2)}, u32[]{:S(2)}) collective-permute-start(bf16[1024,512]{1,0:T(8,128)(2,1)} %get-tuple-element.26), channel_id=1, source_target_pairs={{0,2},{1,3},{2,0},{3,1},{4,6},{5,7},{6,4},{7,5},{8,10},{9,11},{10,... | collective-permute-start | bytes 3145736 | tf_op jit(solution)/shard_map/ppermute | solution.py:240
  20.5 11.8 %all-to-all-done.refs_0_ = bf16[16,96,256]{2,1,0:T(8,128)(2,1)S(1)} async-done(((bf16[16,96,256]{2,1,0:T(8,128)(2,1)}), bf16[16,96,256]{2,1,0:T(8,128)(2,1)S(1)}, u32[]{:S(2)}, u32[]{:S(2)}) %all-to-all-start) | async-done | bytes 786464 | tf_op jit(solution)/shard_map/all_to_all | solution.py:253
  32.3 0.0 copy-done.1
  32.3 0.0 copy-done.2
  32.3 4.1 %shard_map.95 = bf16[512,256]{1,0:T(8,128)(2,1)} custom-call(bf16[16,96,256]{2,1,0:T(8,128)(2,1)S(1)} %all-to-all-done.refs_0_, bf16[256,512]{1,0:T(8,128)(2,1)S(1)} %copy-done.2, bf16[256,512]{1,0:T(8,128)(2,1)S(1)} %copy-done.1), custom_call_target="tpu_custom_call" | custom-call | tf_op jit(solution)/shard_map/pallas_call | solution.py:226
  36.4 5.1 %all-to-all-start.1 = ((bf16[16,32,256]{2,1,0:T(8,128)(2,1)}), bf16[16,32,256]{2,1,0:T(8,128)(2,1)S(1)}, u32[]{:S(2)}, u32[]{:S(2)}) async-start(bf16[16,32,256]{2,1,0:T(8,128)(2,1)} %bitcast.20), calls=%async_computation.1 | async-start | bytes 524288 | tf_op jit(solution)/shard_map/all_to_all | solution.py:253
  41.5 6.3 %shard_map.96 = bf16[16,64,256]{2,1,0:T(8,128)(2,1)} custom-call(bf16[16,96,256]{2,1,0:T(8,128)(2,1)S(1)} %all-to-all-done.refs_0_, bf16[256,512]{1,0:T(8,128)(2,1)S(1)} %copy-done.2, bf16[256,512]{1,0:T(8,128)(2,1)S(1)} %copy-done.1), custom_call_target="tpu_custom_call" | custom-call | tf_op jit(solution)/shard_map/pallas_call | solution.py:226
  47.9 5.1 %all-to-all-done.1 = bf16[16,32,256]{2,1,0:T(8,128)(2,1)S(1)} async-done(((bf16[16,32,256]{2,1,0:T(8,128)(2,1)}), bf16[16,32,256]{2,1,0:T(8,128)(2,1)S(1)}, u32[]{:S(2)}, u32[]{:S(2)}) %all-to-all-start.1) | async-done | bytes 262176 | tf_op jit(solution)/shard_map/all_to_all | solution.py:253
  52.9 0.8 collective-permute-start
  53.8 0.5 collective-permute-start.7
  54.3 0.8 collective-permute-done.7.refs_2_
  55.1 3.6 %all-to-all-start.2 = ((bf16[16,64,256]{2,1,0:T(8,128)(2,1)}), bf16[16,64,256]{2,1,0:T(8,128)(2,1)S(1)}, u32[]{:S(2)}, u32[]{:S(2)}) async-start(bf16[16,64,256]{2,1,0:T(8,128)(2,1)} %shard_map.96), calls=%async_computation.2 | async-start | bytes 1048576 | tf_op jit(solution)/shard_map/all_to_all | solution.py:253
  58.7 0.0 collective-permute-done.1.refs_3_
  58.7 5.5 %collective-permute-done.2.refs_4_ = bf16[1024,512]{1,0:T(8,128)(2,1)} collective-permute-done((bf16[1024,512]{1,0:T(8,128)(2,1)}, bf16[1024,512]{1,0:T(8,128)(2,1)}, u32[]{:S(2)}, u32[]{:S(2)}) %collective-permute-start.2) | collective-permute-done | bytes 1048608 | tf_op jit(solution)/shard_map/ppermute | solution.py:240
  64.2 1.7 %collective-permute-done.3.refs_2_ = bf16[1024,512]{1,0:T(8,128)(2,1)S(1)} collective-permute-done((bf16[1024,512]{1,0:T(8,128)(2,1)}, bf16[1024,512]{1,0:T(8,128)(2,1)S(1)}, u32[]{:S(2)}, u32[]{:S(2)}) %collective-permute-start.3) | collective-permute-done | bytes 1048608 | tf_op jit(solution)/shard_map/ppermute | solution.py:240
  65.9 0.0 copy-start.3
  65.9 0.0 collective-permute-done
  65.9 2.0 %collective-permute-start.6 = (bf16[512,256]{1,0:T(8,128)(2,1)S(1)}, bf16[512,256]{1,0:T(8,128)(2,1)S(1)}, u32[]{:S(2)}, u32[]{:S(2)}) collective-permute-start(bf16[512,256]{1,0:T(8,128)(2,1)S(1)} %collective-permute-done), channel_id=1, source_target_pairs={{0,3},{1,0},{2,1},{3,2},{4,7},{5,4},{6,5},{7,6},{8,11},{9,8},{10,9... | collective-permute-start | bytes 786440 | tf_op jit(solution)/shard_map/ppermute | solution.py:240
  68.0 0.0 collective-permute-start.5
  68.0 1.6 %collective-permute-start.4 = (bf16[512,256]{1,0:T(8,128)(2,1)S(1)}, bf16[512,256]{1,0:T(8,128)(2,1)S(1)}, u32[]{:S(2)}, u32[]{:S(2)}) collective-permute-start(bf16[512,256]{1,0:T(8,128)(2,1)S(1)} %collective-permute-done), channel_id=1, source_target_pairs={{0,2},{1,3},{2,0},{3,1},{4,6},{5,7},{6,4},{7,5},{8,10},{9,11},{10,... | collective-permute-start | bytes 786440 | tf_op jit(solution)/shard_map/ppermute | solution.py:240
  69.5 0.0 copy-done.3
  69.5 1.7 %fusion.refs_0_ = f32[256,1024]{1,0:T(8,128)S(1)} fusion(bf16[512,256]{1,0:T(8,128)(2,1)S(1)} %collective-permute-done, bf16[1,4096,512]{2,1,0:T(8,128)(2,1)} %param.11, s32[]{:T(128)S(6)} %select_n.3), kind=kOutput, calls=%fused_computation | convolution fusion | flops 268435456 | bytes 2359300 | tf_op jit(solution)/shard_map/dot_general | solution.py:316
  71.2 0.0 copy-start
  71.2 3.9 %collective-permute-done.6.refs_2_ = bf16[512,256]{1,0:T(8,128)(2,1)S(1)} collective-permute-done((bf16[512,256]{1,0:T(8,128)(2,1)S(1)}, bf16[512,256]{1,0:T(8,128)(2,1)S(1)}, u32[]{:S(2)}, u32[]{:S(2)}) %collective-permute-start.6) | collective-permute-done | bytes 262176 | tf_op jit(solution)/shard_map/ppermute | solution.py:240
  75.2 6.4 %collective-permute-done.5.refs_1_ = bf16[512,256]{1,0:T(8,128)(2,1)S(1)} collective-permute-done((bf16[512,256]{1,0:T(8,128)(2,1)S(1)}, bf16[512,256]{1,0:T(8,128)(2,1)S(1)}, u32[]{:S(2)}, u32[]{:S(2)}) %collective-permute-start.5) | collective-permute-done | bytes 262176 | tf_op jit(solution)/shard_map/ppermute | solution.py:240
  81.6 2.1 %shard_map.98.refs_0_ = f32[256,1024]{1,0:T(8,128)S(1)} custom-call(f32[256,1024]{1,0:T(8,128)S(1)} %fusion.refs_0_, bf16[512,256]{1,0:T(8,128)(2,1)S(1)} %collective-permute-done.5.refs_1_, bf16[512,256]{1,0:T(8,128)(2,1)S(1)} %collective-permute-done.6.refs_2_, bf16[1024,512]{1,0:T(8,128)(2,1)} %collective-permute-done.1.refs_3_, ...), custom_call_target="tpu_custom_call" | custom-call | flops 7516192768 | bytes 29360128 | tf_op jit(solution)/shard_map/pallas_call | solution.py:226
  83.7 0.0 all-to-all-done.2.refs_0_
  83.7 0.0 copy-done
  83.7 1.0 %shard_map.99 = (bf16[256,512]{1,0:T(8,128)(2,1)}, f32[256,512]{1,0:T(8,128)}) custom-call(bf16[16,64,256]{2,1,0:T(8,128)(2,1)S(1)} %all-to-all-done.2.refs_0_, bf16[256,512]{1,0:T(8,128)(2,1)S(1)} %bitcast.18, bf16[16,128]{1,0:T(8,128)(2,1)S(1)} %collective-permute-done.7.refs_2_), custom_call_target="tpu_custom_call" | custom-call | tf_op jit(solution)/shard_map/pallas_call | solution.py:226
  84.7 0.0 collective-permute-done.4.refs_1_
  84.7 3.0 %shard_map.100 = bf16[256,1024]{1,0:T(8,128)(2,1)} custom-call(f32[256,1024]{1,0:T(8,128)S(1)} %shard_map.98.refs_0_, bf16[512,256]{1,0:T(8,128)(2,1)S(1)} %collective-permute-done.4.refs_1_, bf16[1024,512]{1,0:T(8,128)(2,1)} %copy-done.3), custom_call_target="tpu_custom_call" | custom-call | flops 3758096384 | bytes 14680064 | tf_op jit(solution)/shard_map/pallas_call | solution.py:226
  (1 shorter events, 0.0 us)
Async XLA Ops:
  0.6 31.7 %copy-start.1 = (bf16[256,512]{1,0:T(8,128)(2,1)S(1)}, bf16[256,512]{1,0:T(8,128)(2,1)}, u32[]{:S(2)}) copy-start(bf16[256,512]{1,0:T(8,128)(2,1)} %constant.29.clone.refs_2_) | copy-start | bytes 786436
  0.6 31.7 %copy-start.2 = (bf16[256,512]{1,0:T(8,128)(2,1)S(1)}, bf16[256,512]{1,0:T(8,128)(2,1)}, u32[]{:S(2)}) copy-start(bf16[256,512]{1,0:T(8,128)(2,1)} %constant.28.clone.refs_1_) | copy-start | bytes 786436
  3.0 29.3 %all-to-all-start = ((bf16[16,96,256]{2,1,0:T(8,128)(2,1)}), bf16[16,96,256]{2,1,0:T(8,128)(2,1)S(1)}, u32[]{:S(2)}, u32[]{:S(2)}) async-start(bf16[16,96,256]{2,1,0:T(8,128)(2,1)} %shard_map.94), calls=%async_computation | async-start | bytes 1572864 | tf_op jit(solution)/shard_map/all_to_all | solution.py:253
  15.2 43.4 %collective-permute-start.1 = (bf16[1024,512]{1,0:T(8,128)(2,1)}, bf16[1024,512]{1,0:T(8,128)(2,1)}, u32[]{:S(2)}, u32[]{:S(2)}) collective-permute-start(bf16[1024,512]{1,0:T(8,128)(2,1)} %get-tuple-element.24), channel_id=1, source_target_pairs={{0,1},{1,2},{2,3},{3,0},{4,5},{5,6},{6,7},{7,4},{8,9},{9,10},{10,1... | collective-permute-start | bytes 3145736 | tf_op jit(solution)/shard_map/ppermute | solution.py:240
  16.9 47.3 %collective-permute-start.2 = (bf16[1024,512]{1,0:T(8,128)(2,1)}, bf16[1024,512]{1,0:T(8,128)(2,1)}, u32[]{:S(2)}, u32[]{:S(2)}) collective-permute-start(bf16[1024,512]{1,0:T(8,128)(2,1)} %get-tuple-element.25), channel_id=1, source_target_pairs={{0,3},{1,0},{2,1},{3,2},{4,7},{5,4},{6,5},{7,6},{8,11},{9,8},{10,9... | collective-permute-start | bytes 3145736 | tf_op jit(solution)/shard_map/ppermute | solution.py:240
  18.5 47.4 %collective-permute-start.3 = (bf16[1024,512]{1,0:T(8,128)(2,1)}, bf16[1024,512]{1,0:T(8,128)(2,1)S(1)}, u32[]{:S(2)}, u32[]{:S(2)}) collective-permute-start(bf16[1024,512]{1,0:T(8,128)(2,1)} %get-tuple-element.26), channel_id=1, source_target_pairs={{0,2},{1,3},{2,0},{3,1},{4,6},{5,7},{6,4},{7,5},{8,10},{9,11},{10,... | collective-permute-start | bytes 3145736 | tf_op jit(solution)/shard_map/ppermute | solution.py:240
  36.4 16.5 %all-to-all-start.1 = ((bf16[16,32,256]{2,1,0:T(8,128)(2,1)}), bf16[16,32,256]{2,1,0:T(8,128)(2,1)S(1)}, u32[]{:S(2)}, u32[]{:S(2)}) async-start(bf16[16,32,256]{2,1,0:T(8,128)(2,1)} %bitcast.20), calls=%async_computation.1 | async-start | bytes 524288 | tf_op jit(solution)/shard_map/all_to_all | solution.py:253
  52.9 13.0 %collective-permute-start = (bf16[512,256]{1,0:T(8,128)(2,1)S(1)}, bf16[512,256]{1,0:T(8,128)(2,1)S(1)}, u32[]{:S(2)}, u32[]{:S(2)}) collective-permute-start(bf16[512,256]{1,0:T(8,128)(2,1)S(1)} %bitcast.21), channel_id=1, source_target_pairs={{0,192},{64,0},{128,64},{192,128},{1,193},{65,1},{129,65},{193,129... | collective-permute-start | bytes 786440 | tf_op jit(solution)/shard_map/ppermute | solution.py:240
  53.8 1.3 %collective-permute-start.7 = (bf16[16,128]{1,0:T(8,128)(2,1)S(1)}, bf16[16,128]{1,0:T(8,128)(2,1)S(1)}, u32[]{:S(2)}, u32[]{:S(2)}) collective-permute-start(bf16[16,128]{1,0:T(8,128)(2,1)S(1)} %slice.3), channel_id=1, source_target_pairs={{0,4},{4,0},{8,12},{12,8},{16,20},{20,16},{24,28},{28,24},{32,36},... | collective-permute-start | bytes 12296 | tf_op jit(solution)/shard_map/ppermute | solution.py:310
  55.1 28.6 %all-to-all-start.2 = ((bf16[16,64,256]{2,1,0:T(8,128)(2,1)}), bf16[16,64,256]{2,1,0:T(8,128)(2,1)S(1)}, u32[]{:S(2)}, u32[]{:S(2)}) async-start(bf16[16,64,256]{2,1,0:T(8,128)(2,1)} %shard_map.96), calls=%async_computation.2 | async-start | bytes 1048576 | tf_op jit(solution)/shard_map/all_to_all | solution.py:253
  65.9 3.6 %copy-start.3 = (bf16[1024,512]{1,0:T(8,128)(2,1)}, bf16[1024,512]{1,0:T(8,128)(2,1)S(1)}, u32[]{:S(2)}) copy-start(bf16[1024,512]{1,0:T(8,128)(2,1)S(1)} %collective-permute-done.3.refs_2_) | copy-start | bytes 3145732
  65.9 9.2 %collective-permute-start.6 = (bf16[512,256]{1,0:T(8,128)(2,1)S(1)}, bf16[512,256]{1,0:T(8,128)(2,1)S(1)}, u32[]{:S(2)}, u32[]{:S(2)}) collective-permute-start(bf16[512,256]{1,0:T(8,128)(2,1)S(1)} %collective-permute-done), channel_id=1, source_target_pairs={{0,3},{1,0},{2,1},{3,2},{4,7},{5,4},{6,5},{7,6},{8,11},{9,8},{10,9... | collective-permute-start | bytes 786440 | tf_op jit(solution)/shard_map/ppermute | solution.py:240
  68.0 13.6 %collective-permute-start.5 = (bf16[512,256]{1,0:T(8,128)(2,1)S(1)}, bf16[512,256]{1,0:T(8,128)(2,1)S(1)}, u32[]{:S(2)}, u32[]{:S(2)}) collective-permute-start(bf16[512,256]{1,0:T(8,128)(2,1)S(1)} %collective-permute-done), channel_id=1, source_target_pairs={{0,1},{1,2},{2,3},{3,0},{4,5},{5,6},{6,7},{7,4},{8,9},{9,10},{10,1... | collective-permute-start | bytes 786440 | tf_op jit(solution)/shard_map/ppermute | solution.py:240
  68.0 16.7 %collective-permute-start.4 = (bf16[512,256]{1,0:T(8,128)(2,1)S(1)}, bf16[512,256]{1,0:T(8,128)(2,1)S(1)}, u32[]{:S(2)}, u32[]{:S(2)}) collective-permute-start(bf16[512,256]{1,0:T(8,128)(2,1)S(1)} %collective-permute-done), channel_id=1, source_target_pairs={{0,2},{1,3},{2,0},{3,1},{4,6},{5,7},{6,4},{7,5},{8,10},{9,11},{10,... | collective-permute-start | bytes 786440 | tf_op jit(solution)/shard_map/ppermute | solution.py:240
  71.2 12.4 %copy-start = (bf16[1,256,512]{2,1,0:T(8,128)(2,1)S(1)}, bf16[1,256,512]{2,1,0:T(8,128)(2,1)}, u32[]{:S(2)}) copy-start(bf16[1,256,512]{2,1,0:T(8,128)(2,1)} %param.9) | copy-start | bytes 786436

commit v9 on v7

--- a/solution.py
+++ b/solution.py
@@ -8,7 +8,7 @@
 from jax.sharding import PartitionSpec as P
 
 
-HINT_SCALE = 14
+HINT_SCALE = 8
 
 
 def make_tables(panel_len):
@@ -291,15 +291,6 @@
             block, block_weight, (((0,), (1,)), ((), ())), preferred_element_type=jnp.float32
         )
 
-    gate_grad, filter_grad = call(
-        finish_kernel,
-        panels,
-        (shape(panel_len, width), shape(panel_len, width, dtype=jnp.float32)),
-        [],
-        rest,
-        grad_out[0],
-        token,
-    )
     total = project(received, lax.dynamic_slice_in_dim(weight[0], my_group * outputs, outputs, 0))
     blocks = [shifted(received, "chan", by) for by in (1, 3, 2)]
 
@@ -323,12 +314,17 @@
         )
         return added
 
-    blocks[:2], total = lax.optimization_barrier((blocks[:2], total))
-    total = add_blocks(total, (0, 1), jnp.float32)
-    blocks[2], total, gate_grad, filter_grad = lax.optimization_barrier(
-        (blocks[2], total, gate_grad, filter_grad)
-    )
-    input_grad = add_blocks(total, (2,), jnp.bfloat16)
+    input_grad = add_blocks(total, (0, 1, 2), jnp.bfloat16)
+    rest, input_grad = lax.optimization_barrier((rest, input_grad))
+    gate_grad, filter_grad = call(
+        finish_kernel,
+        panels,
+        (shape(panel_len, width), shape(panel_len, width, dtype=jnp.float32)),
+        [],
+        rest,
+        grad_out[0],
+        token,
+    )
     return gate_grad[None], filter_grad[None], input_grad[None]
 
 

time: 87.7 us -> 86.5 us (0.986)
  Pallas kernels: 21.9 us -> 20.5 us
    pallas_call x6 -> x5, Pallas kernels: 18.4 us -> 17 us  [call(): pl.pallas_call(lambda *refs: kernel(panels, *refs), out_shape=outs, in_sp...]
  transfers between devices with their start and end apart: 11 -> 11, of which waited for: 7 -> 8; matrix products, arithmetic and copies ran while one was open for 2% -> 2% of each run, Pallas kernels for 19% -> 20%
where the time goes in v9:
time: 86.5 us; the launch traced here: 85.3 us
  waiting for transfers between devices  34.5 us (40%)
  starting transfers between devices  27.7 us (32%)
  Pallas kernels  20.5 us (24%)
  matrix products  1.7 us (2%)
    all_to_all x3, starting transfers between devices, swapped(): return lax.all_to_all(parts, 'seq', 0, 0, tiled=True)  17.3 us
    pallas_call x5, Pallas kernels, call(): pl.pallas_call(lambda *refs: kernel(panels, *refs), out_shape=outs, in_sp...  17 us
    all_to_all x3, waiting for transfers between devices, swapped(): return lax.all_to_all(parts, 'seq', 0, 0, tiled=True)  16.9 us
    ppermute x7, waiting for transfers between devices, shifted(): lax.ppermute(x, axis, [(i, (i + by) % length) for i in range(length)])  16.8 us
    ppermute x7, starting transfers between devices, shifted(): lax.ppermute(x, axis, [(i, (i + by) % length) for i in range(length)])  9.94 us
    pallas_call x1, Pallas kernels, on_device(): pl.pallas_call(weight_kernel, out_shape=[pltpu.HBM((outputs, width), jnp....  3.48 us
  transfers between devices with their start and end apart: 11, of which 8 were waited for; matrix products, arithmetic and copies ran while one was open for 2% of the time, Pallas kernels for 20%

profile of v9, /device:TPU:6, one launch (start us, length us, event | category | flops | bytes accessed | tf_op | source)
XLA Modules:
  0.0 85.3 jit_solution(9187390329873829893)
XLA Ops:
  0.6 0.0 copy-start.1
  0.6 0.0 copy-start.2
  0.7 2.4 %shard_map.94 = bf16[16,96,256]{2,1,0:T(8,128)(2,1)} custom-call(bf16[256,512]{1,0:T(8,128)(2,1)} %bitcast.23, bf16[256,512]{1,0:T(8,128)(2,1)} %bitcast.24, bf16[256,512]{1,0:T(8,128)(2,1)} %bitcast.17, bf16[256,512]{1,0:T(8,128)(2,1)} %bitcast.25), custom_call_target="tpu_custom_call" | custom-call | tf_op jit(solution)/shard_map/pallas_call | solution.py:200
  3.0 8.6 %all-to-all-start = ((bf16[16,96,256]{2,1,0:T(8,128)(2,1)}), bf16[16,96,256]{2,1,0:T(8,128)(2,1)S(1)}, u32[]{:S(2)}, u32[]{:S(2)}) async-start(bf16[16,96,256]{2,1,0:T(8,128)(2,1)} %shard_map.94), calls=%async_computation | async-start | bytes 1572864 | tf_op jit(solution)/shard_map/all_to_all | solution.py:227
  11.6 0.1 pad_add_fusion.starts_ref
  11.7 3.5 %shard_map.97 = (bf16[1024,512]{1,0:T(8,128)(2,1)}, bf16[1024,512]{1,0:T(8,128)(2,1)}, bf16[1024,512]{1,0:T(8,128)(2,1)}) custom-call(s32[3]{0:T(128)S(1)} %pad_add_fusion.starts_ref, bf16[4096,512]{1,0:T(8,128)(2,1)} %bitcast.19), custom_call_target="tpu_custom_call" | custom-call | tf_op jit(solution)/shard_map/pallas_call | solution.py:248
  15.2 1.7 %collective-permute-start.2 = (bf16[1024,512]{1,0:T(8,128)(2,1)}, bf16[1024,512]{1,0:T(8,128)(2,1)S(1)}, u32[]{:S(2)}, u32[]{:S(2)}) collective-permute-start(bf16[1024,512]{1,0:T(8,128)(2,1)} %get-tuple-element.21), channel_id=1, source_target_pairs={{0,1},{1,2},{2,3},{3,0},{4,5},{5,6},{6,7},{7,4},{8,9},{9,10},{10,1... | collective-permute-start | bytes 3145736 | tf_op jit(solution)/shard_map/ppermute | solution.py:214
  16.9 1.7 %collective-permute-start.3 = (bf16[1024,512]{1,0:T(8,128)(2,1)}, bf16[1024,512]{1,0:T(8,128)(2,1)}, u32[]{:S(2)}, u32[]{:S(2)}) collective-permute-start(bf16[1024,512]{1,0:T(8,128)(2,1)} %get-tuple-element.22), channel_id=1, source_target_pairs={{0,3},{1,0},{2,1},{3,2},{4,7},{5,4},{6,5},{7,6},{8,11},{9,8},{10,9... | collective-permute-start | bytes 3145736 | tf_op jit(solution)/shard_map/ppermute | solution.py:214
  18.5 2.0 %collective-permute-start.4 = (bf16[1024,512]{1,0:T(8,128)(2,1)}, bf16[1024,512]{1,0:T(8,128)(2,1)}, u32[]{:S(2)}, u32[]{:S(2)}) collective-permute-start(bf16[1024,512]{1,0:T(8,128)(2,1)} %get-tuple-element.23), channel_id=1, source_target_pairs={{0,2},{1,3},{2,0},{3,1},{4,6},{5,7},{6,4},{7,5},{8,10},{9,11},{10,... | collective-permute-start | bytes 3145736 | tf_op jit(solution)/shard_map/ppermute | solution.py:214
  20.5 11.8 %all-to-all-done.refs_0_ = bf16[16,96,256]{2,1,0:T(8,128)(2,1)S(1)} async-done(((bf16[16,96,256]{2,1,0:T(8,128)(2,1)}), bf16[16,96,256]{2,1,0:T(8,128)(2,1)S(1)}, u32[]{:S(2)}, u32[]{:S(2)}) %all-to-all-start) | async-done | bytes 786464 | tf_op jit(solution)/shard_map/all_to_all | solution.py:227
  32.3 0.0 copy-done.1
  32.3 0.0 copy-done.2
  32.3 4.1 %shard_map.95 = bf16[512,256]{1,0:T(8,128)(2,1)} custom-call(bf16[16,96,256]{2,1,0:T(8,128)(2,1)S(1)} %all-to-all-done.refs_0_, bf16[256,512]{1,0:T(8,128)(2,1)S(1)} %copy-done.2, bf16[256,512]{1,0:T(8,128)(2,1)S(1)} %copy-done.1), custom_call_target="tpu_custom_call" | custom-call | tf_op jit(solution)/shard_map/pallas_call | solution.py:200
  36.4 5.1 %all-to-all-start.1 = ((bf16[16,32,256]{2,1,0:T(8,128)(2,1)}), bf16[16,32,256]{2,1,0:T(8,128)(2,1)S(1)}, u32[]{:S(2)}, u32[]{:S(2)}) async-start(bf16[16,32,256]{2,1,0:T(8,128)(2,1)} %bitcast.20), calls=%async_computation.1 | async-start | bytes 524288 | tf_op jit(solution)/shard_map/all_to_all | solution.py:227
  41.5 6.3 %shard_map.96 = bf16[16,64,256]{2,1,0:T(8,128)(2,1)} custom-call(bf16[16,96,256]{2,1,0:T(8,128)(2,1)S(1)} %all-to-all-done.refs_0_, bf16[256,512]{1,0:T(8,128)(2,1)S(1)} %copy-done.2, bf16[256,512]{1,0:T(8,128)(2,1)S(1)} %copy-done.1), custom_call_target="tpu_custom_call" | custom-call | tf_op jit(solution)/shard_map/pallas_call | solution.py:200
  47.9 5.1 %all-to-all-done.1 = bf16[16,32,256]{2,1,0:T(8,128)(2,1)S(1)} async-done(((bf16[16,32,256]{2,1,0:T(8,128)(2,1)}), bf16[16,32,256]{2,1,0:T(8,128)(2,1)S(1)}, u32[]{:S(2)}, u32[]{:S(2)}) %all-to-all-start.1) | async-done | bytes 262176 | tf_op jit(solution)/shard_map/all_to_all | solution.py:227
  52.9 0.8 collective-permute-start.1
  53.8 0.5 collective-permute-start
  54.3 0.8 collective-permute-done.refs_2_
  55.1 3.6 %all-to-all-start.2 = ((bf16[16,64,256]{2,1,0:T(8,128)(2,1)}), bf16[16,64,256]{2,1,0:T(8,128)(2,1)S(1)}, u32[]{:S(2)}, u32[]{:S(2)}) async-start(bf16[16,64,256]{2,1,0:T(8,128)(2,1)} %shard_map.96), calls=%async_computation.2 | async-start | bytes 1048576 | tf_op jit(solution)/shard_map/all_to_all | solution.py:227
  58.7 0.0 collective-permute-done.2.refs_4_
  58.7 0.0 copy-start.3
  58.7 5.5 %collective-permute-done.3.refs_5_ = bf16[1024,512]{1,0:T(8,128)(2,1)} collective-permute-done((bf16[1024,512]{1,0:T(8,128)(2,1)}, bf16[1024,512]{1,0:T(8,128)(2,1)}, u32[]{:S(2)}, u32[]{:S(2)}) %collective-permute-start.3) | collective-permute-done | bytes 1048608 | tf_op jit(solution)/shard_map/ppermute | solution.py:214
  64.2 1.8 %collective-permute-done.4.refs_6_ = bf16[1024,512]{1,0:T(8,128)(2,1)} collective-permute-done((bf16[1024,512]{1,0:T(8,128)(2,1)}, bf16[1024,512]{1,0:T(8,128)(2,1)}, u32[]{:S(2)}, u32[]{:S(2)}) %collective-permute-start.4) | collective-permute-done | bytes 1048608 | tf_op jit(solution)/shard_map/ppermute | solution.py:214
  66.0 0.0 collective-permute-done.1
  66.0 0.7 collective-permute-start.7
  66.8 3.1 %collective-permute-start.6 = (bf16[512,256]{1,0:T(8,128)(2,1)S(1)}, bf16[512,256]{1,0:T(8,128)(2,1)S(1)}, u32[]{:S(2)}, u32[]{:S(2)}) collective-permute-start(bf16[512,256]{1,0:T(8,128)(2,1)S(1)} %collective-permute-done.1), channel_id=1, source_target_pairs={{0,3},{1,0},{2,1},{3,2},{4,7},{5,4},{6,5},{7,6},{8,11},{9,8},{10,9... | collective-permute-start | bytes 786440 | tf_op jit(solution)/shard_map/ppermute | solution.py:214
  69.8 0.0 collective-permute-start.5
  69.8 1.7 %fusion.refs_0_ = f32[256,1024]{1,0:T(8,128)S(1)} fusion(bf16[512,256]{1,0:T(8,128)(2,1)S(1)} %collective-permute-done.1, bf16[1,4096,512]{2,1,0:T(8,128)(2,1)} %param.11, s32[]{:T(128)S(6)} %select_n.3), kind=kOutput, calls=%fused_computation | convolution fusion | flops 268435456 | bytes 2359300 | tf_op jit(solution)/shard_map/dot_general | solution.py:290
  71.5 0.0 copy-start
  71.6 5.2 %collective-permute-done.7.refs_3_ = bf16[512,256]{1,0:T(8,128)(2,1)S(1)} collective-permute-done((bf16[512,256]{1,0:T(8,128)(2,1)S(1)}, bf16[512,256]{1,0:T(8,128)(2,1)S(1)}, u32[]{:S(2)}, u32[]{:S(2)}) %collective-permute-start.7) | collective-permute-done | bytes 262176 | tf_op jit(solution)/shard_map/ppermute | solution.py:214
  76.8 2.9 %collective-permute-done.6.refs_2_ = bf16[512,256]{1,0:T(8,128)(2,1)S(1)} collective-permute-done((bf16[512,256]{1,0:T(8,128)(2,1)S(1)}, bf16[512,256]{1,0:T(8,128)(2,1)S(1)}, u32[]{:S(2)}, u32[]{:S(2)}) %collective-permute-start.6) | collective-permute-done | bytes 262176 | tf_op jit(solution)/shard_map/ppermute | solution.py:214
  79.6 1.4 %collective-permute-done.5.refs_1_ = bf16[512,256]{1,0:T(8,128)(2,1)S(1)} collective-permute-done((bf16[512,256]{1,0:T(8,128)(2,1)S(1)}, bf16[512,256]{1,0:T(8,128)(2,1)S(1)}, u32[]{:S(2)}, u32[]{:S(2)}) %collective-permute-start.5) | collective-permute-done | bytes 262176 | tf_op jit(solution)/shard_map/ppermute | solution.py:214
  81.0 0.0 copy-done.3
  81.0 3.3 %shard_map.98 = bf16[256,1024]{1,0:T(8,128)(2,1)} custom-call(f32[256,1024]{1,0:T(8,128)S(1)} %fusion.refs_0_, bf16[512,256]{1,0:T(8,128)(2,1)S(1)} %collective-permute-done.5.refs_1_, bf16[512,256]{1,0:T(8,128)(2,1)S(1)} %collective-permute-done.6.refs_2_, bf16[512,256]{1,0:T(8,128)(2,1)S(1)} %collective-permute-done.7.refs_3_, ...), custom_call_target="tpu_custom_call" | custom-call | flops 6442450944 | bytes 25165824 | tf_op jit(solution)/shard_map/pallas_call | solution.py:200
  84.3 0.0 all-to-all-done.2.refs_0_
  84.3 0.0 copy-done
  84.3 1.0 %shard_map.99 = (bf16[256,512]{1,0:T(8,128)(2,1)}, f32[256,512]{1,0:T(8,128)}) custom-call(bf16[16,64,256]{2,1,0:T(8,128)(2,1)S(1)} %all-to-all-done.2.refs_0_, bf16[256,512]{1,0:T(8,128)(2,1)S(1)} %bitcast.18, bf16[16,128]{1,0:T(8,128)(2,1)S(1)} %collective-permute-done.refs_2_), custom_call_target="tpu_custom_call" | custom-call | tf_op jit(solution)/shard_map/pallas_call | solution.py:200
  (1 shorter events, 0.0 us)
Async XLA Ops:
  0.6 31.7 %copy-start.1 = (bf16[256,512]{1,0:T(8,128)(2,1)S(1)}, bf16[256,512]{1,0:T(8,128)(2,1)}, u32[]{:S(2)}) copy-start(bf16[256,512]{1,0:T(8,128)(2,1)} %constant.29.clone.refs_2_) | copy-start | bytes 786436
  0.6 31.7 %copy-start.2 = (bf16[256,512]{1,0:T(8,128)(2,1)S(1)}, bf16[256,512]{1,0:T(8,128)(2,1)}, u32[]{:S(2)}) copy-start(bf16[256,512]{1,0:T(8,128)(2,1)} %constant.28.clone.refs_1_) | copy-start | bytes 786436
  3.0 29.3 %all-to-all-start = ((bf16[16,96,256]{2,1,0:T(8,128)(2,1)}), bf16[16,96,256]{2,1,0:T(8,128)(2,1)S(1)}, u32[]{:S(2)}, u32[]{:S(2)}) async-start(bf16[16,96,256]{2,1,0:T(8,128)(2,1)} %shard_map.94), calls=%async_computation | async-start | bytes 1572864 | tf_op jit(solution)/shard_map/all_to_all | solution.py:227
  15.2 43.5 %collective-permute-start.2 = (bf16[1024,512]{1,0:T(8,128)(2,1)}, bf16[1024,512]{1,0:T(8,128)(2,1)S(1)}, u32[]{:S(2)}, u32[]{:S(2)}) collective-permute-start(bf16[1024,512]{1,0:T(8,128)(2,1)} %get-tuple-element.21), channel_id=1, source_target_pairs={{0,1},{1,2},{2,3},{3,0},{4,5},{5,6},{6,7},{7,4},{8,9},{9,10},{10,1... | collective-permute-start | bytes 3145736 | tf_op jit(solution)/shard_map/ppermute | solution.py:214
  16.9 47.3 %collective-permute-start.3 = (bf16[1024,512]{1,0:T(8,128)(2,1)}, bf16[1024,512]{1,0:T(8,128)(2,1)}, u32[]{:S(2)}, u32[]{:S(2)}) collective-permute-start(bf16[1024,512]{1,0:T(8,128)(2,1)} %get-tuple-element.22), channel_id=1, source_target_pairs={{0,3},{1,0},{2,1},{3,2},{4,7},{5,4},{6,5},{7,6},{8,11},{9,8},{10,9... | collective-permute-start | bytes 3145736 | tf_op jit(solution)/shard_map/ppermute | solution.py:214
  18.5 47.5 %collective-permute-start.4 = (bf16[1024,512]{1,0:T(8,128)(2,1)}, bf16[1024,512]{1,0:T(8,128)(2,1)}, u32[]{:S(2)}, u32[]{:S(2)}) collective-permute-start(bf16[1024,512]{1,0:T(8,128)(2,1)} %get-tuple-element.23), channel_id=1, source_target_pairs={{0,2},{1,3},{2,0},{3,1},{4,6},{5,7},{6,4},{7,5},{8,10},{9,11},{10,... | collective-permute-start | bytes 3145736 | tf_op jit(solution)/shard_map/ppermute | solution.py:214
  36.4 16.5 %all-to-all-start.1 = ((bf16[16,32,256]{2,1,0:T(8,128)(2,1)}), bf16[16,32,256]{2,1,0:T(8,128)(2,1)S(1)}, u32[]{:S(2)}, u32[]{:S(2)}) async-start(bf16[16,32,256]{2,1,0:T(8,128)(2,1)} %bitcast.20), calls=%async_computation.1 | async-start | bytes 524288 | tf_op jit(solution)/shard_map/all_to_all | solution.py:227
  52.9 13.1 %collective-permute-start.1 = (bf16[512,256]{1,0:T(8,128)(2,1)S(1)}, bf16[512,256]{1,0:T(8,128)(2,1)S(1)}, u32[]{:S(2)}, u32[]{:S(2)}) collective-permute-start(bf16[512,256]{1,0:T(8,128)(2,1)S(1)} %bitcast.21), channel_id=1, source_target_pairs={{0,192},{64,0},{128,64},{192,128},{1,193},{65,1},{129,65},{193,129... | collective-permute-start | bytes 786440 | tf_op jit(solution)/shard_map/ppermute | solution.py:214
  53.8 1.3 %collective-permute-start = (bf16[16,128]{1,0:T(8,128)(2,1)S(1)}, bf16[16,128]{1,0:T(8,128)(2,1)S(1)}, u32[]{:S(2)}, u32[]{:S(2)}) collective-permute-start(bf16[16,128]{1,0:T(8,128)(2,1)S(1)} %slice.3), channel_id=1, source_target_pairs={{0,4},{4,0},{8,12},{12,8},{16,20},{20,16},{24,28},{28,24},{32,36},... | collective-permute-start | bytes 12296 | tf_op jit(solution)/shard_map/ppermute | solution.py:284
  55.1 29.2 %all-to-all-start.2 = ((bf16[16,64,256]{2,1,0:T(8,128)(2,1)}), bf16[16,64,256]{2,1,0:T(8,128)(2,1)S(1)}, u32[]{:S(2)}, u32[]{:S(2)}) async-start(bf16[16,64,256]{2,1,0:T(8,128)(2,1)} %shard_map.96), calls=%async_computation.2 | async-start | bytes 1048576 | tf_op jit(solution)/shard_map/all_to_all | solution.py:227
  58.7 22.3 %copy-start.3 = (bf16[1024,512]{1,0:T(8,128)(2,1)}, bf16[1024,512]{1,0:T(8,128)(2,1)S(1)}, u32[]{:S(2)}) copy-start(bf16[1024,512]{1,0:T(8,128)(2,1)S(1)} %collective-permute-done.2.refs_4_) | copy-start | bytes 3145732
  66.0 10.7 %collective-permute-start.7 = (bf16[512,256]{1,0:T(8,128)(2,1)S(1)}, bf16[512,256]{1,0:T(8,128)(2,1)S(1)}, u32[]{:S(2)}, u32[]{:S(2)}) collective-permute-start(bf16[512,256]{1,0:T(8,128)(2,1)S(1)} %collective-permute-done.1), channel_id=1, source_target_pairs={{0,2},{1,3},{2,0},{3,1},{4,6},{5,7},{6,4},{7,5},{8,10},{9,11},{10,... | collective-permute-start | bytes 786440 | tf_op jit(solution)/shard_map/ppermute | solution.py:214
  66.8 12.8 %collective-permute-start.6 = (bf16[512,256]{1,0:T(8,128)(2,1)S(1)}, bf16[512,256]{1,0:T(8,128)(2,1)S(1)}, u32[]{:S(2)}, u32[]{:S(2)}) collective-permute-start(bf16[512,256]{1,0:T(8,128)(2,1)S(1)} %collective-permute-done.1), channel_id=1, source_target_pairs={{0,3},{1,0},{2,1},{3,2},{4,7},{5,4},{6,5},{7,6},{8,11},{9,8},{10,9... | collective-permute-start | bytes 786440 | tf_op jit(solution)/shard_map/ppermute | solution.py:214
  69.8 11.2 %collective-permute-start.5 = (bf16[512,256]{1,0:T(8,128)(2,1)S(1)}, bf16[512,256]{1,0:T(8,128)(2,1)S(1)}, u32[]{:S(2)}, u32[]{:S(2)}) collective-permute-start(bf16[512,256]{1,0:T(8,128)(2,1)S(1)} %collective-permute-done.1), channel_id=1, source_target_pairs={{0,1},{1,2},{2,3},{3,0},{4,5},{5,6},{6,7},{7,4},{8,9},{9,10},{10,1... | collective-permute-start | bytes 786440 | tf_op jit(solution)/shard_map/ppermute | solution.py:214
  71.5 12.7 %copy-start = (bf16[1,256,512]{2,1,0:T(8,128)(2,1)S(1)}, bf16[1,256,512]{2,1,0:T(8,128)(2,1)}, u32[]{:S(2)}) copy-start(bf16[1,256,512]{2,1,0:T(8,128)(2,1)} %param.9) | copy-start | bytes 786436
